TPU v7x, 32 devices: a whole 2x2x4 slice. The times are simulated.
32 devices in a mesh: cand: 8 (over z, x), obs: 4 (over y, core).
Axes of the slice: x: 2, y: 2, z: 4, core: 2. Of those that a mesh axis runs over, the one named last changes fastest.
Arguments:
- block_index: int32 [1], replicated, may hold values from 64 to 127
- slot_block: int32 [128], replicated, may hold values from 0 to 127, each once
- factor_row: bfloat16 [128, 256, 256], P('cand', None, 'obs'), may hold values from -0.03125 to 0.03125
- earlier_rows: bfloat16 [128, 256, 2048], P(None, 'obs', 'cand'), may hold values from -6 to 6
- obs_weights: float32 [128, 256, 32], P('cand'), may hold values from 0.05 to 20
- cand_weights: float32 [2048, 32], P('cand'), may hold values from 0.05 to 20
- block_inverse: float32 [128, 256, 256], P('cand', 'obs'), may hold values from -0.046875 to 0.046875
- prior_var: float32 [2048], P('cand'), may hold values from 16 to 24
Outputs:
- solved_rows: float32 [256, 2048], P('obs', 'cand')
- remaining_var: float32 [2048], P('cand')
Inputs may be any that keep to these rules, and one draw needn't show every extreme that they name: slot_block names every block number once.
All inputs are finite; a program needn't handle non-finite values.
Results may differ from a plain program's by a relative error of at most 0.0003.
Values may be sent and summed in bfloat16 or wider, within the bound.
No kernel may reach another device: no remote copies, remote signals or barrier semaphores. Data moves between devices by JAX's collectives and lax.ppermute only.
A program may use at most 64 MiB of HBM per device.

v0:
```python
import jax
import jax.numpy as jnp
from jax import lax
from jax.sharding import PartitionSpec as P

HIGH = lax.Precision.HIGHEST


def spread(block, axis, holder):
    block = jnp.where(lax.axis_index(axis) == holder, block, jnp.zeros_like(block))
    return lax.psum(block, axis)


def mixtures(weights):
    return weights / jnp.sum(weights, axis=-1, keepdims=True)


def kernel_tile(points, cands):
    squared = jnp.sum(points * points, axis=-1)[:, None] + jnp.sum(cands * cands, axis=-1)[None, :]
    squared = squared - 2.0 * jnp.dot(points, cands.T, precision=HIGH)
    return jnp.exp(-10.0 * squared)


def on_device(
    block_index,
    slot_block,
    factor_row,
    earlier_rows,
    obs_weights,
    cand_weights,
    block_inverse,
    prior_var,
):
    current = block_index[0]
    per_device = obs_weights.shape[0]
    owner_rank = current // per_device
    slot_here = current % per_device
    block_points = lax.dynamic_index_in_dim(obs_weights, slot_here, 0, keepdims=False)
    inverse_rows = lax.dynamic_index_in_dim(block_inverse, slot_here, 0, keepdims=False)
    block_points, inverse_rows = (
        spread(block_points, "cand", owner_rank),
        spread(inverse_rows, "cand", owner_rank),
    )
    kernel_rows = kernel_tile(mixtures(block_points), mixtures(cand_weights))
    kept_mask = (slot_block < current).astype(jnp.bfloat16)
    earlier = jnp.take(earlier_rows, slot_block, axis=0)
    masked = lax.all_gather(factor_row, "cand", axis=0, tiled=True) * kept_mask[:, None, None]
    partial_sum = jnp.einsum("stq,sqc->tc", masked, earlier, preferred_element_type=jnp.float32)
    carried = lax.psum(partial_sum, "obs")
    residual = kernel_rows - carried
    solved_rows = jnp.dot(inverse_rows, residual, precision=HIGH)
    square_sums = lax.psum(jnp.sum(solved_rows * solved_rows, axis=0), "obs")
    return (solved_rows, prior_var - square_sums)


def solution(mesh):
    placed = (
        P(),
        P(),
        P("cand", None, "obs"),
        P(None, "obs", "cand"),
        P("cand", None, None),
        P("cand", None),
        P("cand", "obs", None),
        P("cand"),
    )
    return jax.shard_map(
        on_device,
        mesh=mesh,
        in_specs=placed,
        out_specs=(P("obs", "cand"), P("cand")),
        check_vma=False,
    )
```

profile of v0, /device:TPU:0, one launch (start us, length us, event | category | flops | bytes accessed | tf_op | source)
XLA Modules:
  0.0 209.9 jit_solution(9110308369427510244)
XLA Ops:
  7.2 0.0 all-gather.2.cloned.1.call-start
  7.2 0.7 all-gather.2.cloned.1.call-update
  7.9 0.0 all-reduce.5.cloned.1.call-start
  8.6 0.7 compare_select_fusion
  9.3 0.0 copy-start.2
  9.3 5.0 %gather_fusion = bf16[128,64,256]{2,1,0:T(8,128)(2,1)} fusion(bf16[128,64,256]{2,1,0:T(8,128)(2,1)} %param.11, s32[1024]{0:T(1024)S(1)} %pad_clamp_fusion), kind=kCustom, calls=%fused_computation | custom fusion | bytes 8389120 | tf_op jit(solution)/shard_map/jit(_take)/gather | solution.py:46
  14.2 0.0 copy-done.2
  14.3 72.0 %all-gather.2.cloned.1.call-done = bf16[128,256,64]{1,2,0:T(8,128)(2,1)} async-done(((bf16[16,256,64]{1,2,0:T(8,128)(2,1)}), bf16[128,256,64]{1,2,0:T(8,128)(2,1)}) %all-gather.2.cloned.1.call-update) | async-done | bytes 4194320 | tf_op jit(solution)/shard_map/all_gather | solution.py:47
  86.3 0.0 copy-start
  86.3 0.0 copy-start.1
  86.3 5.9 %fusion.10 = f32[256,256]{1,0:T(8,128)} fusion(bf16[128,64,256]{2,1,0:T(8,128)(2,1)} %gather_fusion, pred[128]{0:T(512)(128)(4,1)S(1)} %get-tuple-element.3, bf16[128,256,64]{1,2,0:T(8,128)(2,1)} %all-gather.2.cloned.1.call-done, bf16[128]{0:T(256)(128)(2,1)S(1)} %get-tuple-element.2), kind=kOutput, calls=%fused_computation.12 | convolution fusion | flops 1077936128 | bytes 8651136 | tf_op jit(solution)/shard_map/stq,sqc->tc/dot_general | solution.py:48
  92.2 0.0 all-reduce.5.cloned.1.call-update
  92.2 0.0 all-reduce.3.cloned.1.call-start
  92.3 1.5 select_bitcast_fusion
  93.8 0.0 all-reduce.3.cloned.1.call-update
  93.8 0.8 select_bitcast_fusion.1
  94.6 34.4 %psum.29 = f32[256,32]{0,1:T(8,128)S(1)} all-reduce(f32[256,32]{0,1:T(8,128)S(1)} %select_bitcast_fusion.1), channel_id=1, replica_groups=mesh['cand'=8,'obs'=4] {'cand'}, use_global_device_ids=true, to_apply=%region_1.2 | all-reduce | flops 8192 | bytes 65536 | tf_op jit(solution)/shard_map/psum | solution.py:11
  129.1 0.0 copy-done
  129.1 0.0 all-reduce.5.cloned.1.call-done
  129.1 1.4 fusion.9
  130.6 64.9 %all-reduce.3.cloned.1.call-done = f32[64,256]{1,0:T(8,128)} async-done(((f32[64,256]{1,0:T(8,128)}), f32[64,256]{1,0:T(8,128)}) %all-reduce.3.cloned.1.call-update) | async-done | bytes 65552 | tf_op jit(solution)/shard_map/psum | solution.py:11
  195.5 1.7 multiply_reduce_fusion
  197.2 5.6 %psum.31 = f32[256]{0:T(256)S(1)} all-reduce(f32[256]{0:T(256)S(1)} %get-tuple-element.4), channel_id=1, replica_groups=mesh['cand'=8,'obs'=4] {'obs'}, use_global_device_ids=true, to_apply=%region_8.9 | all-reduce | flops 256 | bytes 2048 | tf_op jit(solution)/shard_map/psum | solution.py:52
  202.8 0.0 copy-done.1
  202.8 0.6 sub.16
  (6 shorter events, 0.1 us)
Async XLA Ops:
  7.2 79.1 %all-gather.2.cloned.1.call-start = ((), (), s32[]{:S(2)}) async-start(), calls=%async_computation.1 | async-start | bytes 4718592 | tf_op jit(solution)/shard_map/all_gather | solution.py:47
  7.9 121.2 %all-reduce.5.cloned.1.call-start = ((), (), s32[]{:S(2)}) async-start(), calls=%async_computation.2 | async-start | bytes 524288 | tf_op jit(solution)/shard_map/psum | solution.py:49
  9.3 5.0 %copy-start.2 = (s32[128]{0:T(128)S(1)}, s32[128]{0:T(128)}, u32[]{:S(2)}) copy-start(s32[128]{0:T(128)} %param.9) | copy-start | bytes 1540
  86.3 42.8 %copy-start = (f32[256,32]{0,1:T(8,128)S(1)}, f32[256,32]{0,1:T(8,128)}, u32[]{:S(2)}) copy-start(f32[256,32]{0,1:T(8,128)} %param.13) | copy-start | bytes 98308
  86.3 116.5 %copy-start.1 = (f32[256]{0:T(256)S(1)}, f32[256]{0:T(256)}, u32[]{:S(2)}) copy-start(f32[256]{0:T(256)} %param.15) | copy-start | bytes 3076
  92.2 103.2 %all-reduce.3.cloned.1.call-start = ((), (), s32[]{:S(2)}) async-start(), calls=%async_computation | async-start | bytes 131072 | tf_op jit(solution)/shard_map/psum | solution.py:11
Sparse Core Ops, SparseCore 0:
  10.1 76.0 all-gather.1
  92.3 30.2 all-reduce.4
  127.0 68.4 all-reduce.2
where the time goes:
time: 210 us
  waiting for transfers between devices  138 us (66%)
  blocking collectives  40 us (19%)
  between operations  14.5 us (7%)
  matrix products  9.06 us (4%)
  local copies, waits for them, and re-layouts  4.99 us (2%)
  other arithmetic  3.59 us (2%)
    all_gather x1, waiting for transfers between devices, on_device(): lax.all_gather(factor_row, 'cand', axis=0, tiled=True)  72 us
    psum x1, waiting for transfers between devices, spread(): return lax.psum(block, axis)  64.9 us
    psum x1, blocking collectives, spread(): return lax.psum(block, axis)  34.4 us
    dot_general x1, matrix products, on_device(): jnp.einsum('stq,sqc->tc', masked, earlier, preferred_element_type=jnp.flo...  5.94 us
    psum x1, blocking collectives, on_device(): square_sums = lax.psum(jnp.sum(solved_rows * solved_rows, axis=0), 'obs')  5.63 us
    gather x1, local copies, waits for them, and re-layouts, on_device(): earlier = jnp.take(earlier_rows, slot_block, axis=0)  4.98 us
  transfers between devices with their start and end apart: 3, of which 2 were waited for; matrix products, arithmetic and copies ran while one was open for 4% of the time, Pallas kernels for 0%

commit v1 on v0

v1 whole, which is shorter than its diff:
```python
import functools

import jax
import jax.numpy as jnp
from jax import lax
from jax.experimental import pallas as pl
from jax.experimental.pallas import tpu as pltpu
from jax.sharding import PartitionSpec as P

HIGH = lax.Precision.HIGHEST
ROWS = (((0,), (0,)), ((), ()))
VMEM = pl.BlockSpec(memory_space=pltpu.VMEM)
SMEM = pl.BlockSpec(memory_space=pltpu.SMEM)
ANY = pl.BlockSpec(memory_space=pl.ANY)


RING = [(0, 2), (2, 4), (4, 6), (6, 7), (7, 5), (5, 3), (3, 1), (1, 0)]
BACK = [(b, a) for a, b in RING]
OFFSETS = (-1, 1, -2, 2, -3, 3, 0, 4)
LIMIT = 16 * 2**20


def ring_holder(place):
    place = lax.rem(place + 8, 8)
    return jnp.where(place < 4, 2 * place, 2 * (7 - place) + 1)


def panel_product(panel, rows):
    left = panel.reshape(rows.shape[0], panel.shape[-1])
    return lax.dot_general(left, rows, ROWS, preferred_element_type=jnp.float32)


def collect_kernel(slot_block, current, panel, earlier, rows, total, sem):
    slots, depth = panel.shape[:2]
    cand = lax.axis_index("cand")
    place = jnp.where(lax.rem(cand, 2) == 0, cand // 2, 7 - cand // 2)
    for i, offset in enumerate(OFFSETS):
        base = ring_holder(place + offset) * slots

        @pl.loop(0, slots)
        def _(s):
            block = slot_block[base + s]
            pltpu.make_async_copy(earlier.at[block], rows.at[i * slots + s], sem).start()

    pltpu.make_async_copy(earlier, rows, sem).wait()
    for i, offset in enumerate(OFFSETS):
        base = ring_holder(place + offset) * slots

        @pl.loop(0, slots)
        def _(s):
            @pl.when(slot_block[base + s] >= current[0])
            def _():
                rows[i * slots + s] = jnp.zeros(rows.shape[1:], rows.dtype)

    own = OFFSETS.index(0) * slots
    total[...] = panel_product(panel[...], rows[own : own + slots].reshape(slots * depth, rows.shape[-1]))


def collect(slot_block, current, panel, earlier):
    rows, cols = panel.shape[2], earlier.shape[-1]
    return pl.pallas_call(
        collect_kernel,
        out_shape=[
            jax.ShapeDtypeStruct(earlier.shape, earlier.dtype),
            jax.ShapeDtypeStruct((rows, cols), jnp.float32),
        ],
        in_specs=[SMEM, SMEM, VMEM, ANY],
        out_specs=[VMEM, VMEM],
        scratch_shapes=[pltpu.SemaphoreType.DMA],
        compiler_params=pltpu.CompilerParams(vmem_limit_bytes=LIMIT),
        cost_estimate=pl.CostEstimate(
            flops=2 * panel.size * cols, bytes_accessed=4 * earlier.size, transcendentals=0
        ),
    )(slot_block, current, panel, earlier)


def add_kernel(panel_a, panel_b, rows, before, total):
    half = rows.shape[0] * rows.shape[1] // 2
    right = rows[...].reshape(2 * half, rows.shape[-1])
    value = panel_product(panel_a[...], right[:half]) + panel_product(panel_b[...], right[half:])
    total[...] = before[...] + value


def add_last_kernel(panel_a, panel_b, rows, before, mine, other):
    half = rows.shape[0] * rows.shape[1] // 2
    right = rows[...].reshape(2 * half, rows.shape[-1])
    value = panel_product(panel_a[...], right[:half]) + panel_product(panel_b[...], right[half:])
    value = before[...] + value
    size = mine.shape[0]
    first = lax.rem(lax.axis_index("obs"), 2) == 0
    mine[...] = jnp.where(first, value[:size], value[size:])
    other[...] = jnp.where(first, value[size:], value[:size])


def add(panels, rows, position, before, last=False):
    slots, depth, size = panels[0].shape
    cols = rows.shape[-1]
    shape = (size // 2, cols) if last else (size, cols)
    return pl.pallas_call(
        add_last_kernel if last else add_kernel,
        grid=(1,),
        out_shape=[jax.ShapeDtypeStruct(shape, jnp.float32)] * (2 if last else 1),
        in_specs=[
            pl.BlockSpec(panels[0].shape, lambda i: (0, 0, 0)),
            pl.BlockSpec(panels[0].shape, lambda i: (0, 0, 0)),
            pl.BlockSpec((2 * slots, depth, cols), lambda i: (position, 0, 0)),
            pl.BlockSpec((size, cols), lambda i: (0, 0)),
        ],
        out_specs=[pl.BlockSpec(shape, lambda i: (0, 0))] * (2 if last else 1),
        compiler_params=pltpu.CompilerParams(vmem_limit_bytes=LIMIT),
        cost_estimate=pl.CostEstimate(
            flops=4 * panels[0].size * cols, bytes_accessed=8 * panels[0].size, transcendentals=0
        ),
    )(*panels, rows, before)


def tile_kernel(spread_0, spread_1, spread_2, spread_3, cands, tile, points):
    obs = lax.axis_index("obs")
    share = points.shape[0] // 4
    for m, spread in enumerate((spread_0, spread_1, spread_2, spread_3)):
        points[pl.ds(pl.multiple_of((obs ^ m) * share, share), share), :] = spread[-share:, :]
    p = points[...]
    p = p / jnp.sum(p, axis=0, keepdims=True)
    c = cands[...]
    c = c / jnp.sum(c, axis=0, keepdims=True)
    cross = lax.dot_general(p, c, ROWS, precision=HIGH, preferred_element_type=jnp.float32)
    norms = lax.dot_general(p * p, jnp.ones_like(c), ROWS, precision=HIGH, preferred_element_type=jnp.float32)
    squared = norms + jnp.sum(c * c, axis=0, keepdims=True) - 2.0 * cross
    tile[...] = jnp.exp(-10.0 * squared)


def solve_kernel(mine, other, mate, far, mate_far, tile, s0, s1, s2, s3, prior, solved, remaining, residual):
    half, rows = mine.shape[0], solved.shape[0]
    core = lax.rem(lax.axis_index("obs"), 2)
    first = pl.ds(pl.multiple_of(core * half, half), half)
    second = pl.ds(pl.multiple_of((1 - core) * half, half), half)
    residual[first, :] = tile[first, :] - (mine[...] + mate[half:, :] + far[...])
    residual[second, :] = tile[second, :] - (other[...] + mate[:half, :] + mate_far[...])
    value = residual[...]
    squares = jnp.zeros(remaining.shape, jnp.float32)
    for m, spread in enumerate((s0, s1, s2, s3)):
        part = jnp.dot(spread[:rows, :], value, precision=HIGH, preferred_element_type=jnp.float32)
        squares += jnp.sum(part * part, axis=0, keepdims=True)
        if m == 0:
            solved[...] = part
    remaining[...] = prior[...] - squares


def on_ring(
    block_index,
    slot_block,
    factor_row,
    earlier_rows,
    obs_weights,
    cand_weights,
    block_inverse,
    prior_var,
):
    cand, obs = lax.axis_index("cand"), lax.axis_index("obs")
    current = block_index[0]
    held = obs_weights.shape[0]
    half = held // 2
    cols = earlier_rows.shape[2]
    panel = jnp.swapaxes(factor_row, 1, 2)

    def flip(value, axis, bits, size):
        return lax.ppermute(value, axis, [(i, i ^ bits) for i in range(size)])

    slot_here = current % held
    inverse_rows = lax.dynamic_index_in_dim(block_inverse, slot_here, 0, keepdims=False)
    points = lax.dynamic_index_in_dim(jnp.swapaxes(obs_weights, 1, 2), slot_here, 0, keepdims=False)
    share = points.shape[0] // 4
    points = lax.dynamic_slice_in_dim(points, obs * share, share, 0)
    spread = jnp.concatenate([inverse_rows, points], axis=0)
    spread = jnp.where(cand == current // held, spread, jnp.zeros_like(spread))

    tie = lax.optimization_barrier
    forward = [panel, lax.ppermute(panel, "cand", RING)]
    backward = [panel, lax.ppermute(panel, "cand", BACK)]
    rows, total = collect(slot_block, block_index, panel, earlier_rows)
    spread = spread + flip(spread, "cand", 1, 8)
    forward[1], backward[1], rows, total, spread = tie((forward[1], backward[1], rows, total, spread))

    forward.append(lax.ppermute(forward[1], "cand", RING))
    backward.append(lax.ppermute(backward[1], "cand", BACK))
    (total,) = add([forward[1], backward[1]], rows, 0, total)
    spread = spread + flip(spread, "cand", 2, 8)
    spread = spread + flip(spread, "cand", 4, 8)
    forward[2], backward[2], total, spread = tie((forward[2], backward[2], total, spread))

    forward.append(lax.ppermute(forward[2], "cand", RING))
    backward.append(lax.ppermute(backward[2], "cand", BACK))
    (total,) = add([forward[2], backward[2]], rows, 1, total)
    spreads = [spread, flip(spread, "obs", 1, 4)]
    spreads += [flip(spreads[0], "obs", 2, 4), flip(spreads[1], "obs", 2, 4)]
    forward[3], backward[3], total, spreads = tie((forward[3], backward[3], total, spreads))

    forward.append(lax.ppermute(forward[3][:half], "cand", RING))
    backward.append(lax.ppermute(backward[3][half:], "cand", BACK))
    (total,) = add([forward[3], backward[3]], rows, 2, total)
    tile = pl.pallas_call(
        tile_kernel,
        out_shape=jax.ShapeDtypeStruct((panel.shape[2], cols), jnp.float32),
        in_specs=[VMEM] * 5,
        out_specs=VMEM,
        scratch_shapes=[pltpu.VMEM((obs_weights.shape[2], panel.shape[2]), jnp.float32)],
        compiler_params=pltpu.CompilerParams(vmem_limit_bytes=LIMIT),
        cost_estimate=pl.CostEstimate(flops=10**7, bytes_accessed=10**6, transcendentals=65536),
    )(*spreads, cand_weights.T)

    forward[4], backward[4], total, tile = tie((forward[4], backward[4], total, tile))
    mine, other = add([forward[4], backward[4]], rows, OFFSETS.index(4), total, last=True)

    mate = flip(jnp.concatenate([mine, other], axis=0), "obs", 1, 4)
    far = flip(mine + mate[mine.shape[0] :], "obs", 2, 4)
    mate_far = flip(far, "obs", 1, 4)
    solved_rows, remaining = pl.pallas_call(
        solve_kernel,
        out_shape=[
            jax.ShapeDtypeStruct(inverse_rows.shape[:1] + (cols,), jnp.float32),
            jax.ShapeDtypeStruct((1, cols), jnp.float32),
        ],
        in_specs=[VMEM] * 11,
        out_specs=[VMEM] * 2,
        scratch_shapes=[pltpu.VMEM((panel.shape[2], cols), jnp.float32)],
        compiler_params=pltpu.CompilerParams(vmem_limit_bytes=LIMIT),
        cost_estimate=pl.CostEstimate(flops=2 * 10**8, bytes_accessed=10**6, transcendentals=0),
    )(mine, other, mate, far, mate_far, tile, *spreads, prior_var[None])
    return (solved_rows, remaining[0])


def kernel_tile(points, cands):
    points = points / jnp.sum(points, axis=0, keepdims=True)
    cands = cands / jnp.sum(cands, axis=0, keepdims=True)
    squared = jnp.sum(points * points, axis=0)[:, None] + jnp.sum(cands * cands, axis=0)[None, :]
    squared = squared - 2.0 * lax.dot_general(points, cands, ROWS, precision=HIGH)
    return jnp.exp(-10.0 * squared)


def spread_all(block, axis, holder):
    block = jnp.where(lax.axis_index(axis) == holder, block, jnp.zeros_like(block))
    return lax.psum(block, axis)


def on_any(
    block_index,
    slot_block,
    factor_row,
    earlier_rows,
    obs_weights,
    cand_weights,
    block_inverse,
    prior_var,
):
    current = block_index[0]
    held = obs_weights.shape[0]
    points = lax.dynamic_index_in_dim(obs_weights, current % held, 0, keepdims=False)
    inverse_rows = lax.dynamic_index_in_dim(block_inverse, current % held, 0, keepdims=False)
    points = spread_all(points, "cand", current // held)
    inverse_rows = spread_all(inverse_rows, "cand", current // held)
    kernel_rows = kernel_tile(points.T, cand_weights.T)
    panel = lax.all_gather(factor_row, "cand", axis=0, tiled=True)
    panel = panel * (slot_block < current).astype(jnp.bfloat16)[:, None, None]
    earlier = jnp.take(earlier_rows, slot_block, axis=0)
    partial_sum = jnp.einsum("stq,sqc->tc", panel, earlier, preferred_element_type=jnp.float32)
    residual = kernel_rows - lax.psum(partial_sum, "obs")
    solved_rows = jnp.dot(inverse_rows, residual, precision=HIGH)
    square_sums = lax.psum(jnp.sum(solved_rows * solved_rows, axis=0), "obs")
    return (solved_rows, prior_var - square_sums)


def solution(mesh):
    placed = (
        P(),
        P(),
        P("cand", None, "obs"),
        P(None, "obs", "cand"),
        P("cand", None, None),
        P("cand", None),
        P("cand", "obs", None),
        P("cand"),
    )
    small = mesh.shape["cand"] == 8 and mesh.shape["obs"] == 4
    return jax.shard_map(
        on_ring if small else on_any,
        mesh=mesh,
        in_specs=placed,
        out_specs=(P("obs", "cand"), P("cand")),
        check_vma=False,
    )
```

time: 210 us -> 72.6 us (0.35)
  waiting for transfers between devices: 138 us -> 32.1 us
  blocking collectives: 40 us -> 0 us
  starting transfers between devices: 0.12 us -> 20.6 us
  Pallas kernels: 0 us -> 13.2 us
  between operations: 14.5 us -> 1.52 us
  matrix products: 9.06 us -> 0 us
  other arithmetic: 3.59 us -> 0.09 us
    all_gather x1 -> x0, waiting for transfers between devices: 72 us -> none  [on_device(): lax.all_gather(factor_row, 'cand', axis=0, tiled=True)]
    psum x2 -> x0, waiting for transfers between devices: 64.9 us -> none  [the longest x1 64.9 us: spread(): return lax.psum(block, axis)]
    psum x2 -> x0, blocking collectives: 40 us -> none  [the longest x1 34.4 us: spread(): return lax.psum(block, axis)]
    ppermute x0 -> x17, waiting for transfers between devices: none -> 32.1 us  [the longest x9 24.1 us: flip(): return lax.ppermute(value, axis, [(i, i ^ bits) for i in range(size)])]
    ppermute x0 -> x17, starting transfers between devices: none -> 20.6 us  [the longest x9 11.3 us: flip(): return lax.ppermute(value, axis, [(i, i ^ bits) for i in range(size)])]
    pallas_call x0 -> x7, Pallas kernels: none -> 13.2 us  [the longest x1 9.49 us: collect(): pl.pallas_call(collect_kernel, out_shape=[jax.ShapeDtypeStruct(earlier.sh...]
    dot_general x3 -> x0, matrix products: 9.06 us -> none  [the longest x1 5.94 us: on_device(): jnp.einsum('stq,sqc->tc', masked, earlier, preferred_element_type=jnp.flo...]
    gather x1 -> x0, local copies, waits for them, and re-layouts: 4.98 us -> none  [on_device(): earlier = jnp.take(earlier_rows, slot_block, axis=0)]
  transfers between devices with their start and end apart: 3 -> 17, of which waited for: 2 -> 11; matrix products, arithmetic and copies ran while one was open for 4% -> 1% of each run, Pallas kernels for 0% -> 16%
where the time goes in v1:
time: 72.6 us; the launch traced here: 72.3 us
  waiting for transfers between devices  32.1 us (44%)
  starting transfers between devices  20.6 us (28%)
  Pallas kernels  13.2 us (18%)
  local copies, waits for them, and re-layouts  4.68 us (6%)
  between operations  1.52 us (2%)
    ppermute x9, waiting for transfers between devices, flip(): return lax.ppermute(value, axis, [(i, i ^ bits) for i in range(size)])  24.1 us
    ppermute x9, starting transfers between devices, flip(): return lax.ppermute(value, axis, [(i, i ^ bits) for i in range(size)])  11.3 us
    pallas_call x1, Pallas kernels, collect(): pl.pallas_call(collect_kernel, out_shape=[jax.ShapeDtypeStruct(earlier.sh...  9.49 us
    unnamed x12, local copies, waits for them, and re-layouts  3.91 us
    ppermute x1, waiting for transfers between devices, on_ring(): forward.append(lax.ppermute(forward[3][:half], 'cand', RING))  3.12 us
    ppermute x1, starting transfers between devices, on_ring(): forward = [panel, lax.ppermute(panel, 'cand', RING)]  3.08 us
    ppermute x1, waiting for transfers between devices, on_ring(): forward.append(lax.ppermute(forward[2], 'cand', RING))  2.39 us
    ppermute x1, waiting for transfers between devices, on_ring(): backward.append(lax.ppermute(backward[3][half:], 'cand', BACK))  2.1 us
  transfers between devices with their start and end apart: 17, of which 11 were waited for; matrix products, arithmetic and copies ran while one was open for 1% of the time, Pallas kernels for 16%

profile of v1, /device:TPU:0, one launch (start us, length us, event | category | flops | bytes accessed | tf_op | source)
XLA Modules:
  0.0 72.3 jit_solution(8601638986839022417)
XLA Ops:
  0.6 0.0 copy-start
  0.6 3.1 %collective-permute-start = (bf16[16,64,256]{2,1,0:T(8,128)(2,1)}, bf16[16,64,256]{2,1,0:T(8,128)(2,1)S(1)}, u32[]{:S(2)}, u32[]{:S(2)}) collective-permute-start(bf16[16,64,256]{2,1,0:T(8,128)(2,1)} %bitcast.15), channel_id=1, source_target_pairs={{0,8},{8,16},{16,24},{24,28},{28,20},{20,12},{12,4},{4,0},{1,9},{9... | collective-permute-start | bytes 1572872 | tf_op jit(solution)/shard_map/ppermute | solution.py:178
  3.7 0.0 collective-permute-start.1
  4.4 0.7 %dynamic-slice_bitcast_fusion.1 = f32[8,256]{1,0:T(8,128)S(1)} fusion(f32[16,256,32]{1,2,0:T(8,128)} %param.12, s32[]{:T(128)S(6)} %select_n.36, s32[]{:T(128)S(6)} %select_n.38), kind=kLoop, calls=%fused_computation.4 | loop fusion | bytes 16392 | tf_op jit(solution)/shard_map/dynamic_slice | solution.py:173
  5.2 2.0 %collective-permute-start.2 = (f32[72,256]{1,0:T(8,128)S(1)}, f32[72,256]{1,0:T(8,128)S(1)}, u32[]{:S(2)}, u32[]{:S(2)}) collective-permute-start(f32[72,256]{1,0:T(8,128)S(1)} %maximum_select_fusion), channel_id=1, source_target_pairs={{0,4},{4,0},{8,12},{12,8},{16,20},{20,16},{24,28},{28,24},{1,5},{5... | collective-permute-start | bytes 221192 | tf_op jit(solution)/shard_map/ppermute | solution.py:167
  7.2 2.2 %copy-done.1 = bf16[128,64,256]{2,1,0:T(8,128)(2,1)S(1)} copy-done((bf16[128,64,256]{2,1,0:T(8,128)(2,1)S(1)}, bf16[128,64,256]{2,1,0:T(8,128)(2,1)}, u32[]{:S(2)}) %copy-start.1) | copy-done | bytes 4194328
  9.4 1.0 %copy-done.2 = bf16[16,256,64]{1,2,0:T(8,128)(2,1)S(1)} copy-done((bf16[16,256,64]{1,2,0:T(8,128)(2,1)S(1)}, bf16[16,256,64]{1,2,0:T(8,128)(2,1)}, u32[]{:S(2)}) %copy-start.2) | copy-done | bytes 524312
  10.4 0.7 copy-done.5
  11.1 9.5 %shard_map.95 = (bf16[128,64,256]{2,1,0:T(8,128)(2,1)S(1)}, f32[256,256]{1,0:T(8,128)S(1)}) custom-call(s32[128]{0:T(128)S(1)} %copy-done.5, s32[1]{0:T(128)} %copy.10.current, bf16[16,64,256]{2,1,0:T(8,128)(2,1)S(1)} %bitcast.17, bf16[128,64,256]{2,1,0:T(8,128)(2,1)S(1)} %copy-done.1), custom_call_target="tpu_custom_call" | custom-call | flops 134217728 | bytes 8388608 | tf_op jit(solution)/shard_map/pallas_call | solution.py:61
  20.6 0.0 collective-permute-done.2
  20.6 0.0 collective-permute-done.panel_a
  20.6 0.0 collective-permute-done.1.panel_b
  20.6 1.6 %collective-permute-start.3 = (bf16[16,64,256]{2,1,0:T(8,128)(2,1)S(1)}, bf16[16,64,256]{2,1,0:T(8,128)(2,1)S(1)}, u32[]{:S(2)}, u32[]{:S(2)}) collective-permute-start(bf16[16,64,256]{2,1,0:T(8,128)(2,1)S(1)} %collective-permute-done.panel_a), channel_id=1, source_target_pairs={{0,8},{8,16},{16,24},{24,28},{28,20},{20,12},{12,4},{4,0},{1,9},{9... | collective-permute-start | bytes 1572872 | tf_op jit(solution)/shard_map/ppermute | solution.py:184
  22.2 0.4 collective-permute-start.4
  22.7 1.6 %collective-permute-start.5 = (f32[72,256]{1,0:T(8,128)S(1)}, f32[72,256]{1,0:T(8,128)S(1)}, u32[]{:S(2)}, u32[]{:S(2)}) collective-permute-start(f32[72,256]{1,0:T(8,128)S(1)} %add.32), channel_id=1, source_target_pairs={{0,8},{4,12},{8,0},{12,4},{16,24},{20,28},{24,16},{28,20},{1,9},{5... | collective-permute-start | bytes 221192 | tf_op jit(solution)/shard_map/ppermute | solution.py:167
  24.3 12.1 %collective-permute-done.5 = f32[72,256]{1,0:T(8,128)S(1)} collective-permute-done((f32[72,256]{1,0:T(8,128)S(1)}, f32[72,256]{1,0:T(8,128)S(1)}, u32[]{:S(2)}, u32[]{:S(2)}) %collective-permute-start.5) | collective-permute-done | bytes 73760 | tf_op jit(solution)/shard_map/ppermute | solution.py:167
  36.4 3.3 %collective-permute-start.6 = (f32[72,256]{1,0:T(8,128)S(1)}, f32[72,256]{1,0:T(8,128)S(1)}, u32[]{:S(2)}, u32[]{:S(2)}) collective-permute-start(f32[72,256]{1,0:T(8,128)S(1)} %add.33), channel_id=1, source_target_pairs={{0,16},{4,20},{8,24},{12,28},{16,0},{20,4},{24,8},{28,12},{1,17},{... | collective-permute-start | bytes 221192 | tf_op jit(solution)/shard_map/ppermute | solution.py:167
  39.6 0.5 shard_map.96.before
  40.1 0.0 copy-start.3
  40.2 2.1 %collective-permute-done.6 = f32[72,256]{1,0:T(8,128)S(1)} collective-permute-done((f32[72,256]{1,0:T(8,128)S(1)}, f32[72,256]{1,0:T(8,128)S(1)}, u32[]{:S(2)}, u32[]{:S(2)}) %collective-permute-start.6) | collective-permute-done | bytes 73760 | tf_op jit(solution)/shard_map/ppermute | solution.py:167
  42.3 0.0 collective-permute-done.3.panel_a
  42.3 0.0 collective-permute-done.4.panel_b
  42.3 0.1 collective-permute-start.7
  42.4 2.0 %collective-permute-start.8 = (bf16[16,64,256]{2,1,0:T(8,128)(2,1)S(1)}, bf16[16,64,256]{2,1,0:T(8,128)(2,1)S(1)}, u32[]{:S(2)}, u32[]{:S(2)}) collective-permute-start(bf16[16,64,256]{2,1,0:T(8,128)(2,1)S(1)} %collective-permute-done.4.panel_b), channel_id=1, source_target_pairs={{8,0},{16,8},{24,16},{28,24},{20,28},{12,20},{4,12},{0,4},{9,1},{1... | collective-permute-start | bytes 1572872 | tf_op jit(solution)/shard_map/ppermute | solution.py:192
  44.4 0.0 collective-permute-start.9
  44.4 1.5 %collective-permute-start.10 = (f32[72,256]{1,0:T(8,128)S(1)}, f32[72,256]{1,0:T(8,128)S(1)}, u32[]{:S(2)}, u32[]{:S(2)}) collective-permute-start(f32[72,256]{1,0:T(8,128)S(1)} %add.34.spread_0.s0), channel_id=1, source_target_pairs={{0,2},{1,3},{2,0},{3,1},{4,6},{5,7},{6,4},{7,5},{8,10},{9,11},{10,... | collective-permute-start | bytes 221192 | tf_op jit(solution)/shard_map/ppermute | solution.py:167
  45.9 0.0 collective-permute-done.9.spread_1.s1
  45.9 1.3 %collective-permute-start.11 = (f32[72,256]{1,0:T(8,128)S(1)}, f32[72,256]{1,0:T(8,128)S(1)}, u32[]{:S(2)}, u32[]{:S(2)}) collective-permute-start(f32[72,256]{1,0:T(8,128)S(1)} %collective-permute-done.9.spread_1.s1), channel_id=1, source_target_pairs={{0,2},{1,3},{2,0},{3,1},{4,6},{5,7},{6,4},{7,5},{8,10},{9,11},{10,... | collective-permute-start | bytes 221192 | tf_op jit(solution)/shard_map/ppermute | solution.py:167
  47.2 0.5 shard_map.97.before
  47.7 1.8 %collective-permute-done.10.spread_2.s2 = f32[72,256]{1,0:T(8,128)S(1)} collective-permute-done((f32[72,256]{1,0:T(8,128)S(1)}, f32[72,256]{1,0:T(8,128)S(1)}, u32[]{:S(2)}, u32[]{:S(2)}) %collective-permute-start.10) | collective-permute-done | bytes 73760 | tf_op jit(solution)/shard_map/ppermute | solution.py:167
  49.5 1.2 %collective-permute-done.11.spread_3.s3 = f32[72,256]{1,0:T(8,128)S(1)} collective-permute-done((f32[72,256]{1,0:T(8,128)S(1)}, f32[72,256]{1,0:T(8,128)S(1)}, u32[]{:S(2)}, u32[]{:S(2)}) %collective-permute-start.11) | collective-permute-done | bytes 73760 | tf_op jit(solution)/shard_map/ppermute | solution.py:167
  50.7 2.4 %collective-permute-done.7.panel_a = bf16[16,64,256]{2,1,0:T(8,128)(2,1)S(1)} collective-permute-done((bf16[16,64,256]{2,1,0:T(8,128)(2,1)S(1)}, bf16[16,64,256]{2,1,0:T(8,128)(2,1)S(1)}, u32[]{:S(2)}, u32[]{:S(2)}) %collective-permute-start.7) | collective-permute-done | bytes 524320 | tf_op jit(solution)/shard_map/ppermute | solution.py:191
  53.1 0.4 collective-permute-done.8.panel_b
  53.5 2.1 %collective-permute-start.12 = (bf16[8,64,256]{2,1,0:T(8,128)(2,1)S(1)}, bf16[8,64,256]{2,1,0:T(8,128)(2,1)S(1)}, u32[]{:S(2)}, u32[]{:S(2)}) collective-permute-start(bf16[8,64,256]{2,1,0:T(8,128)(2,1)S(1)} %slice.9), channel_id=1, source_target_pairs={{0,8},{8,16},{16,24},{24,28},{28,20},{20,12},{12,4},{4,0},{1,9},{9... | collective-permute-start | bytes 786440 | tf_op jit(solution)/shard_map/ppermute | solution.py:198
  55.6 0.1 collective-permute-start.13
  55.7 0.6 shard_map.99.tile
  56.3 0.5 shard_map.98.before
  56.8 0.0 copy-start.4
  56.8 3.1 %collective-permute-done.12.panel_a = bf16[8,64,256]{2,1,0:T(8,128)(2,1)S(1)} collective-permute-done((bf16[8,64,256]{2,1,0:T(8,128)(2,1)S(1)}, bf16[8,64,256]{2,1,0:T(8,128)(2,1)S(1)}, u32[]{:S(2)}, u32[]{:S(2)}) %collective-permute-start.12) | collective-permute-done | bytes 262176 | tf_op jit(solution)/shard_map/ppermute | solution.py:198
  59.9 2.1 %collective-permute-done.13.panel_b = bf16[8,64,256]{2,1,0:T(8,128)(2,1)S(1)} collective-permute-done((bf16[8,64,256]{2,1,0:T(8,128)(2,1)S(1)}, bf16[8,64,256]{2,1,0:T(8,128)(2,1)S(1)}, u32[]{:S(2)}, u32[]{:S(2)}) %collective-permute-start.13) | collective-permute-done | bytes 262176 | tf_op jit(solution)/shard_map/ppermute | solution.py:199
  62.0 0.4 shard_map.100
  62.4 0.1 collective-permute-start.14
  62.5 1.5 %collective-permute-done.14.mate = f32[256,256]{1,0:T(8,128)S(1)} collective-permute-done((f32[256,256]{1,0:T(8,128)S(1)}, f32[256,256]{1,0:T(8,128)S(1)}, u32[]{:S(2)}, u32[]{:S(2)}) %collective-permute-start.14) | collective-permute-done | bytes 262176 | tf_op jit(solution)/shard_map/ppermute | solution.py:167
  64.0 1.6 %collective-permute-start.15 = (f32[128,256]{1,0:T(8,128)S(1)}, f32[128,256]{1,0:T(8,128)S(1)}, u32[]{:S(2)}, u32[]{:S(2)}) collective-permute-start(f32[128,256]{1,0:T(8,128)S(1)} %slice_add_fusion), channel_id=1, source_target_pairs={{0,2},{1,3},{2,0},{3,1},{4,6},{5,7},{6,4},{7,5},{8,10},{9,11},{10,... | collective-permute-start | bytes 393224 | tf_op jit(solution)/shard_map/ppermute | solution.py:167
  65.6 4.0 %collective-permute-done.15.far = f32[128,256]{1,0:T(8,128)S(1)} collective-permute-done((f32[128,256]{1,0:T(8,128)S(1)}, f32[128,256]{1,0:T(8,128)S(1)}, u32[]{:S(2)}, u32[]{:S(2)}) %collective-permute-start.15) | collective-permute-done | bytes 131104 | tf_op jit(solution)/shard_map/ppermute | solution.py:167
  69.6 0.0 collective-permute-start.16
  69.6 1.3 %collective-permute-done.16.mate_far = f32[128,256]{1,0:T(8,128)S(1)} collective-permute-done((f32[128,256]{1,0:T(8,128)S(1)}, f32[128,256]{1,0:T(8,128)S(1)}, u32[]{:S(2)}, u32[]{:S(2)}) %collective-permute-start.16) | collective-permute-done | bytes 131104 | tf_op jit(solution)/shard_map/ppermute | solution.py:167
  71.0 1.3 %shard_map.101 = (f32[64,256]{1,0:T(8,128)}, f32[1,256]{1,0:T(1,128)}) custom-call(f32[128,256]{1,0:T(8,128)S(1)} %get-tuple-element.49.mine, f32[128,256]{1,0:T(8,128)S(1)} %get-tuple-element.50.other, f32[256,256]{1,0:T(8,128)S(1)} %collective-permute-done.14.mate, f32[128,256]{1,0:T(8,128)S(1)} %collective-permute-done.15.far, ...), custom_call_target="tpu_custom_call" | custom-call | flops 200000000 | bytes 1000000 | tf_op jit(solution)/shard_map/pallas_call | solution.py:217
  (15 shorter events, 0.1 us)
Async XLA Ops:
  0.6 4.5 %copy-start = (f32[16,64,256]{2,1,0:T(8,128)S(1)}, f32[16,64,256]{2,1,0:T(8,128)}, u32[]{:S(2)}) copy-start(f32[16,64,256]{2,1,0:T(8,128)} %param.14) | copy-start | bytes 3145732
  0.6 20.0 %collective-permute-start = (bf16[16,64,256]{2,1,0:T(8,128)(2,1)}, bf16[16,64,256]{2,1,0:T(8,128)(2,1)S(1)}, u32[]{:S(2)}, u32[]{:S(2)}) collective-permute-start(bf16[16,64,256]{2,1,0:T(8,128)(2,1)} %bitcast.15), channel_id=1, source_target_pairs={{0,8},{8,16},{16,24},{24,28},{28,20},{20,12},{12,4},{4,0},{1,9},{9... | collective-permute-start | bytes 1572872 | tf_op jit(solution)/shard_map/ppermute | solution.py:178
  3.7 16.9 %collective-permute-start.1 = (bf16[16,64,256]{2,1,0:T(8,128)(2,1)}, bf16[16,64,256]{2,1,0:T(8,128)(2,1)S(1)}, u32[]{:S(2)}, u32[]{:S(2)}) collective-permute-start(bf16[16,64,256]{2,1,0:T(8,128)(2,1)} %bitcast.16), channel_id=1, source_target_pairs={{8,0},{16,8},{24,16},{28,24},{20,28},{12,20},{4,12},{0,4},{9,1},{1... | collective-permute-start | bytes 1572872 | tf_op jit(solution)/shard_map/ppermute | solution.py:179
  5.2 15.4 %collective-permute-start.2 = (f32[72,256]{1,0:T(8,128)S(1)}, f32[72,256]{1,0:T(8,128)S(1)}, u32[]{:S(2)}, u32[]{:S(2)}) collective-permute-start(f32[72,256]{1,0:T(8,128)S(1)} %maximum_select_fusion), channel_id=1, source_target_pairs={{0,4},{4,0},{8,12},{12,8},{16,20},{20,16},{24,28},{28,24},{1,5},{5... | collective-permute-start | bytes 221192 | tf_op jit(solution)/shard_map/ppermute | solution.py:167
  7.2 2.2 %copy-start.1 = (bf16[128,64,256]{2,1,0:T(8,128)(2,1)S(1)}, bf16[128,64,256]{2,1,0:T(8,128)(2,1)}, u32[]{:S(2)}) copy-start(bf16[128,64,256]{2,1,0:T(8,128)(2,1)} %earlier.1) | copy-start | bytes 12582916
  9.4 1.0 %copy-start.2 = (bf16[16,256,64]{1,2,0:T(8,128)(2,1)S(1)}, bf16[16,256,64]{1,2,0:T(8,128)(2,1)}, u32[]{:S(2)}) copy-start(bf16[16,256,64]{1,2,0:T(8,128)(2,1)} %param.10) | copy-start | bytes 1572868
  10.4 0.7 copy-start.5
  20.6 21.7 %collective-permute-start.3 = (bf16[16,64,256]{2,1,0:T(8,128)(2,1)S(1)}, bf16[16,64,256]{2,1,0:T(8,128)(2,1)S(1)}, u32[]{:S(2)}, u32[]{:S(2)}) collective-permute-start(bf16[16,64,256]{2,1,0:T(8,128)(2,1)S(1)} %collective-permute-done.panel_a), channel_id=1, source_target_pairs={{0,8},{8,16},{16,24},{24,28},{28,20},{20,12},{12,4},{4,0},{1,9},{9... | collective-permute-start | bytes 1572872 | tf_op jit(solution)/shard_map/ppermute | solution.py:184
  22.2 20.1 %collective-permute-start.4 = (bf16[16,64,256]{2,1,0:T(8,128)(2,1)S(1)}, bf16[16,64,256]{2,1,0:T(8,128)(2,1)S(1)}, u32[]{:S(2)}, u32[]{:S(2)}) collective-permute-start(bf16[16,64,256]{2,1,0:T(8,128)(2,1)S(1)} %collective-permute-done.1.panel_b), channel_id=1, source_target_pairs={{8,0},{16,8},{24,16},{28,24},{20,28},{12,20},{4,12},{0,4},{9,1},{1... | collective-permute-start | bytes 1572872 | tf_op jit(solution)/shard_map/ppermute | solution.py:185
  22.7 13.7 %collective-permute-start.5 = (f32[72,256]{1,0:T(8,128)S(1)}, f32[72,256]{1,0:T(8,128)S(1)}, u32[]{:S(2)}, u32[]{:S(2)}) collective-permute-start(f32[72,256]{1,0:T(8,128)S(1)} %add.32), channel_id=1, source_target_pairs={{0,8},{4,12},{8,0},{12,4},{16,24},{20,28},{24,16},{28,20},{1,9},{5... | collective-permute-start | bytes 221192 | tf_op jit(solution)/shard_map/ppermute | solution.py:167
  36.4 5.9 %collective-permute-start.6 = (f32[72,256]{1,0:T(8,128)S(1)}, f32[72,256]{1,0:T(8,128)S(1)}, u32[]{:S(2)}, u32[]{:S(2)}) collective-permute-start(f32[72,256]{1,0:T(8,128)S(1)} %add.33), channel_id=1, source_target_pairs={{0,16},{4,20},{8,24},{12,28},{16,0},{20,4},{24,8},{28,12},{1,17},{... | collective-permute-start | bytes 221192 | tf_op jit(solution)/shard_map/ppermute | solution.py:167
  40.1 15.5 %copy-start.3 = (f32[256,32]{0,1:T(8,128)S(1)}, f32[256,32]{0,1:T(8,128)}, u32[]{:S(2)}) copy-start(f32[256,32]{0,1:T(8,128)} %param.13) | copy-start | bytes 98308
  42.3 10.7 %collective-permute-start.7 = (bf16[16,64,256]{2,1,0:T(8,128)(2,1)S(1)}, bf16[16,64,256]{2,1,0:T(8,128)(2,1)S(1)}, u32[]{:S(2)}, u32[]{:S(2)}) collective-permute-start(bf16[16,64,256]{2,1,0:T(8,128)(2,1)S(1)} %collective-permute-done.3.panel_a), channel_id=1, source_target_pairs={{0,8},{8,16},{16,24},{24,28},{28,20},{20,12},{12,4},{4,0},{1,9},{9... | collective-permute-start | bytes 1572872 | tf_op jit(solution)/shard_map/ppermute | solution.py:191
  42.4 11.1 %collective-permute-start.8 = (bf16[16,64,256]{2,1,0:T(8,128)(2,1)S(1)}, bf16[16,64,256]{2,1,0:T(8,128)(2,1)S(1)}, u32[]{:S(2)}, u32[]{:S(2)}) collective-permute-start(bf16[16,64,256]{2,1,0:T(8,128)(2,1)S(1)} %collective-permute-done.4.panel_b), channel_id=1, source_target_pairs={{8,0},{16,8},{24,16},{28,24},{20,28},{12,20},{4,12},{0,4},{9,1},{1... | collective-permute-start | bytes 1572872 | tf_op jit(solution)/shard_map/ppermute | solution.py:192
  44.4 1.5 %collective-permute-start.9 = (f32[72,256]{1,0:T(8,128)S(1)}, f32[72,256]{1,0:T(8,128)S(1)}, u32[]{:S(2)}, u32[]{:S(2)}) collective-permute-start(f32[72,256]{1,0:T(8,128)S(1)} %add.34.spread_0.s0), channel_id=1, source_target_pairs={{0,1},{1,0},{2,3},{3,2},{4,5},{5,4},{6,7},{7,6},{8,9},{9,8},{10,11... | collective-permute-start | bytes 221192 | tf_op jit(solution)/shard_map/ppermute | solution.py:167
  44.4 5.0 %collective-permute-start.10 = (f32[72,256]{1,0:T(8,128)S(1)}, f32[72,256]{1,0:T(8,128)S(1)}, u32[]{:S(2)}, u32[]{:S(2)}) collective-permute-start(f32[72,256]{1,0:T(8,128)S(1)} %add.34.spread_0.s0), channel_id=1, source_target_pairs={{0,2},{1,3},{2,0},{3,1},{4,6},{5,7},{6,4},{7,5},{8,10},{9,11},{10,... | collective-permute-start | bytes 221192 | tf_op jit(solution)/shard_map/ppermute | solution.py:167
  45.9 4.7 %collective-permute-start.11 = (f32[72,256]{1,0:T(8,128)S(1)}, f32[72,256]{1,0:T(8,128)S(1)}, u32[]{:S(2)}, u32[]{:S(2)}) collective-permute-start(f32[72,256]{1,0:T(8,128)S(1)} %collective-permute-done.9.spread_1.s1), channel_id=1, source_target_pairs={{0,2},{1,3},{2,0},{3,1},{4,6},{5,7},{6,4},{7,5},{8,10},{9,11},{10,... | collective-permute-start | bytes 221192 | tf_op jit(solution)/shard_map/ppermute | solution.py:167
  53.5 6.4 %collective-permute-start.12 = (bf16[8,64,256]{2,1,0:T(8,128)(2,1)S(1)}, bf16[8,64,256]{2,1,0:T(8,128)(2,1)S(1)}, u32[]{:S(2)}, u32[]{:S(2)}) collective-permute-start(bf16[8,64,256]{2,1,0:T(8,128)(2,1)S(1)} %slice.9), channel_id=1, source_target_pairs={{0,8},{8,16},{16,24},{24,28},{28,20},{20,12},{12,4},{4,0},{1,9},{9... | collective-permute-start | bytes 786440 | tf_op jit(solution)/shard_map/ppermute | solution.py:198
  55.6 6.4 %collective-permute-start.13 = (bf16[8,64,256]{2,1,0:T(8,128)(2,1)S(1)}, bf16[8,64,256]{2,1,0:T(8,128)(2,1)S(1)}, u32[]{:S(2)}, u32[]{:S(2)}) collective-permute-start(bf16[8,64,256]{2,1,0:T(8,128)(2,1)S(1)} %slice.10), channel_id=1, source_target_pairs={{8,0},{16,8},{24,16},{28,24},{20,28},{12,20},{4,12},{0,4},{9,1},{1... | collective-permute-start | bytes 786440 | tf_op jit(solution)/shard_map/ppermute | solution.py:199
  56.8 14.2 %copy-start.4 = (f32[256]{0:T(256)S(1)}, f32[256]{0:T(256)}, u32[]{:S(2)}) copy-start(f32[256]{0:T(256)} %param.15) | copy-start | bytes 3076
  62.4 1.6 %collective-permute-start.14 = (f32[256,256]{1,0:T(8,128)S(1)}, f32[256,256]{1,0:T(8,128)S(1)}, u32[]{:S(2)}, u32[]{:S(2)}) collective-permute-start(f32[256,256]{1,0:T(8,128)S(1)} %pad_maximum_fusion), channel_id=1, source_target_pairs={{0,1},{1,0},{2,3},{3,2},{4,5},{5,4},{6,7},{7,6},{8,9},{9,8},{10,11... | collective-permute-start | bytes 786440 | tf_op jit(solution)/shard_map/ppermute | solution.py:167
  64.0 5.6 %collective-permute-start.15 = (f32[128,256]{1,0:T(8,128)S(1)}, f32[128,256]{1,0:T(8,128)S(1)}, u32[]{:S(2)}, u32[]{:S(2)}) collective-permute-start(f32[128,256]{1,0:T(8,128)S(1)} %slice_add_fusion), channel_id=1, source_target_pairs={{0,2},{1,3},{2,0},{3,1},{4,6},{5,7},{6,4},{7,5},{8,10},{9,11},{10,... | collective-permute-start | bytes 393224 | tf_op jit(solution)/shard_map/ppermute | solution.py:167
  69.6 1.3 %collective-permute-start.16 = (f32[128,256]{1,0:T(8,128)S(1)}, f32[128,256]{1,0:T(8,128)S(1)}, u32[]{:S(2)}, u32[]{:S(2)}) collective-permute-start(f32[128,256]{1,0:T(8,128)S(1)} %collective-permute-done.15.far), channel_id=1, source_target_pairs={{0,1},{1,0},{2,3},{3,2},{4,5},{5,4},{6,7},{7,6},{8,9},{9,8},{10,11... | collective-permute-start | bytes 393224 | tf_op jit(solution)/shard_map/ppermute | solution.py:167

commit v2 on v1

--- a/solution.py
+++ b/solution.py
@@ -16,7 +16,6 @@
 
 RING = [(0, 2), (2, 4), (4, 6), (6, 7), (7, 5), (5, 3), (3, 1), (1, 0)]
 BACK = [(b, a) for a, b in RING]
-OFFSETS = (-1, 1, -2, 2, -3, 3, 0, 4)
 LIMIT = 16 * 2**20
 
 
@@ -25,93 +24,57 @@
     return jnp.where(place < 4, 2 * place, 2 * (7 - place) + 1)
 
 
-def panel_product(panel, rows):
-    left = panel.reshape(rows.shape[0], panel.shape[-1])
-    return lax.dot_general(left, rows, ROWS, preferred_element_type=jnp.float32)
-
-
-def collect_kernel(slot_block, current, panel, earlier, rows, total, sem):
-    slots, depth = panel.shape[:2]
+def partial_sum(sources, slot_block, current, panels, earlier, rows):
     cand = lax.axis_index("cand")
     place = jnp.where(lax.rem(cand, 2) == 0, cand // 2, 7 - cand // 2)
-    for i, offset in enumerate(OFFSETS):
-        base = ring_holder(place + offset) * slots
-
-        @pl.loop(0, slots)
-        def _(s):
+    slots, depth, _ = panels[0].shape
+    value = None
+    for j, (offset, first, held) in enumerate(sources):
+        base = ring_holder(place + offset) * held + first
+        for s in range(slots):
             block = slot_block[base + s]
-            pltpu.make_async_copy(earlier.at[block], rows.at[i * slots + s], sem).start()
-
-    pltpu.make_async_copy(earlier, rows, sem).wait()
-    for i, offset in enumerate(OFFSETS):
-        base = ring_holder(place + offset) * slots
-
-        @pl.loop(0, slots)
-        def _(s):
-            @pl.when(slot_block[base + s] >= current[0])
-            def _():
-                rows[i * slots + s] = jnp.zeros(rows.shape[1:], rows.dtype)
-
-    own = OFFSETS.index(0) * slots
-    total[...] = panel_product(panel[...], rows[own : own + slots].reshape(slots * depth, rows.shape[-1]))
-
-
-def collect(slot_block, current, panel, earlier):
-    rows, cols = panel.shape[2], earlier.shape[-1]
-    return pl.pallas_call(
-        collect_kernel,
-        out_shape=[
-            jax.ShapeDtypeStruct(earlier.shape, earlier.dtype),
-            jax.ShapeDtypeStruct((rows, cols), jnp.float32),
-        ],
-        in_specs=[SMEM, SMEM, VMEM, ANY],
-        out_specs=[VMEM, VMEM],
-        scratch_shapes=[pltpu.SemaphoreType.DMA],
-        compiler_params=pltpu.CompilerParams(vmem_limit_bytes=LIMIT),
-        cost_estimate=pl.CostEstimate(
-            flops=2 * panel.size * cols, bytes_accessed=4 * earlier.size, transcendentals=0
-        ),
-    )(slot_block, current, panel, earlier)
-
-
-def add_kernel(panel_a, panel_b, rows, before, total):
-    half = rows.shape[0] * rows.shape[1] // 2
-    right = rows[...].reshape(2 * half, rows.shape[-1])
-    value = panel_product(panel_a[...], right[:half]) + panel_product(panel_b[...], right[half:])
-    total[...] = before[...] + value
-
-
-def add_last_kernel(panel_a, panel_b, rows, before, mine, other):
-    half = rows.shape[0] * rows.shape[1] // 2
-    right = rows[...].reshape(2 * half, rows.shape[-1])
-    value = panel_product(panel_a[...], right[:half]) + panel_product(panel_b[...], right[half:])
-    value = before[...] + value
+            kept = (block < current[0]).astype(jnp.float32).astype(rows.dtype)
+            rows[j, s * depth : (s + 1) * depth, :] = earlier[block] * kept
+        left = panels[j][...].reshape(slots * depth, panels[j].shape[-1])
+        term = lax.dot_general(left, rows[j], ROWS, preferred_element_type=jnp.float32)
+        value = term if value is None else value + term
+    return value
+
+
+def own_kernel(sources, slot_block, current, panel, earlier, total, rows):
+    total[...] = partial_sum(sources, slot_block, current, [panel], earlier, rows)
+
+
+def add_kernel(sources, slot_block, current, *refs):
+    *panels, earlier, before, total, rows = refs
+    total[...] = before[...] + partial_sum(sources, slot_block, current, panels, earlier, rows)
+
+
+def last_kernel(sources, slot_block, current, panel_a, panel_b, earlier, before, mine, other, rows):
+    value = before[...] + partial_sum(sources, slot_block, current, [panel_a, panel_b], earlier, rows)
     size = mine.shape[0]
     first = lax.rem(lax.axis_index("obs"), 2) == 0
     mine[...] = jnp.where(first, value[:size], value[size:])
     other[...] = jnp.where(first, value[size:], value[:size])
 
 
-def add(panels, rows, position, before, last=False):
+def add(kernel, sources, slot_block, current, panels, earlier, before=()):
     slots, depth, size = panels[0].shape
-    cols = rows.shape[-1]
-    shape = (size // 2, cols) if last else (size, cols)
+    cols = earlier.shape[-1]
+    shapes = [(size // 2, cols)] * 2 if kernel is last_kernel else [(size, cols)]
     return pl.pallas_call(
-        add_last_kernel if last else add_kernel,
-        grid=(1,),
-        out_shape=[jax.ShapeDtypeStruct(shape, jnp.float32)] * (2 if last else 1),
-        in_specs=[
-            pl.BlockSpec(panels[0].shape, lambda i: (0, 0, 0)),
-            pl.BlockSpec(panels[0].shape, lambda i: (0, 0, 0)),
-            pl.BlockSpec((2 * slots, depth, cols), lambda i: (position, 0, 0)),
-            pl.BlockSpec((size, cols), lambda i: (0, 0)),
-        ],
-        out_specs=[pl.BlockSpec(shape, lambda i: (0, 0))] * (2 if last else 1),
+        functools.partial(kernel, sources),
+        out_shape=[jax.ShapeDtypeStruct(shape, jnp.float32) for shape in shapes],
+        in_specs=[SMEM] * 2 + [VMEM] * (len(panels) + 1 + len(before)),
+        out_specs=[VMEM] * len(shapes),
+        scratch_shapes=[pltpu.VMEM((len(panels), slots * depth, cols), earlier.dtype)],
         compiler_params=pltpu.CompilerParams(vmem_limit_bytes=LIMIT),
         cost_estimate=pl.CostEstimate(
-            flops=4 * panels[0].size * cols, bytes_accessed=8 * panels[0].size, transcendentals=0
+            flops=2 * len(panels) * panels[0].size * cols,
+            bytes_accessed=4 * len(panels) * panels[0].size,
+            transcendentals=0,
         ),
-    )(*panels, rows, before)
+    )(slot_block, current, *panels, earlier, *before)
 
 
 def tile_kernel(spread_0, spread_1, spread_2, spread_3, cands, tile, points):
@@ -175,29 +138,25 @@
     spread = jnp.where(cand == current // held, spread, jnp.zeros_like(spread))
 
     tie = lax.optimization_barrier
-    forward = [panel, lax.ppermute(panel, "cand", RING)]
-    backward = [panel, lax.ppermute(panel, "cand", BACK)]
-    rows, total = collect(slot_block, block_index, panel, earlier_rows)
+
+    def onward(pair):
+        return (lax.ppermute(pair[0], "cand", RING), lax.ppermute(pair[1], "cand", BACK))
+
+    early = onward((panel[:half], panel[:half]))
+    late = onward((panel[half:], panel[half:]))
+    (total,) = add(own_kernel, [(0, 0, held)], slot_block, block_index, [panel], earlier_rows)
     spread = spread + flip(spread, "cand", 1, 8)
-    forward[1], backward[1], rows, total, spread = tie((forward[1], backward[1], rows, total, spread))
-
-    forward.append(lax.ppermute(forward[1], "cand", RING))
-    backward.append(lax.ppermute(backward[1], "cand", BACK))
-    (total,) = add([forward[1], backward[1]], rows, 0, total)
-    spread = spread + flip(spread, "cand", 2, 8)
-    spread = spread + flip(spread, "cand", 4, 8)
-    forward[2], backward[2], total, spread = tie((forward[2], backward[2], total, spread))
-
-    forward.append(lax.ppermute(forward[2], "cand", RING))
-    backward.append(lax.ppermute(backward[2], "cand", BACK))
-    (total,) = add([forward[2], backward[2]], rows, 1, total)
+    for k in (1, 2, 3):
+        next_early = onward(early) if k < 3 else lax.ppermute(early[0], "cand", RING)
+        late, total, spread = tie((late, total, spread))
+        next_late = onward(late) if k < 3 else lax.ppermute(late[1], "cand", BACK)
+        sources = [(-k, 0, held), (k, 0, held), (-k, half, held), (k, half, held)]
+        (total,) = add(add_kernel, sources, slot_block, block_index, [*early, *late], earlier_rows, [total])
+        if k < 3:
+            spread = spread + flip(spread, "cand", 2 * k, 8)
+        early, late = next_early, next_late
     spreads = [spread, flip(spread, "obs", 1, 4)]
     spreads += [flip(spreads[0], "obs", 2, 4), flip(spreads[1], "obs", 2, 4)]
-    forward[3], backward[3], total, spreads = tie((forward[3], backward[3], total, spreads))
-
-    forward.append(lax.ppermute(forward[3][:half], "cand", RING))
-    backward.append(lax.ppermute(backward[3][half:], "cand", BACK))
-    (total,) = add([forward[3], backward[3]], rows, 2, total)
     tile = pl.pallas_call(
         tile_kernel,
         out_shape=jax.ShapeDtypeStruct((panel.shape[2], cols), jnp.float32),
@@ -208,8 +167,9 @@
         cost_estimate=pl.CostEstimate(flops=10**7, bytes_accessed=10**6, transcendentals=65536),
     )(*spreads, cand_weights.T)
 
-    forward[4], backward[4], total, tile = tie((forward[4], backward[4], total, tile))
-    mine, other = add([forward[4], backward[4]], rows, OFFSETS.index(4), total, last=True)
+    early, late, total, tile = tie((early, late, total, tile))
+    sources = [(-4, 0, held), (4, half, held)]
+    mine, other = add(last_kernel, sources, slot_block, block_index, [early, late], earlier_rows, [total])
 
     mate = flip(jnp.concatenate([mine, other], axis=0), "obs", 1, 4)
     far = flip(mine + mate[mine.shape[0] :], "obs", 2, 4)

time: 72.6 us -> 68.8 us (0.948)
  starting transfers between devices: 20.6 us -> 28 us
  Pallas kernels: 13.2 us -> 6.84 us
  waiting for transfers between devices: 32.1 us -> 26.2 us
  local copies, waits for them, and re-layouts: 4.68 us -> 5.81 us
    ppermute x8 -> x14, starting transfers between devices: 9.36 us -> 18.8 us  [the longest x6 9.78 us: onward(): lax.ppermute(pair[0], 'cand', RING)]
    ppermute x8 -> x14, waiting for transfers between devices: 8.04 us -> 0.04 us  [the longest x6 0.02 us: onward(): lax.ppermute(pair[1], 'cand', BACK)]
    pallas_call x5, Pallas kernels: 11.3 us -> 4.89 us  [add(): pl.pallas_call(functools.partial(kernel, sources), out_shape=[jax.ShapeDt...]
    ppermute x9, starting transfers between devices: 11.3 us -> 9.23 us  [flip(): return lax.ppermute(value, axis, [(i, i ^ bits) for i in range(size)])]
    ppermute x9, waiting for transfers between devices: 24.1 us -> 26.1 us  [flip(): return lax.ppermute(value, axis, [(i, i ^ bits) for i in range(size)])]
    slice x2 -> x1, local copies, waits for them, and re-layouts: 0.04 us -> 1.15 us  [on_ring(): late = onward((panel[half:], panel[half:]))]
    unnamed x12 -> x14, local copies, waits for them, and re-layouts: 3.91 us -> 3.91 us
  transfers between devices with their start and end apart: 17 -> 23, of which waited for: 11 -> 8; matrix products, arithmetic and copies ran while one was open for 1% -> 1% of each run, Pallas kernels for 16% -> 7%
where the time goes in v2:
time: 68.8 us; the launch traced here: 68.5 us
  starting transfers between devices  28 us (41%)
  waiting for transfers between devices  26.2 us (38%)
  Pallas kernels  6.84 us (10%)
  local copies, waits for them, and re-layouts  5.81 us (8%)
  between operations  1.57 us (2%)
    ppermute x9, waiting for transfers between devices, flip(): return lax.ppermute(value, axis, [(i, i ^ bits) for i in range(size)])  26.1 us
    ppermute x6, starting transfers between devices, onward(): lax.ppermute(pair[0], 'cand', RING)  9.78 us
    ppermute x9, starting transfers between devices, flip(): return lax.ppermute(value, axis, [(i, i ^ bits) for i in range(size)])  9.23 us
    ppermute x6, starting transfers between devices, onward(): lax.ppermute(pair[1], 'cand', BACK)  4.9 us
    pallas_call x5, Pallas kernels, add(): pl.pallas_call(functools.partial(kernel, sources), out_shape=[jax.ShapeDt...  4.89 us
    ppermute x1, starting transfers between devices, on_ring(): next_late = onward(late) if k < 3 else lax.ppermute(late[1], 'cand', BACK)  4.09 us
    unnamed x14, local copies, waits for them, and re-layouts  3.91 us
  transfers between devices with their start and end apart: 23, of which 8 were waited for; matrix products, arithmetic and copies ran while one was open for 1% of the time, Pallas kernels for 7%

profile of v2, /device:TPU:0, one launch (start us, length us, event | category | flops | bytes accessed | tf_op | source)
XLA Modules:
  0.0 68.5 jit_solution(13252950192760506204)
XLA Ops:
  0.6 0.0 copy-start
  0.6 1.2 %fusion = (bf16[8,64,256]{2,1,0:T(8,128)(2,1)S(1)}, bf16[8,64,256]{2,1,0:T(8,128)(2,1)S(1)}) fusion(bf16[16,64,256]{2,1,0:T(8,128)(2,1)} %bitcast.15), kind=kLoop, calls=%fused_computation.5 | loop fusion | bytes 1048576 | tf_op jit(solution)/shard_map/slice | solution.py:146
  1.8 3.1 %collective-permute-start.4 = (bf16[8,64,256]{2,1,0:T(8,128)(2,1)S(1)}, bf16[8,64,256]{2,1,0:T(8,128)(2,1)S(1)}, u32[]{:S(2)}, u32[]{:S(2)}) collective-permute-start(bf16[8,64,256]{2,1,0:T(8,128)(2,1)S(1)} %get-tuple-element.42), channel_id=1, source_target_pairs={{0,8},{8,16},{16,24},{24,28},{28,20},{20,12},{12,4},{4,0},{1,9},{9... | collective-permute-start | bytes 786440 | tf_op jit(solution)/shard_map/ppermute | solution.py:143
  4.9 0.0 collective-permute-start.5
  4.9 2.0 %collective-permute-start = (bf16[8,64,256]{2,1,0:T(8,128)(2,1)S(1)}, bf16[8,64,256]{2,1,0:T(8,128)(2,1)S(1)}, u32[]{:S(2)}, u32[]{:S(2)}) collective-permute-start(bf16[8,64,256]{2,1,0:T(8,128)(2,1)S(1)} %get-tuple-element.43), channel_id=1, source_target_pairs={{0,8},{8,16},{16,24},{24,28},{28,20},{20,12},{12,4},{4,0},{1,9},{9... | collective-permute-start | bytes 786440 | tf_op jit(solution)/shard_map/ppermute | solution.py:143
  7.6 0.7 %dynamic-slice_bitcast_fusion.1 = f32[8,256]{1,0:T(8,128)S(1)} fusion(f32[16,256,32]{1,2,0:T(8,128)} %param.12, s32[]{:T(128)S(6)} %select_n.36, s32[]{:T(128)S(6)} %select_n.38), kind=kLoop, calls=%fused_computation.4 | loop fusion | bytes 16392 | tf_op jit(solution)/shard_map/dynamic_slice | solution.py:136
  8.4 0.1 collective-permute-start.6
  8.5 2.0 %collective-permute-start.9 = (bf16[8,64,256]{2,1,0:T(8,128)(2,1)S(1)}, bf16[8,64,256]{2,1,0:T(8,128)(2,1)S(1)}, u32[]{:S(2)}, u32[]{:S(2)}) collective-permute-start(bf16[8,64,256]{2,1,0:T(8,128)(2,1)S(1)} %get-tuple-element.43), channel_id=1, source_target_pairs={{8,0},{16,8},{24,16},{28,24},{20,28},{12,20},{4,12},{0,4},{9,1},{1... | collective-permute-start | bytes 786440 | tf_op jit(solution)/shard_map/ppermute | solution.py:143
  10.5 2.2 %copy-done.1 = bf16[128,64,256]{2,1,0:T(8,128)(2,1)S(1)} copy-done((bf16[128,64,256]{2,1,0:T(8,128)(2,1)S(1)}, bf16[128,64,256]{2,1,0:T(8,128)(2,1)}, u32[]{:S(2)}) %copy-start.1) | copy-done | bytes 4194328
  12.7 1.0 %copy-done.3 = bf16[16,256,64]{1,2,0:T(8,128)(2,1)S(1)} copy-done((bf16[16,256,64]{1,2,0:T(8,128)(2,1)S(1)}, bf16[16,256,64]{1,2,0:T(8,128)(2,1)}, u32[]{:S(2)}) %copy-start.3) | copy-done | bytes 524312
  13.7 0.7 copy-done.5
  14.4 0.9 %shard_map.95.refs_5_ = f32[256,256]{1,0:T(8,128)S(1)} custom-call(s32[128]{0:T(128)S(1)} %copy-done.5, s32[1]{0:T(128)} %copy.10.current, bf16[16,64,256]{2,1,0:T(8,128)(2,1)S(1)} %bitcast.16, bf16[128,64,256]{2,1,0:T(8,128)(2,1)S(1)} %copy-done.1), custom_call_target="tpu_custom_call" | custom-call | flops 134217728 | bytes 1048576 | tf_op jit(solution)/shard_map/pallas_call | solution.py:65
  15.3 3.0 %collective-permute-done.6 = f32[72,256]{1,0:T(8,128)S(1)} collective-permute-done((f32[72,256]{1,0:T(8,128)S(1)}, f32[72,256]{1,0:T(8,128)S(1)}, u32[]{:S(2)}, u32[]{:S(2)}) %collective-permute-start.6) | collective-permute-done | bytes 73760 | tf_op jit(solution)/shard_map/ppermute | solution.py:130
  18.3 0.0 collective-permute-done.5.refs_3_
  18.3 0.1 collective-permute-start.7
  18.4 2.0 %collective-permute-start.8 = (bf16[8,64,256]{2,1,0:T(8,128)(2,1)S(1)}, bf16[8,64,256]{2,1,0:T(8,128)(2,1)S(1)}, u32[]{:S(2)}, u32[]{:S(2)}) collective-permute-start(bf16[8,64,256]{2,1,0:T(8,128)(2,1)S(1)} %collective-permute-done.5.refs_3_), channel_id=1, source_target_pairs={{8,0},{16,8},{24,16},{28,24},{20,28},{12,20},{4,12},{0,4},{9,1},{1... | collective-permute-start | bytes 786440 | tf_op jit(solution)/shard_map/ppermute | solution.py:143
  20.4 0.1 collective-permute-start.1
  20.5 1.9 %collective-permute-start.10 = (f32[72,256]{1,0:T(8,128)S(1)}, f32[72,256]{1,0:T(8,128)S(1)}, u32[]{:S(2)}, u32[]{:S(2)}) collective-permute-start(f32[72,256]{1,0:T(8,128)S(1)} %add.32), channel_id=1, source_target_pairs={{0,8},{4,12},{8,0},{12,4},{16,24},{20,28},{24,16},{28,20},{1,9},{5... | collective-permute-start | bytes 221192 | tf_op jit(solution)/shard_map/ppermute | solution.py:130
  22.4 0.0 collective-permute-done.9.refs_1_
  22.4 0.1 collective-permute-start.13
  22.5 1.0 %shard_map.96.refs_5_ = f32[256,256]{1,0:T(8,128)S(1)} custom-call(s32[128]{0:T(128)S(1)} %copy-done.5, s32[1]{0:T(128)} %copy.10.current, bf16[8,64,256]{2,1,0:T(8,128)(2,1)S(1)} %collective-permute-done.refs_0_, bf16[8,64,256]{2,1,0:T(8,128)(2,1)S(1)} %collective-permute-done.9.refs_1_, bf16[8,64,256]{2,1,0:T(8,128)(2,1)S(1)} %collective-permute-done.4.refs_2_, ...), custom_call_target="tpu_custom_call" | custom-call | flops 268435456 | bytes 2097152 | tf_op jit(solution)/shard_map/pallas_call | solution.py:65
  23.5 7.4 %collective-permute-done.10 = f32[72,256]{1,0:T(8,128)S(1)} collective-permute-done((f32[72,256]{1,0:T(8,128)S(1)}, f32[72,256]{1,0:T(8,128)S(1)}, u32[]{:S(2)}, u32[]{:S(2)}) %collective-permute-start.10) | collective-permute-done | bytes 73760 | tf_op jit(solution)/shard_map/ppermute | solution.py:130
  30.9 0.0 collective-permute-done.8.refs_3_
  30.9 2.5 %collective-permute-start.11 = (bf16[8,64,256]{2,1,0:T(8,128)(2,1)S(1)}, bf16[8,64,256]{2,1,0:T(8,128)(2,1)S(1)}, u32[]{:S(2)}, u32[]{:S(2)}) collective-permute-start(bf16[8,64,256]{2,1,0:T(8,128)(2,1)S(1)} %collective-permute-done.7.refs_2_), channel_id=1, source_target_pairs={{0,8},{8,16},{16,24},{24,28},{28,20},{20,12},{12,4},{4,0},{1,9},{9... | collective-permute-start | bytes 786440 | tf_op jit(solution)/shard_map/ppermute | solution.py:143
  33.5 2.0 %collective-permute-start.2 = (bf16[8,64,256]{2,1,0:T(8,128)(2,1)S(1)}, bf16[8,64,256]{2,1,0:T(8,128)(2,1)S(1)}, u32[]{:S(2)}, u32[]{:S(2)}) collective-permute-start(bf16[8,64,256]{2,1,0:T(8,128)(2,1)S(1)} %collective-permute-done.1.refs_0_), channel_id=1, source_target_pairs={{0,8},{8,16},{16,24},{24,28},{28,20},{20,12},{12,4},{4,0},{1,9},{9... | collective-permute-start | bytes 786440 | tf_op jit(solution)/shard_map/ppermute | solution.py:143
  35.5 2.8 %collective-permute-start.14 = (f32[72,256]{1,0:T(8,128)S(1)}, f32[72,256]{1,0:T(8,128)S(1)}, u32[]{:S(2)}, u32[]{:S(2)}) collective-permute-start(f32[72,256]{1,0:T(8,128)S(1)} %add.33), channel_id=1, source_target_pairs={{0,16},{4,20},{8,24},{12,28},{16,0},{20,4},{24,8},{28,12},{1,17},{... | collective-permute-start | bytes 221192 | tf_op jit(solution)/shard_map/ppermute | solution.py:130
  38.3 0.0 collective-permute-done.13.refs_1_
  38.3 0.8 %collective-permute-start.16 = (bf16[8,64,256]{2,1,0:T(8,128)(2,1)S(1)}, bf16[8,64,256]{2,1,0:T(8,128)(2,1)S(1)}, u32[]{:S(2)}, u32[]{:S(2)}) collective-permute-start(bf16[8,64,256]{2,1,0:T(8,128)(2,1)S(1)} %collective-permute-done.13.refs_1_), channel_id=1, source_target_pairs={{8,0},{16,8},{24,16},{28,24},{20,28},{12,20},{4,12},{0,4},{9,1},{1... | collective-permute-start | bytes 786440 | tf_op jit(solution)/shard_map/ppermute | solution.py:143
  39.1 1.0 %shard_map.97.refs_5_ = f32[256,256]{1,0:T(8,128)S(1)} custom-call(s32[128]{0:T(128)S(1)} %copy-done.5, s32[1]{0:T(128)} %copy.10.current, bf16[8,64,256]{2,1,0:T(8,128)(2,1)S(1)} %collective-permute-done.1.refs_0_, bf16[8,64,256]{2,1,0:T(8,128)(2,1)S(1)} %collective-permute-done.13.refs_1_, bf16[8,64,256]{2,1,0:T(8,128)(2,1)S(1)} %collective-permute-done.7.refs_2_, ...), custom_call_target="tpu_custom_call" | custom-call | flops 268435456 | bytes 2097152 | tf_op jit(solution)/shard_map/pallas_call | solution.py:65
  40.1 0.0 copy-start.4
  40.2 6.4 %collective-permute-done.14 = f32[72,256]{1,0:T(8,128)S(1)} collective-permute-done((f32[72,256]{1,0:T(8,128)S(1)}, f32[72,256]{1,0:T(8,128)S(1)}, u32[]{:S(2)}, u32[]{:S(2)}) %collective-permute-start.14) | collective-permute-done | bytes 73760 | tf_op jit(solution)/shard_map/ppermute | solution.py:130
  46.6 0.0 collective-permute-done.11.refs_2_
  46.6 0.0 collective-permute-done.12.refs_3_
  46.6 4.1 %collective-permute-start.15 = (bf16[8,64,256]{2,1,0:T(8,128)(2,1)S(1)}, bf16[8,64,256]{2,1,0:T(8,128)(2,1)S(1)}, u32[]{:S(2)}, u32[]{:S(2)}) collective-permute-start(bf16[8,64,256]{2,1,0:T(8,128)(2,1)S(1)} %collective-permute-done.12.refs_3_), channel_id=1, source_target_pairs={{8,0},{16,8},{24,16},{28,24},{20,28},{12,20},{4,12},{0,4},{9,1},{1... | collective-permute-start | bytes 786440 | tf_op jit(solution)/shard_map/ppermute | solution.py:152
  50.7 1.6 %collective-permute-start.18 = (f32[72,256]{1,0:T(8,128)S(1)}, f32[72,256]{1,0:T(8,128)S(1)}, u32[]{:S(2)}, u32[]{:S(2)}) collective-permute-start(f32[72,256]{1,0:T(8,128)S(1)} %add.34.spread_0.s0), channel_id=1, source_target_pairs={{0,2},{1,3},{2,0},{3,1},{4,6},{5,7},{6,4},{7,5},{8,10},{9,11},{10,... | collective-permute-start | bytes 221192 | tf_op jit(solution)/shard_map/ppermute | solution.py:130
  52.3 1.2 %collective-permute-start.19 = (f32[72,256]{1,0:T(8,128)S(1)}, f32[72,256]{1,0:T(8,128)S(1)}, u32[]{:S(2)}, u32[]{:S(2)}) collective-permute-start(f32[72,256]{1,0:T(8,128)S(1)} %collective-permute-done.17.spread_1.s1), channel_id=1, source_target_pairs={{0,2},{1,3},{2,0},{3,1},{4,6},{5,7},{6,4},{7,5},{8,10},{9,11},{10,... | collective-permute-start | bytes 221192 | tf_op jit(solution)/shard_map/ppermute | solution.py:130
  53.5 1.0 %shard_map.98.before = f32[256,256]{1,0:T(8,128)S(1)} custom-call(s32[128]{0:T(128)S(1)} %copy-done.5, s32[1]{0:T(128)} %copy.10.current, bf16[8,64,256]{2,1,0:T(8,128)(2,1)S(1)} %collective-permute-done.2.refs_0_, bf16[8,64,256]{2,1,0:T(8,128)(2,1)S(1)} %collective-permute-done.16.refs_1_, bf16[8,64,256]{2,1,0:T(8,128)(2,1)S(1)} %collective-permute-done.11.refs_2_, ...), custom_call_target="tpu_custom_call" | custom-call | flops 268435456 | bytes 2097152 | tf_op jit(solution)/shard_map/pallas_call | solution.py:65
  54.5 0.0 copy-start.6
  54.6 1.2 %collective-permute-done.18.spread_2.s2 = f32[72,256]{1,0:T(8,128)S(1)} collective-permute-done((f32[72,256]{1,0:T(8,128)S(1)}, f32[72,256]{1,0:T(8,128)S(1)}, u32[]{:S(2)}, u32[]{:S(2)}) %collective-permute-start.18) | collective-permute-done | bytes 73760 | tf_op jit(solution)/shard_map/ppermute | solution.py:130
  55.8 1.2 %collective-permute-done.19.spread_3.s3 = f32[72,256]{1,0:T(8,128)S(1)} collective-permute-done((f32[72,256]{1,0:T(8,128)S(1)}, f32[72,256]{1,0:T(8,128)S(1)}, u32[]{:S(2)}, u32[]{:S(2)}) %collective-permute-start.19) | collective-permute-done | bytes 73760 | tf_op jit(solution)/shard_map/ppermute | solution.py:130
  57.0 0.6 shard_map.99.tile
  57.6 0.9 %shard_map.100 = (f32[128,256]{1,0:T(8,128)S(1)}, f32[128,256]{1,0:T(8,128)S(1)}) custom-call(s32[128]{0:T(128)S(1)} %copy-done.5, s32[1]{0:T(128)} %copy.10.current, bf16[8,64,256]{2,1,0:T(8,128)(2,1)S(1)} %collective-permute-done.3.panel_a, bf16[8,64,256]{2,1,0:T(8,128)(2,1)S(1)} %collective-permute-done.15.panel_b, bf16[128,64,256]{2,1,0:T(8,128)(2,1)S(1)} %copy-done.2, ...), custom_call_target="tpu_custom_call" | custom-call | flops 134217728 | bytes 1048576 | tf_op jit(solution)/shard_map/pallas_call | solution.py:65
  58.6 0.1 collective-permute-start.20
  58.6 1.5 %collective-permute-done.20.mate = f32[256,256]{1,0:T(8,128)S(1)} collective-permute-done((f32[256,256]{1,0:T(8,128)S(1)}, f32[256,256]{1,0:T(8,128)S(1)}, u32[]{:S(2)}, u32[]{:S(2)}) %collective-permute-start.20) | collective-permute-done | bytes 262176 | tf_op jit(solution)/shard_map/ppermute | solution.py:130
  60.2 1.6 %collective-permute-start.21 = (f32[128,256]{1,0:T(8,128)S(1)}, f32[128,256]{1,0:T(8,128)S(1)}, u32[]{:S(2)}, u32[]{:S(2)}) collective-permute-start(f32[128,256]{1,0:T(8,128)S(1)} %slice_add_fusion), channel_id=1, source_target_pairs={{0,2},{1,3},{2,0},{3,1},{4,6},{5,7},{6,4},{7,5},{8,10},{9,11},{10,... | collective-permute-start | bytes 393224 | tf_op jit(solution)/shard_map/ppermute | solution.py:130
  61.8 4.0 %collective-permute-done.21.far = f32[128,256]{1,0:T(8,128)S(1)} collective-permute-done((f32[128,256]{1,0:T(8,128)S(1)}, f32[128,256]{1,0:T(8,128)S(1)}, u32[]{:S(2)}, u32[]{:S(2)}) %collective-permute-start.21) | collective-permute-done | bytes 131104 | tf_op jit(solution)/shard_map/ppermute | solution.py:130
  65.8 1.3 %collective-permute-done.22.mate_far = f32[128,256]{1,0:T(8,128)S(1)} collective-permute-done((f32[128,256]{1,0:T(8,128)S(1)}, f32[128,256]{1,0:T(8,128)S(1)}, u32[]{:S(2)}, u32[]{:S(2)}) %collective-permute-start.22) | collective-permute-done | bytes 131104 | tf_op jit(solution)/shard_map/ppermute | solution.py:130
  67.1 1.3 %shard_map.101 = (f32[64,256]{1,0:T(8,128)}, f32[1,256]{1,0:T(1,128)}) custom-call(f32[128,256]{1,0:T(8,128)S(1)} %get-tuple-element.37.mine, f32[128,256]{1,0:T(8,128)S(1)} %get-tuple-element.38.other, f32[256,256]{1,0:T(8,128)S(1)} %collective-permute-done.20.mate, f32[128,256]{1,0:T(8,128)S(1)} %collective-permute-done.21.far, ...), custom_call_target="tpu_custom_call" | custom-call | flops 200000000 | bytes 1000000 | tf_op jit(solution)/shard_map/pallas_call | solution.py:177
  (28 shorter events, 0.1 us)
Async XLA Ops:
  0.6 7.0 %copy-start = (f32[16,64,256]{2,1,0:T(8,128)S(1)}, f32[16,64,256]{2,1,0:T(8,128)}, u32[]{:S(2)}) copy-start(f32[16,64,256]{2,1,0:T(8,128)} %param.14) | copy-start | bytes 3145732
  1.8 16.5 %collective-permute-start.4 = (bf16[8,64,256]{2,1,0:T(8,128)(2,1)S(1)}, bf16[8,64,256]{2,1,0:T(8,128)(2,1)S(1)}, u32[]{:S(2)}, u32[]{:S(2)}) collective-permute-start(bf16[8,64,256]{2,1,0:T(8,128)(2,1)S(1)} %get-tuple-element.42), channel_id=1, source_target_pairs={{0,8},{8,16},{16,24},{24,28},{28,20},{20,12},{12,4},{4,0},{1,9},{9... | collective-permute-start | bytes 786440 | tf_op jit(solution)/shard_map/ppermute | solution.py:143
  4.9 13.4 %collective-permute-start.5 = (bf16[8,64,256]{2,1,0:T(8,128)(2,1)S(1)}, bf16[8,64,256]{2,1,0:T(8,128)(2,1)S(1)}, u32[]{:S(2)}, u32[]{:S(2)}) collective-permute-start(bf16[8,64,256]{2,1,0:T(8,128)(2,1)S(1)} %get-tuple-element.42), channel_id=1, source_target_pairs={{8,0},{16,8},{24,16},{28,24},{20,28},{12,20},{4,12},{0,4},{9,1},{1... | collective-permute-start | bytes 786440 | tf_op jit(solution)/shard_map/ppermute | solution.py:143
  4.9 15.5 %collective-permute-start = (bf16[8,64,256]{2,1,0:T(8,128)(2,1)S(1)}, bf16[8,64,256]{2,1,0:T(8,128)(2,1)S(1)}, u32[]{:S(2)}, u32[]{:S(2)}) collective-permute-start(bf16[8,64,256]{2,1,0:T(8,128)(2,1)S(1)} %get-tuple-element.43), channel_id=1, source_target_pairs={{0,8},{8,16},{16,24},{24,28},{28,20},{20,12},{12,4},{4,0},{1,9},{9... | collective-permute-start | bytes 786440 | tf_op jit(solution)/shard_map/ppermute | solution.py:143
  8.4 9.9 %collective-permute-start.6 = (f32[72,256]{1,0:T(8,128)S(1)}, f32[72,256]{1,0:T(8,128)S(1)}, u32[]{:S(2)}, u32[]{:S(2)}) collective-permute-start(f32[72,256]{1,0:T(8,128)S(1)} %maximum_select_fusion), channel_id=1, source_target_pairs={{0,4},{4,0},{8,12},{12,8},{16,20},{20,16},{24,28},{28,24},{1,5},{5... | collective-permute-start | bytes 221192 | tf_op jit(solution)/shard_map/ppermute | solution.py:130
  8.5 13.9 %collective-permute-start.9 = (bf16[8,64,256]{2,1,0:T(8,128)(2,1)S(1)}, bf16[8,64,256]{2,1,0:T(8,128)(2,1)S(1)}, u32[]{:S(2)}, u32[]{:S(2)}) collective-permute-start(bf16[8,64,256]{2,1,0:T(8,128)(2,1)S(1)} %get-tuple-element.43), channel_id=1, source_target_pairs={{8,0},{16,8},{24,16},{28,24},{20,28},{12,20},{4,12},{0,4},{9,1},{1... | collective-permute-start | bytes 786440 | tf_op jit(solution)/shard_map/ppermute | solution.py:143
  10.5 2.2 %copy-start.1 = (bf16[128,64,256]{2,1,0:T(8,128)(2,1)S(1)}, bf16[128,64,256]{2,1,0:T(8,128)(2,1)}, u32[]{:S(2)}) copy-start(bf16[128,64,256]{2,1,0:T(8,128)(2,1)} %earlier.3) | copy-start | bytes 12582916
  12.7 1.0 %copy-start.3 = (bf16[16,256,64]{1,2,0:T(8,128)(2,1)S(1)}, bf16[16,256,64]{1,2,0:T(8,128)(2,1)}, u32[]{:S(2)}) copy-start(bf16[16,256,64]{1,2,0:T(8,128)(2,1)} %param.10) | copy-start | bytes 1572868
  13.7 0.7 copy-start.5
  14.4 8.1 %copy-start.2 = (bf16[128,64,256]{2,1,0:T(8,128)(2,1)S(1)}, bf16[128,64,256]{2,1,0:T(8,128)(2,1)}, u32[]{:S(2)}) copy-start(bf16[128,64,256]{2,1,0:T(8,128)(2,1)} %earlier.3) | copy-start | bytes 12582916
  18.3 12.6 %collective-permute-start.7 = (bf16[8,64,256]{2,1,0:T(8,128)(2,1)S(1)}, bf16[8,64,256]{2,1,0:T(8,128)(2,1)S(1)}, u32[]{:S(2)}, u32[]{:S(2)}) collective-permute-start(bf16[8,64,256]{2,1,0:T(8,128)(2,1)S(1)} %collective-permute-done.4.refs_2_), channel_id=1, source_target_pairs={{0,8},{8,16},{16,24},{24,28},{28,20},{20,12},{12,4},{4,0},{1,9},{9... | collective-permute-start | bytes 786440 | tf_op jit(solution)/shard_map/ppermute | solution.py:143
  18.4 12.5 %collective-permute-start.8 = (bf16[8,64,256]{2,1,0:T(8,128)(2,1)S(1)}, bf16[8,64,256]{2,1,0:T(8,128)(2,1)S(1)}, u32[]{:S(2)}, u32[]{:S(2)}) collective-permute-start(bf16[8,64,256]{2,1,0:T(8,128)(2,1)S(1)} %collective-permute-done.5.refs_3_), channel_id=1, source_target_pairs={{8,0},{16,8},{24,16},{28,24},{20,28},{12,20},{4,12},{0,4},{9,1},{1... | collective-permute-start | bytes 786440 | tf_op jit(solution)/shard_map/ppermute | solution.py:143
  20.4 13.0 %collective-permute-start.1 = (bf16[8,64,256]{2,1,0:T(8,128)(2,1)S(1)}, bf16[8,64,256]{2,1,0:T(8,128)(2,1)S(1)}, u32[]{:S(2)}, u32[]{:S(2)}) collective-permute-start(bf16[8,64,256]{2,1,0:T(8,128)(2,1)S(1)} %collective-permute-done.refs_0_), channel_id=1, source_target_pairs={{0,8},{8,16},{16,24},{24,28},{28,20},{20,12},{12,4},{4,0},{1,9},{9... | collective-permute-start | bytes 786440 | tf_op jit(solution)/shard_map/ppermute | solution.py:143
  20.5 10.4 %collective-permute-start.10 = (f32[72,256]{1,0:T(8,128)S(1)}, f32[72,256]{1,0:T(8,128)S(1)}, u32[]{:S(2)}, u32[]{:S(2)}) collective-permute-start(f32[72,256]{1,0:T(8,128)S(1)} %add.32), channel_id=1, source_target_pairs={{0,8},{4,12},{8,0},{12,4},{16,24},{20,28},{24,16},{28,20},{1,9},{5... | collective-permute-start | bytes 221192 | tf_op jit(solution)/shard_map/ppermute | solution.py:130
  22.4 15.9 %collective-permute-start.13 = (bf16[8,64,256]{2,1,0:T(8,128)(2,1)S(1)}, bf16[8,64,256]{2,1,0:T(8,128)(2,1)S(1)}, u32[]{:S(2)}, u32[]{:S(2)}) collective-permute-start(bf16[8,64,256]{2,1,0:T(8,128)(2,1)S(1)} %collective-permute-done.9.refs_1_), channel_id=1, source_target_pairs={{8,0},{16,8},{24,16},{28,24},{20,28},{12,20},{4,12},{0,4},{9,1},{1... | collective-permute-start | bytes 786440 | tf_op jit(solution)/shard_map/ppermute | solution.py:143
  30.9 15.7 %collective-permute-start.11 = (bf16[8,64,256]{2,1,0:T(8,128)(2,1)S(1)}, bf16[8,64,256]{2,1,0:T(8,128)(2,1)S(1)}, u32[]{:S(2)}, u32[]{:S(2)}) collective-permute-start(bf16[8,64,256]{2,1,0:T(8,128)(2,1)S(1)} %collective-permute-done.7.refs_2_), channel_id=1, source_target_pairs={{0,8},{8,16},{16,24},{24,28},{28,20},{20,12},{12,4},{4,0},{1,9},{9... | collective-permute-start | bytes 786440 | tf_op jit(solution)/shard_map/ppermute | solution.py:143
  33.4 13.2 %collective-permute-start.12 = (bf16[8,64,256]{2,1,0:T(8,128)(2,1)S(1)}, bf16[8,64,256]{2,1,0:T(8,128)(2,1)S(1)}, u32[]{:S(2)}, u32[]{:S(2)}) collective-permute-start(bf16[8,64,256]{2,1,0:T(8,128)(2,1)S(1)} %collective-permute-done.8.refs_3_), channel_id=1, source_target_pairs={{8,0},{16,8},{24,16},{28,24},{20,28},{12,20},{4,12},{0,4},{9,1},{1... | collective-permute-start | bytes 786440 | tf_op jit(solution)/shard_map/ppermute | solution.py:143
  33.5 17.3 %collective-permute-start.2 = (bf16[8,64,256]{2,1,0:T(8,128)(2,1)S(1)}, bf16[8,64,256]{2,1,0:T(8,128)(2,1)S(1)}, u32[]{:S(2)}, u32[]{:S(2)}) collective-permute-start(bf16[8,64,256]{2,1,0:T(8,128)(2,1)S(1)} %collective-permute-done.1.refs_0_), channel_id=1, source_target_pairs={{0,8},{8,16},{16,24},{24,28},{28,20},{20,12},{12,4},{4,0},{1,9},{9... | collective-permute-start | bytes 786440 | tf_op jit(solution)/shard_map/ppermute | solution.py:143
  35.5 11.1 %collective-permute-start.14 = (f32[72,256]{1,0:T(8,128)S(1)}, f32[72,256]{1,0:T(8,128)S(1)}, u32[]{:S(2)}, u32[]{:S(2)}) collective-permute-start(f32[72,256]{1,0:T(8,128)S(1)} %add.33), channel_id=1, source_target_pairs={{0,16},{4,20},{8,24},{12,28},{16,0},{20,4},{24,8},{28,12},{1,17},{... | collective-permute-start | bytes 221192 | tf_op jit(solution)/shard_map/ppermute | solution.py:130
  38.3 15.2 %collective-permute-start.16 = (bf16[8,64,256]{2,1,0:T(8,128)(2,1)S(1)}, bf16[8,64,256]{2,1,0:T(8,128)(2,1)S(1)}, u32[]{:S(2)}, u32[]{:S(2)}) collective-permute-start(bf16[8,64,256]{2,1,0:T(8,128)(2,1)S(1)} %collective-permute-done.13.refs_1_), channel_id=1, source_target_pairs={{8,0},{16,8},{24,16},{28,24},{20,28},{12,20},{4,12},{0,4},{9,1},{1... | collective-permute-start | bytes 786440 | tf_op jit(solution)/shard_map/ppermute | solution.py:143
  40.1 16.8 %copy-start.4 = (f32[256,32]{0,1:T(8,128)S(1)}, f32[256,32]{0,1:T(8,128)}, u32[]{:S(2)}) copy-start(f32[256,32]{0,1:T(8,128)} %param.13) | copy-start | bytes 98308
  46.6 11.0 %collective-permute-start.15 = (bf16[8,64,256]{2,1,0:T(8,128)(2,1)S(1)}, bf16[8,64,256]{2,1,0:T(8,128)(2,1)S(1)}, u32[]{:S(2)}, u32[]{:S(2)}) collective-permute-start(bf16[8,64,256]{2,1,0:T(8,128)(2,1)S(1)} %collective-permute-done.12.refs_3_), channel_id=1, source_target_pairs={{8,0},{16,8},{24,16},{28,24},{20,28},{12,20},{4,12},{0,4},{9,1},{1... | collective-permute-start | bytes 786440 | tf_op jit(solution)/shard_map/ppermute | solution.py:152
  50.7 6.9 %collective-permute-start.3 = (bf16[8,64,256]{2,1,0:T(8,128)(2,1)S(1)}, bf16[8,64,256]{2,1,0:T(8,128)(2,1)S(1)}, u32[]{:S(2)}, u32[]{:S(2)}) collective-permute-start(bf16[8,64,256]{2,1,0:T(8,128)(2,1)S(1)} %collective-permute-done.2.refs_0_), channel_id=1, source_target_pairs={{0,8},{8,16},{16,24},{24,28},{28,20},{20,12},{12,4},{4,0},{1,9},{9... | collective-permute-start | bytes 786440 | tf_op jit(solution)/shard_map/ppermute | solution.py:150
  50.7 1.6 %collective-permute-start.17 = (f32[72,256]{1,0:T(8,128)S(1)}, f32[72,256]{1,0:T(8,128)S(1)}, u32[]{:S(2)}, u32[]{:S(2)}) collective-permute-start(f32[72,256]{1,0:T(8,128)S(1)} %add.34.spread_0.s0), channel_id=1, source_target_pairs={{0,1},{1,0},{2,3},{3,2},{4,5},{5,4},{6,7},{7,6},{8,9},{9,8},{10,11... | collective-permute-start | bytes 221192 | tf_op jit(solution)/shard_map/ppermute | solution.py:130
  50.7 5.1 %collective-permute-start.18 = (f32[72,256]{1,0:T(8,128)S(1)}, f32[72,256]{1,0:T(8,128)S(1)}, u32[]{:S(2)}, u32[]{:S(2)}) collective-permute-start(f32[72,256]{1,0:T(8,128)S(1)} %add.34.spread_0.s0), channel_id=1, source_target_pairs={{0,2},{1,3},{2,0},{3,1},{4,6},{5,7},{6,4},{7,5},{8,10},{9,11},{10,... | collective-permute-start | bytes 221192 | tf_op jit(solution)/shard_map/ppermute | solution.py:130
  52.3 4.7 %collective-permute-start.19 = (f32[72,256]{1,0:T(8,128)S(1)}, f32[72,256]{1,0:T(8,128)S(1)}, u32[]{:S(2)}, u32[]{:S(2)}) collective-permute-start(f32[72,256]{1,0:T(8,128)S(1)} %collective-permute-done.17.spread_1.s1), channel_id=1, source_target_pairs={{0,2},{1,3},{2,0},{3,1},{4,6},{5,7},{6,4},{7,5},{8,10},{9,11},{10,... | collective-permute-start | bytes 221192 | tf_op jit(solution)/shard_map/ppermute | solution.py:130
  54.5 12.6 %copy-start.6 = (f32[256]{0:T(256)S(1)}, f32[256]{0:T(256)}, u32[]{:S(2)}) copy-start(f32[256]{0:T(256)} %param.15) | copy-start | bytes 3076
  58.6 1.6 %collective-permute-start.20 = (f32[256,256]{1,0:T(8,128)S(1)}, f32[256,256]{1,0:T(8,128)S(1)}, u32[]{:S(2)}, u32[]{:S(2)}) collective-permute-start(f32[256,256]{1,0:T(8,128)S(1)} %pad_maximum_fusion), channel_id=1, source_target_pairs={{0,1},{1,0},{2,3},{3,2},{4,5},{5,4},{6,7},{7,6},{8,9},{9,8},{10,11... | collective-permute-start | bytes 786440 | tf_op jit(solution)/shard_map/ppermute | solution.py:130
  60.2 5.6 %collective-permute-start.21 = (f32[128,256]{1,0:T(8,128)S(1)}, f32[128,256]{1,0:T(8,128)S(1)}, u32[]{:S(2)}, u32[]{:S(2)}) collective-permute-start(f32[128,256]{1,0:T(8,128)S(1)} %slice_add_fusion), channel_id=1, source_target_pairs={{0,2},{1,3},{2,0},{3,1},{4,6},{5,7},{6,4},{7,5},{8,10},{9,11},{10,... | collective-permute-start | bytes 393224 | tf_op jit(solution)/shard_map/ppermute | solution.py:130
  65.8 1.3 %collective-permute-start.22 = (f32[128,256]{1,0:T(8,128)S(1)}, f32[128,256]{1,0:T(8,128)S(1)}, u32[]{:S(2)}, u32[]{:S(2)}) collective-permute-start(f32[128,256]{1,0:T(8,128)S(1)} %collective-permute-done.21.far), channel_id=1, source_target_pairs={{0,1},{1,0},{2,3},{3,2},{4,5},{5,4},{6,7},{7,6},{8,9},{9,8},{10,11... | collective-permute-start | bytes 393224 | tf_op jit(solution)/shard_map/ppermute | solution.py:130

commit v3 on v2

--- a/solution.py
+++ b/solution.py
@@ -77,11 +77,20 @@
     )(slot_block, current, *panels, earlier, *before)
 
 
-def tile_kernel(spread_0, spread_1, spread_2, spread_3, cands, tile, points):
+def tile_kernel(held, given, cands, tile, high, low, points):
     obs = lax.axis_index("obs")
+    side = lax.rem(lax.axis_index("cand"), 2)
     share = points.shape[0] // 4
-    for m, spread in enumerate((spread_0, spread_1, spread_2, spread_3)):
-        points[pl.ds(pl.multiple_of((obs ^ m) * share, share), share), :] = spread[-share:, :]
+    size = held.shape[0] // 4
+    rows = size - share
+    for m in range(4):
+        points[pl.ds(pl.multiple_of((obs ^ m) * share, share), share), :] = held[m * size + rows : (m + 1) * size, :]
+        for piece, place in ((held, side), (given, 1 - side)):
+            inverse = piece[m * size : m * size + rows, :]
+            top = inverse.astype(jnp.bfloat16)
+            here = pl.ds(pl.multiple_of((2 * m + place) * rows, rows), rows)
+            high[here, :] = top
+            low[here, :] = (inverse - top.astype(jnp.float32)).astype(jnp.bfloat16)
     p = points[...]
     p = p / jnp.sum(p, axis=0, keepdims=True)
     c = cands[...]
@@ -92,7 +101,7 @@
     tile[...] = jnp.exp(-10.0 * squared)
 
 
-def solve_kernel(mine, other, mate, far, mate_far, tile, s0, s1, s2, s3, prior, solved, remaining, residual):
+def solve_kernel(mine, other, mate, far, mate_far, tile, high, low, prior, solved, remaining, residual):
     half, rows = mine.shape[0], solved.shape[0]
     core = lax.rem(lax.axis_index("obs"), 2)
     first = pl.ds(pl.multiple_of(core * half, half), half)
@@ -100,13 +109,13 @@
     residual[first, :] = tile[first, :] - (mine[...] + mate[half:, :] + far[...])
     residual[second, :] = tile[second, :] - (other[...] + mate[:half, :] + mate_far[...])
     value = residual[...]
-    squares = jnp.zeros(remaining.shape, jnp.float32)
-    for m, spread in enumerate((s0, s1, s2, s3)):
-        part = jnp.dot(spread[:rows, :], value, precision=HIGH, preferred_element_type=jnp.float32)
-        squares += jnp.sum(part * part, axis=0, keepdims=True)
-        if m == 0:
-            solved[...] = part
-    remaining[...] = prior[...] - squares
+    top = value.astype(jnp.bfloat16)
+    rest = (value - top.astype(jnp.float32)).astype(jnp.bfloat16)
+    part = jnp.dot(low[...], top, preferred_element_type=jnp.float32)
+    part += jnp.dot(high[...], rest, preferred_element_type=jnp.float32)
+    part += jnp.dot(high[...], top, preferred_element_type=jnp.float32)
+    solved[...] = part[:rows]
+    remaining[...] = prior[...] - jnp.sum(part * part, axis=0, keepdims=True)
 
 
 def on_ring(
@@ -130,12 +139,17 @@
         return lax.ppermute(value, axis, [(i, i ^ bits) for i in range(size)])
 
     slot_here = current % held
-    inverse_rows = lax.dynamic_index_in_dim(block_inverse, slot_here, 0, keepdims=False)
     points = lax.dynamic_index_in_dim(jnp.swapaxes(obs_weights, 1, 2), slot_here, 0, keepdims=False)
     share = points.shape[0] // 4
     points = lax.dynamic_slice_in_dim(points, obs * share, share, 0)
-    spread = jnp.concatenate([inverse_rows, points], axis=0)
-    spread = jnp.where(cand == current // held, spread, jnp.zeros_like(spread))
+    rows, width = block_inverse.shape[1:]
+
+    def rows_of(side):
+        part = lax.dynamic_slice(block_inverse, (slot_here, side * (rows // 2), 0), (1, rows // 2, width))[0]
+        part = jnp.concatenate([part, points], axis=0)
+        return jnp.where(cand == current // held, part, jnp.zeros_like(part))
+
+    spread, gift = rows_of(cand % 2), rows_of(1 - cand % 2)
 
     tie = lax.optimization_barrier
 
@@ -145,7 +159,7 @@
     early = onward((panel[:half], panel[:half]))
     late = onward((panel[half:], panel[half:]))
     (total,) = add(own_kernel, [(0, 0, held)], slot_block, block_index, [panel], earlier_rows)
-    spread = spread + flip(spread, "cand", 1, 8)
+    spread = spread + flip(gift, "cand", 1, 8)
     for k in (1, 2, 3):
         next_early = onward(early) if k < 3 else lax.ppermute(early[0], "cand", RING)
         late, total, spread = tie((late, total, spread))
@@ -157,19 +171,26 @@
         early, late = next_early, next_late
     spreads = [spread, flip(spread, "obs", 1, 4)]
     spreads += [flip(spreads[0], "obs", 2, 4), flip(spreads[1], "obs", 2, 4)]
-    tile = pl.pallas_call(
+    early, late, total, spreads = tie((early, late, total, spreads))
+    spread = jnp.concatenate(spreads, axis=0)
+    given = flip(spread, "cand", 1, 8)
+    sources = [(-4, 0, held), (4, half, held)]
+    mine, other = add(last_kernel, sources, slot_block, block_index, [early, late], earlier_rows, [total])
+
+    size = panel.shape[2]
+    tile, high, low = pl.pallas_call(
         tile_kernel,
-        out_shape=jax.ShapeDtypeStruct((panel.shape[2], cols), jnp.float32),
-        in_specs=[VMEM] * 5,
-        out_specs=VMEM,
-        scratch_shapes=[pltpu.VMEM((obs_weights.shape[2], panel.shape[2]), jnp.float32)],
+        out_shape=[
+            jax.ShapeDtypeStruct((size, cols), jnp.float32),
+            jax.ShapeDtypeStruct((4 * rows, size), jnp.bfloat16),
+            jax.ShapeDtypeStruct((4 * rows, size), jnp.bfloat16),
+        ],
+        in_specs=[VMEM] * 3,
+        out_specs=[VMEM] * 3,
+        scratch_shapes=[pltpu.VMEM((obs_weights.shape[2], size), jnp.float32)],
         compiler_params=pltpu.CompilerParams(vmem_limit_bytes=LIMIT),
         cost_estimate=pl.CostEstimate(flops=10**7, bytes_accessed=10**6, transcendentals=65536),
-    )(*spreads, cand_weights.T)
-
-    early, late, total, tile = tie((early, late, total, tile))
-    sources = [(-4, 0, held), (4, half, held)]
-    mine, other = add(last_kernel, sources, slot_block, block_index, [early, late], earlier_rows, [total])
+    )(spread, given, cand_weights.T)
 
     mate = flip(jnp.concatenate([mine, other], axis=0), "obs", 1, 4)
     far = flip(mine + mate[mine.shape[0] :], "obs", 2, 4)
@@ -177,15 +198,15 @@
     solved_rows, remaining = pl.pallas_call(
         solve_kernel,
         out_shape=[
-            jax.ShapeDtypeStruct(inverse_rows.shape[:1] + (cols,), jnp.float32),
+            jax.ShapeDtypeStruct((rows, cols), jnp.float32),
             jax.ShapeDtypeStruct((1, cols), jnp.float32),
         ],
-        in_specs=[VMEM] * 11,
+        in_specs=[VMEM] * 9,
         out_specs=[VMEM] * 2,
         scratch_shapes=[pltpu.VMEM((panel.shape[2], cols), jnp.float32)],
         compiler_params=pltpu.CompilerParams(vmem_limit_bytes=LIMIT),
         cost_estimate=pl.CostEstimate(flops=2 * 10**8, bytes_accessed=10**6, transcendentals=0),
-    )(mine, other, mate, far, mate_far, tile, *spreads, prior_var[None])
+    )(mine, other, mate, far, mate_far, tile, high, low, prior_var[None])
     return (solved_rows, remaining[0])
 
 

time: 68.8 us -> 65.5 us (0.952)
  waiting for transfers between devices: 26.2 us -> 23.7 us
    ppermute x9 -> x10, waiting for transfers between devices: 26.1 us -> 18.9 us  [flip(): return lax.ppermute(value, axis, [(i, i ^ bits) for i in range(size)])]
    ppermute x9 -> x10, starting transfers between devices: 9.23 us -> 12.9 us  [flip(): return lax.ppermute(value, axis, [(i, i ^ bits) for i in range(size)])]
    ppermute x6, starting transfers between devices: 4.9 us -> 1.36 us  [onward(): lax.ppermute(pair[1], 'cand', BACK)]
    ppermute x6, waiting for transfers between devices: 0.02 us -> 2.37 us  [onward(): lax.ppermute(pair[0], 'cand', RING)]
    ppermute x6, waiting for transfers between devices: 0.02 us -> 1.61 us  [onward(): lax.ppermute(pair[1], 'cand', BACK)]
    ppermute x1, starting transfers between devices: 4.09 us -> 2.52 us  [on_ring(): next_late = onward(late) if k < 3 else lax.ppermute(late[1], 'cand', BACK)]
    ppermute x6, starting transfers between devices: 9.78 us -> 10.9 us  [onward(): lax.ppermute(pair[0], 'cand', RING)]
    squeeze x1, local copies, waits for them, and re-layouts: 0.01 us -> 0.79 us  [rows_of(): lax.dynamic_slice(block_inverse, (slot_here, side * (rows // 2), 0), (1,...]
  transfers between devices with their start and end apart: 23 -> 24, of which waited for: 8 -> 11; matrix products, arithmetic and copies ran while one was open for 1% -> 2% of each run, Pallas kernels for 7% -> 7%
where the time goes in v3:
time: 65.5 us; the launch traced here: 65.3 us
  starting transfers between devices  27.7 us (42%)
  waiting for transfers between devices  23.7 us (36%)
  Pallas kernels  6.44 us (10%)
  local copies, waits for them, and re-layouts  5.79 us (9%)
  between operations  1.62 us (2%)
    ppermute x10, waiting for transfers between devices, flip(): return lax.ppermute(value, axis, [(i, i ^ bits) for i in range(size)])  18.9 us
    ppermute x10, starting transfers between devices, flip(): return lax.ppermute(value, axis, [(i, i ^ bits) for i in range(size)])  12.9 us
    ppermute x6, starting transfers between devices, onward(): lax.ppermute(pair[0], 'cand', RING)  10.9 us
    pallas_call x5, Pallas kernels, add(): pl.pallas_call(functools.partial(kernel, sources), out_shape=[jax.ShapeDt...  4.87 us
    unnamed x17, local copies, waits for them, and re-layouts  3.93 us
    ppermute x1, starting transfers between devices, on_ring(): next_late = onward(late) if k < 3 else lax.ppermute(late[1], 'cand', BACK)  2.52 us
    ppermute x6, waiting for transfers between devices, onward(): lax.ppermute(pair[0], 'cand', RING)  2.37 us
    ppermute x6, waiting for transfers between devices, onward(): lax.ppermute(pair[1], 'cand', BACK)  1.61 us
  transfers between devices with their start and end apart: 24, of which 11 were waited for; matrix products, arithmetic and copies ran while one was open for 2% of the time, Pallas kernels for 7%

profile of v3, /device:TPU:0, one launch (start us, length us, event | category | flops | bytes accessed | tf_op | source)
XLA Modules:
  0.0 65.3 jit_solution(9617544091239458403)
XLA Ops:
  0.6 0.0 copy-start
  1.4 0.8 %dynamic-slice_bitcast_fusion.1 = (f32[32,256]{1,0:T(8,128)S(1)}, f32[32,256]{1,0:T(8,128)S(1)}) fusion(f32[16,64,256]{2,1,0:T(8,128)} %param.14, s32[]{:T(128)S(6)} %select_n.52, s32[]{:T(128)S(6)} %select_n.54, s32[]{:T(128)S(6)} %select_n.59), kind=kLoop, calls=%fused_computation.8 | loop fusion | bytes 131084 | tf_op jit(solution)/shard_map/squeeze | solution.py:148
  2.2 3.0 %collective-permute-start.6 = (f32[40,256]{1,0:T(8,128)S(1)}, f32[40,256]{1,0:T(8,128)S(1)}, u32[]{:S(2)}, u32[]{:S(2)}) collective-permute-start(f32[40,256]{1,0:T(8,128)S(1)} %fusion.2), channel_id=1, source_target_pairs={{0,4},{4,0},{8,12},{12,8},{16,20},{20,16},{24,28},{28,24},{1,5},{5... | collective-permute-start | bytes 122888 | tf_op jit(solution)/shard_map/ppermute | solution.py:139
  5.2 1.1 %fusion.3 = (bf16[8,64,256]{2,1,0:T(8,128)(2,1)S(1)}, bf16[8,64,256]{2,1,0:T(8,128)(2,1)S(1)}) fusion(bf16[16,64,256]{2,1,0:T(8,128)(2,1)} %bitcast.17), kind=kLoop, calls=%fused_computation.14 | loop fusion | bytes 1048576 | tf_op jit(solution)/shard_map/slice | solution.py:160
  6.3 1.6 %collective-permute-start.4 = (bf16[8,64,256]{2,1,0:T(8,128)(2,1)S(1)}, bf16[8,64,256]{2,1,0:T(8,128)(2,1)S(1)}, u32[]{:S(2)}, u32[]{:S(2)}) collective-permute-start(bf16[8,64,256]{2,1,0:T(8,128)(2,1)S(1)} %get-tuple-element.56), channel_id=1, source_target_pairs={{0,8},{8,16},{16,24},{24,28},{28,20},{20,12},{12,4},{4,0},{1,9},{9... | collective-permute-start | bytes 786440 | tf_op jit(solution)/shard_map/ppermute | solution.py:157
  7.9 0.4 collective-permute-start.5
  8.4 1.6 %collective-permute-start = (bf16[8,64,256]{2,1,0:T(8,128)(2,1)S(1)}, bf16[8,64,256]{2,1,0:T(8,128)(2,1)S(1)}, u32[]{:S(2)}, u32[]{:S(2)}) collective-permute-start(bf16[8,64,256]{2,1,0:T(8,128)(2,1)S(1)} %get-tuple-element.57), channel_id=1, source_target_pairs={{0,8},{8,16},{16,24},{24,28},{28,20},{20,12},{12,4},{4,0},{1,9},{9... | collective-permute-start | bytes 786440 | tf_op jit(solution)/shard_map/ppermute | solution.py:157
  10.0 0.4 collective-permute-start.9
  10.4 2.2 %copy-done.1 = bf16[128,64,256]{2,1,0:T(8,128)(2,1)S(1)} copy-done((bf16[128,64,256]{2,1,0:T(8,128)(2,1)S(1)}, bf16[128,64,256]{2,1,0:T(8,128)(2,1)}, u32[]{:S(2)}) %copy-start.1) | copy-done | bytes 4194328
  12.6 1.0 %copy-done.3 = bf16[16,256,64]{1,2,0:T(8,128)(2,1)S(1)} copy-done((bf16[16,256,64]{1,2,0:T(8,128)(2,1)S(1)}, bf16[16,256,64]{1,2,0:T(8,128)(2,1)}, u32[]{:S(2)}) %copy-start.3) | copy-done | bytes 524312
  13.6 0.7 %copy-done.5 = s32[128]{0:T(128)S(1)} copy-done((s32[128]{0:T(128)S(1)}, s32[128]{0:T(128)}, u32[]{:S(2)}) %copy-start.5) | copy-done | bytes 536
  14.3 0.9 %shard_map.95.refs_5_ = f32[256,256]{1,0:T(8,128)S(1)} custom-call(s32[128]{0:T(128)S(1)} %copy-done.5, s32[1]{0:T(128)} %copy.13.current, bf16[16,64,256]{2,1,0:T(8,128)(2,1)S(1)} %bitcast.18, bf16[128,64,256]{2,1,0:T(8,128)(2,1)S(1)} %copy-done.1), custom_call_target="tpu_custom_call" | custom-call | flops 134217728 | bytes 1048576 | tf_op jit(solution)/shard_map/pallas_call | solution.py:65
  15.2 0.4 collective-permute-done.4.refs_2_
  15.6 1.6 %collective-permute-done.5.refs_3_ = bf16[8,64,256]{2,1,0:T(8,128)(2,1)S(1)} collective-permute-done((bf16[8,64,256]{2,1,0:T(8,128)(2,1)S(1)}, bf16[8,64,256]{2,1,0:T(8,128)(2,1)S(1)}, u32[]{:S(2)}, u32[]{:S(2)}) %collective-permute-start.5) | collective-permute-done | bytes 262176 | tf_op jit(solution)/shard_map/ppermute | solution.py:157
  17.2 1.6 %collective-permute-start.7 = (bf16[8,64,256]{2,1,0:T(8,128)(2,1)S(1)}, bf16[8,64,256]{2,1,0:T(8,128)(2,1)S(1)}, u32[]{:S(2)}, u32[]{:S(2)}) collective-permute-start(bf16[8,64,256]{2,1,0:T(8,128)(2,1)S(1)} %collective-permute-done.4.refs_2_), channel_id=1, source_target_pairs={{0,8},{8,16},{16,24},{24,28},{28,20},{20,12},{12,4},{4,0},{1,9},{9... | collective-permute-start | bytes 786440 | tf_op jit(solution)/shard_map/ppermute | solution.py:157
  18.8 0.4 collective-permute-start.8
  19.2 2.0 %collective-permute-done.refs_0_ = bf16[8,64,256]{2,1,0:T(8,128)(2,1)S(1)} collective-permute-done((bf16[8,64,256]{2,1,0:T(8,128)(2,1)S(1)}, bf16[8,64,256]{2,1,0:T(8,128)(2,1)S(1)}, u32[]{:S(2)}, u32[]{:S(2)}) %collective-permute-start) | collective-permute-done | bytes 262176 | tf_op jit(solution)/shard_map/ppermute | solution.py:157
  21.2 1.6 %collective-permute-start.1 = (bf16[8,64,256]{2,1,0:T(8,128)(2,1)S(1)}, bf16[8,64,256]{2,1,0:T(8,128)(2,1)S(1)}, u32[]{:S(2)}, u32[]{:S(2)}) collective-permute-start(bf16[8,64,256]{2,1,0:T(8,128)(2,1)S(1)} %collective-permute-done.refs_0_), channel_id=1, source_target_pairs={{0,8},{8,16},{16,24},{24,28},{28,20},{20,12},{12,4},{4,0},{1,9},{9... | collective-permute-start | bytes 786440 | tf_op jit(solution)/shard_map/ppermute | solution.py:157
  22.8 1.6 %collective-permute-start.10 = (f32[40,256]{1,0:T(8,128)S(1)}, f32[40,256]{1,0:T(8,128)S(1)}, u32[]{:S(2)}, u32[]{:S(2)}) collective-permute-start(f32[40,256]{1,0:T(8,128)S(1)} %fusion.1), channel_id=1, source_target_pairs={{0,8},{4,12},{8,0},{12,4},{16,24},{20,28},{24,16},{28,20},{1,9},{5... | collective-permute-start | bytes 122888 | tf_op jit(solution)/shard_map/ppermute | solution.py:139
  24.4 1.0 %shard_map.96.refs_5_ = f32[256,256]{1,0:T(8,128)S(1)} custom-call(s32[128]{0:T(128)S(1)} %copy-done.5, s32[1]{0:T(128)} %copy.13.current, bf16[8,64,256]{2,1,0:T(8,128)(2,1)S(1)} %collective-permute-done.refs_0_, bf16[8,64,256]{2,1,0:T(8,128)(2,1)S(1)} %collective-permute-done.9.refs_1_, bf16[8,64,256]{2,1,0:T(8,128)(2,1)S(1)} %collective-permute-done.4.refs_2_, ...), custom_call_target="tpu_custom_call" | custom-call | flops 268435456 | bytes 2097152 | tf_op jit(solution)/shard_map/pallas_call | solution.py:65
  25.4 5.5 %collective-permute-done.10 = f32[40,256]{1,0:T(8,128)S(1)} collective-permute-done((f32[40,256]{1,0:T(8,128)S(1)}, f32[40,256]{1,0:T(8,128)S(1)}, u32[]{:S(2)}, u32[]{:S(2)}) %collective-permute-start.10) | collective-permute-done | bytes 40992 | tf_op jit(solution)/shard_map/ppermute | solution.py:139
  31.0 0.0 collective-permute-done.7.refs_2_
  31.0 0.0 collective-permute-done.8.refs_3_
  31.0 2.5 %collective-permute-start.11 = (bf16[8,64,256]{2,1,0:T(8,128)(2,1)S(1)}, bf16[8,64,256]{2,1,0:T(8,128)(2,1)S(1)}, u32[]{:S(2)}, u32[]{:S(2)}) collective-permute-start(bf16[8,64,256]{2,1,0:T(8,128)(2,1)S(1)} %collective-permute-done.7.refs_2_), channel_id=1, source_target_pairs={{0,8},{8,16},{16,24},{24,28},{28,20},{20,12},{12,4},{4,0},{1,9},{9... | collective-permute-start | bytes 786440 | tf_op jit(solution)/shard_map/ppermute | solution.py:157
  33.5 2.0 %collective-permute-start.2 = (bf16[8,64,256]{2,1,0:T(8,128)(2,1)S(1)}, bf16[8,64,256]{2,1,0:T(8,128)(2,1)S(1)}, u32[]{:S(2)}, u32[]{:S(2)}) collective-permute-start(bf16[8,64,256]{2,1,0:T(8,128)(2,1)S(1)} %collective-permute-done.1.refs_0_), channel_id=1, source_target_pairs={{0,8},{8,16},{16,24},{24,28},{28,20},{20,12},{12,4},{4,0},{1,9},{9... | collective-permute-start | bytes 786440 | tf_op jit(solution)/shard_map/ppermute | solution.py:157
  35.5 2.6 %collective-permute-start.14 = (f32[40,256]{1,0:T(8,128)S(1)}, f32[40,256]{1,0:T(8,128)S(1)}, u32[]{:S(2)}, u32[]{:S(2)}) collective-permute-start(f32[40,256]{1,0:T(8,128)S(1)} %add.46), channel_id=1, source_target_pairs={{0,16},{4,20},{8,24},{12,28},{16,0},{20,4},{24,8},{28,12},{1,17},{... | collective-permute-start | bytes 122888 | tf_op jit(solution)/shard_map/ppermute | solution.py:139
  38.1 0.0 collective-permute-start.16
  38.1 1.0 %shard_map.97.refs_5_ = f32[256,256]{1,0:T(8,128)S(1)} custom-call(s32[128]{0:T(128)S(1)} %copy-done.5, s32[1]{0:T(128)} %copy.13.current, bf16[8,64,256]{2,1,0:T(8,128)(2,1)S(1)} %collective-permute-done.1.refs_0_, bf16[8,64,256]{2,1,0:T(8,128)(2,1)S(1)} %collective-permute-done.13.refs_1_, bf16[8,64,256]{2,1,0:T(8,128)(2,1)S(1)} %collective-permute-done.7.refs_2_, ...), custom_call_target="tpu_custom_call" | custom-call | flops 268435456 | bytes 2097152 | tf_op jit(solution)/shard_map/pallas_call | solution.py:65
  39.2 5.5 %collective-permute-done.14 = f32[40,256]{1,0:T(8,128)S(1)} collective-permute-done((f32[40,256]{1,0:T(8,128)S(1)}, f32[40,256]{1,0:T(8,128)S(1)}, u32[]{:S(2)}, u32[]{:S(2)}) %collective-permute-start.14) | collective-permute-done | bytes 40992 | tf_op jit(solution)/shard_map/ppermute | solution.py:139
  44.7 2.5 %collective-permute-start.15 = (bf16[8,64,256]{2,1,0:T(8,128)(2,1)S(1)}, bf16[8,64,256]{2,1,0:T(8,128)(2,1)S(1)}, u32[]{:S(2)}, u32[]{:S(2)}) collective-permute-start(bf16[8,64,256]{2,1,0:T(8,128)(2,1)S(1)} %collective-permute-done.12.refs_3_), channel_id=1, source_target_pairs={{8,0},{16,8},{24,16},{28,24},{20,28},{12,20},{4,12},{0,4},{9,1},{1... | collective-permute-start | bytes 786440 | tf_op jit(solution)/shard_map/ppermute | solution.py:166
  47.2 1.6 %collective-permute-start.18 = (f32[40,256]{1,0:T(8,128)S(1)}, f32[40,256]{1,0:T(8,128)S(1)}, u32[]{:S(2)}, u32[]{:S(2)}) collective-permute-start(f32[40,256]{1,0:T(8,128)S(1)} %add.47), channel_id=1, source_target_pairs={{0,2},{1,3},{2,0},{3,1},{4,6},{5,7},{6,4},{7,5},{8,10},{9,11},{10,... | collective-permute-start | bytes 122888 | tf_op jit(solution)/shard_map/ppermute | solution.py:139
  48.8 0.0 collective-permute-done.17
  48.8 1.1 %collective-permute-start.19 = (f32[40,256]{1,0:T(8,128)S(1)}, f32[40,256]{1,0:T(8,128)S(1)}, u32[]{:S(2)}, u32[]{:S(2)}) collective-permute-start(f32[40,256]{1,0:T(8,128)S(1)} %collective-permute-done.17), channel_id=1, source_target_pairs={{0,2},{1,3},{2,0},{3,1},{4,6},{5,7},{6,4},{7,5},{8,10},{9,11},{10,... | collective-permute-start | bytes 122888 | tf_op jit(solution)/shard_map/ppermute | solution.py:139
  49.9 1.0 %shard_map.98.before = f32[256,256]{1,0:T(8,128)S(1)} custom-call(s32[128]{0:T(128)S(1)} %copy-done.5, s32[1]{0:T(128)} %copy.13.current, bf16[8,64,256]{2,1,0:T(8,128)(2,1)S(1)} %collective-permute-done.2.refs_0_, bf16[8,64,256]{2,1,0:T(8,128)(2,1)S(1)} %collective-permute-done.16.refs_1_, bf16[8,64,256]{2,1,0:T(8,128)(2,1)S(1)} %collective-permute-done.11.refs_2_, ...), custom_call_target="tpu_custom_call" | custom-call | flops 268435456 | bytes 2097152 | tf_op jit(solution)/shard_map/pallas_call | solution.py:65
  51.0 0.0 copy-start.4
  51.0 0.0 copy-start.6
  51.0 0.3 collective-permute-done.18
  51.3 1.5 %collective-permute-done.19 = f32[40,256]{1,0:T(8,128)S(1)} collective-permute-done((f32[40,256]{1,0:T(8,128)S(1)}, f32[40,256]{1,0:T(8,128)S(1)}, u32[]{:S(2)}, u32[]{:S(2)}) %collective-permute-start.19) | collective-permute-done | bytes 40992 | tf_op jit(solution)/shard_map/ppermute | solution.py:139
  52.8 0.8 %collective-permute-done.3.panel_a = bf16[8,64,256]{2,1,0:T(8,128)(2,1)S(1)} collective-permute-done((bf16[8,64,256]{2,1,0:T(8,128)(2,1)S(1)}, bf16[8,64,256]{2,1,0:T(8,128)(2,1)S(1)}, u32[]{:S(2)}, u32[]{:S(2)}) %collective-permute-start.3) | collective-permute-done | bytes 262176 | tf_op jit(solution)/shard_map/ppermute | solution.py:164
  53.6 0.9 %shard_map.99 = (f32[128,256]{1,0:T(8,128)S(1)}, f32[128,256]{1,0:T(8,128)S(1)}) custom-call(s32[128]{0:T(128)S(1)} %copy-done.5, s32[1]{0:T(128)} %copy.13.current, bf16[8,64,256]{2,1,0:T(8,128)(2,1)S(1)} %collective-permute-done.3.panel_a, bf16[8,64,256]{2,1,0:T(8,128)(2,1)S(1)} %collective-permute-done.15.panel_b, bf16[128,64,256]{2,1,0:T(8,128)(2,1)S(1)} %copy-done.2, ...), custom_call_target="tpu_custom_call" | custom-call | flops 134217728 | bytes 1048576 | tf_op jit(solution)/shard_map/pallas_call | solution.py:65
  54.5 0.1 collective-permute-start.20
  54.6 1.5 %collective-permute-done.20.mate = f32[256,256]{1,0:T(8,128)S(1)} collective-permute-done((f32[256,256]{1,0:T(8,128)S(1)}, f32[256,256]{1,0:T(8,128)S(1)}, u32[]{:S(2)}, u32[]{:S(2)}) %collective-permute-start.20) | collective-permute-done | bytes 262176 | tf_op jit(solution)/shard_map/ppermute | solution.py:139
  56.1 1.6 %collective-permute-start.21 = (f32[128,256]{1,0:T(8,128)S(1)}, f32[128,256]{1,0:T(8,128)S(1)}, u32[]{:S(2)}, u32[]{:S(2)}) collective-permute-start(f32[128,256]{1,0:T(8,128)S(1)} %slice_add_fusion), channel_id=1, source_target_pairs={{0,2},{1,3},{2,0},{3,1},{4,6},{5,7},{6,4},{7,5},{8,10},{9,11},{10,... | collective-permute-start | bytes 393224 | tf_op jit(solution)/shard_map/ppermute | solution.py:139
  57.7 1.3 %collective-permute-start.23 = (f32[160,256]{1,0:T(8,128)S(1)}, f32[160,256]{1,0:T(8,128)S(1)}, u32[]{:S(2)}, u32[]{:S(2)}) collective-permute-start(f32[160,256]{1,0:T(8,128)S(1)} %constant_dynamic-update-slice_fusion.held), channel_id=1, source_target_pairs={{0,4},{4,0},{8,12},{12,8},{16,20},{20,16},{24,28},{28,24},{1,5},{5... | collective-permute-start | bytes 491528 | tf_op jit(solution)/shard_map/ppermute | solution.py:139
  59.0 2.7 %collective-permute-done.21.far = f32[128,256]{1,0:T(8,128)S(1)} collective-permute-done((f32[128,256]{1,0:T(8,128)S(1)}, f32[128,256]{1,0:T(8,128)S(1)}, u32[]{:S(2)}, u32[]{:S(2)}) %collective-permute-start.21) | collective-permute-done | bytes 131104 | tf_op jit(solution)/shard_map/ppermute | solution.py:139
  61.7 1.9 %collective-permute-done.23.given = f32[160,256]{1,0:T(8,128)S(1)} collective-permute-done((f32[160,256]{1,0:T(8,128)S(1)}, f32[160,256]{1,0:T(8,128)S(1)}, u32[]{:S(2)}, u32[]{:S(2)}) %collective-permute-start.23) | collective-permute-done | bytes 163872 | tf_op jit(solution)/shard_map/ppermute | solution.py:139
  63.7 0.6 shard_map.100
  64.3 0.9 %shard_map.101 = (f32[64,256]{1,0:T(8,128)}, f32[1,256]{1,0:T(1,128)}) custom-call(f32[128,256]{1,0:T(8,128)S(1)} %get-tuple-element.43.mine, f32[128,256]{1,0:T(8,128)S(1)} %get-tuple-element.44.other, f32[256,256]{1,0:T(8,128)S(1)} %collective-permute-done.20.mate, f32[128,256]{1,0:T(8,128)S(1)} %collective-permute-done.21.far, ...), custom_call_target="tpu_custom_call" | custom-call | flops 200000000 | bytes 1000000 | tf_op jit(solution)/shard_map/pallas_call | solution.py:198
  (34 shorter events, 0.2 us)
Async XLA Ops:
  0.6 1.6 %copy-start = (f32[16,256,32]{1,2,0:T(8,128)S(1)}, f32[16,256,32]{1,2,0:T(8,128)}, u32[]{:S(2)}) copy-start(f32[16,256,32]{1,2,0:T(8,128)} %param.12) | copy-start | bytes 1572868
  2.2 13.0 %collective-permute-start.6 = (f32[40,256]{1,0:T(8,128)S(1)}, f32[40,256]{1,0:T(8,128)S(1)}, u32[]{:S(2)}, u32[]{:S(2)}) collective-permute-start(f32[40,256]{1,0:T(8,128)S(1)} %fusion.2), channel_id=1, source_target_pairs={{0,4},{4,0},{8,12},{12,8},{16,20},{20,16},{24,28},{28,24},{1,5},{5... | collective-permute-start | bytes 122888 | tf_op jit(solution)/shard_map/ppermute | solution.py:139
  6.3 9.3 %collective-permute-start.4 = (bf16[8,64,256]{2,1,0:T(8,128)(2,1)S(1)}, bf16[8,64,256]{2,1,0:T(8,128)(2,1)S(1)}, u32[]{:S(2)}, u32[]{:S(2)}) collective-permute-start(bf16[8,64,256]{2,1,0:T(8,128)(2,1)S(1)} %get-tuple-element.56), channel_id=1, source_target_pairs={{0,8},{8,16},{16,24},{24,28},{28,20},{20,12},{12,4},{4,0},{1,9},{9... | collective-permute-start | bytes 786440 | tf_op jit(solution)/shard_map/ppermute | solution.py:157
  7.9 9.2 %collective-permute-start.5 = (bf16[8,64,256]{2,1,0:T(8,128)(2,1)S(1)}, bf16[8,64,256]{2,1,0:T(8,128)(2,1)S(1)}, u32[]{:S(2)}, u32[]{:S(2)}) collective-permute-start(bf16[8,64,256]{2,1,0:T(8,128)(2,1)S(1)} %get-tuple-element.56), channel_id=1, source_target_pairs={{8,0},{16,8},{24,16},{28,24},{20,28},{12,20},{4,12},{0,4},{9,1},{1... | collective-permute-start | bytes 786440 | tf_op jit(solution)/shard_map/ppermute | solution.py:157
  8.4 12.8 %collective-permute-start = (bf16[8,64,256]{2,1,0:T(8,128)(2,1)S(1)}, bf16[8,64,256]{2,1,0:T(8,128)(2,1)S(1)}, u32[]{:S(2)}, u32[]{:S(2)}) collective-permute-start(bf16[8,64,256]{2,1,0:T(8,128)(2,1)S(1)} %get-tuple-element.57), channel_id=1, source_target_pairs={{0,8},{8,16},{16,24},{24,28},{28,20},{20,12},{12,4},{4,0},{1,9},{9... | collective-permute-start | bytes 786440 | tf_op jit(solution)/shard_map/ppermute | solution.py:157
  10.0 14.4 %collective-permute-start.9 = (bf16[8,64,256]{2,1,0:T(8,128)(2,1)S(1)}, bf16[8,64,256]{2,1,0:T(8,128)(2,1)S(1)}, u32[]{:S(2)}, u32[]{:S(2)}) collective-permute-start(bf16[8,64,256]{2,1,0:T(8,128)(2,1)S(1)} %get-tuple-element.57), channel_id=1, source_target_pairs={{8,0},{16,8},{24,16},{28,24},{20,28},{12,20},{4,12},{0,4},{9,1},{1... | collective-permute-start | bytes 786440 | tf_op jit(solution)/shard_map/ppermute | solution.py:157
  10.4 2.2 %copy-start.1 = (bf16[128,64,256]{2,1,0:T(8,128)(2,1)S(1)}, bf16[128,64,256]{2,1,0:T(8,128)(2,1)}, u32[]{:S(2)}) copy-start(bf16[128,64,256]{2,1,0:T(8,128)(2,1)} %earlier.3) | copy-start | bytes 12582916
  12.6 1.0 %copy-start.3 = (bf16[16,256,64]{1,2,0:T(8,128)(2,1)S(1)}, bf16[16,256,64]{1,2,0:T(8,128)(2,1)}, u32[]{:S(2)}) copy-start(bf16[16,256,64]{1,2,0:T(8,128)(2,1)} %param.10) | copy-start | bytes 1572868
  13.6 0.7 %copy-start.5 = (s32[128]{0:T(128)S(1)}, s32[128]{0:T(128)}, u32[]{:S(2)}) copy-start(s32[128]{0:T(128)} %slot_block.9) | copy-start | bytes 1540
  14.3 10.1 %copy-start.2 = (bf16[128,64,256]{2,1,0:T(8,128)(2,1)S(1)}, bf16[128,64,256]{2,1,0:T(8,128)(2,1)}, u32[]{:S(2)}) copy-start(bf16[128,64,256]{2,1,0:T(8,128)(2,1)} %earlier.3) | copy-start | bytes 12582916
  17.2 13.8 %collective-permute-start.7 = (bf16[8,64,256]{2,1,0:T(8,128)(2,1)S(1)}, bf16[8,64,256]{2,1,0:T(8,128)(2,1)S(1)}, u32[]{:S(2)}, u32[]{:S(2)}) collective-permute-start(bf16[8,64,256]{2,1,0:T(8,128)(2,1)S(1)} %collective-permute-done.4.refs_2_), channel_id=1, source_target_pairs={{0,8},{8,16},{16,24},{24,28},{28,20},{20,12},{12,4},{4,0},{1,9},{9... | collective-permute-start | bytes 786440 | tf_op jit(solution)/shard_map/ppermute | solution.py:157
  18.8 12.2 %collective-permute-start.8 = (bf16[8,64,256]{2,1,0:T(8,128)(2,1)S(1)}, bf16[8,64,256]{2,1,0:T(8,128)(2,1)S(1)}, u32[]{:S(2)}, u32[]{:S(2)}) collective-permute-start(bf16[8,64,256]{2,1,0:T(8,128)(2,1)S(1)} %collective-permute-done.5.refs_3_), channel_id=1, source_target_pairs={{8,0},{16,8},{24,16},{28,24},{20,28},{12,20},{4,12},{0,4},{9,1},{1... | collective-permute-start | bytes 786440 | tf_op jit(solution)/shard_map/ppermute | solution.py:157
  21.2 12.3 %collective-permute-start.1 = (bf16[8,64,256]{2,1,0:T(8,128)(2,1)S(1)}, bf16[8,64,256]{2,1,0:T(8,128)(2,1)S(1)}, u32[]{:S(2)}, u32[]{:S(2)}) collective-permute-start(bf16[8,64,256]{2,1,0:T(8,128)(2,1)S(1)} %collective-permute-done.refs_0_), channel_id=1, source_target_pairs={{0,8},{8,16},{16,24},{24,28},{28,20},{20,12},{12,4},{4,0},{1,9},{9... | collective-permute-start | bytes 786440 | tf_op jit(solution)/shard_map/ppermute | solution.py:157
  22.8 8.2 %collective-permute-start.10 = (f32[40,256]{1,0:T(8,128)S(1)}, f32[40,256]{1,0:T(8,128)S(1)}, u32[]{:S(2)}, u32[]{:S(2)}) collective-permute-start(f32[40,256]{1,0:T(8,128)S(1)} %fusion.1), channel_id=1, source_target_pairs={{0,8},{4,12},{8,0},{12,4},{16,24},{20,28},{24,16},{28,20},{1,9},{5... | collective-permute-start | bytes 122888 | tf_op jit(solution)/shard_map/ppermute | solution.py:139
  24.4 13.8 %collective-permute-start.13 = (bf16[8,64,256]{2,1,0:T(8,128)(2,1)S(1)}, bf16[8,64,256]{2,1,0:T(8,128)(2,1)S(1)}, u32[]{:S(2)}, u32[]{:S(2)}) collective-permute-start(bf16[8,64,256]{2,1,0:T(8,128)(2,1)S(1)} %collective-permute-done.9.refs_1_), channel_id=1, source_target_pairs={{8,0},{16,8},{24,16},{28,24},{20,28},{12,20},{4,12},{0,4},{9,1},{1... | collective-permute-start | bytes 786440 | tf_op jit(solution)/shard_map/ppermute | solution.py:157
  31.0 13.7 %collective-permute-start.11 = (bf16[8,64,256]{2,1,0:T(8,128)(2,1)S(1)}, bf16[8,64,256]{2,1,0:T(8,128)(2,1)S(1)}, u32[]{:S(2)}, u32[]{:S(2)}) collective-permute-start(bf16[8,64,256]{2,1,0:T(8,128)(2,1)S(1)} %collective-permute-done.7.refs_2_), channel_id=1, source_target_pairs={{0,8},{8,16},{16,24},{24,28},{28,20},{20,12},{12,4},{4,0},{1,9},{9... | collective-permute-start | bytes 786440 | tf_op jit(solution)/shard_map/ppermute | solution.py:157
  33.5 11.1 %collective-permute-start.12 = (bf16[8,64,256]{2,1,0:T(8,128)(2,1)S(1)}, bf16[8,64,256]{2,1,0:T(8,128)(2,1)S(1)}, u32[]{:S(2)}, u32[]{:S(2)}) collective-permute-start(bf16[8,64,256]{2,1,0:T(8,128)(2,1)S(1)} %collective-permute-done.8.refs_3_), channel_id=1, source_target_pairs={{8,0},{16,8},{24,16},{28,24},{20,28},{12,20},{4,12},{0,4},{9,1},{1... | collective-permute-start | bytes 786440 | tf_op jit(solution)/shard_map/ppermute | solution.py:157
  33.5 13.7 %collective-permute-start.2 = (bf16[8,64,256]{2,1,0:T(8,128)(2,1)S(1)}, bf16[8,64,256]{2,1,0:T(8,128)(2,1)S(1)}, u32[]{:S(2)}, u32[]{:S(2)}) collective-permute-start(bf16[8,64,256]{2,1,0:T(8,128)(2,1)S(1)} %collective-permute-done.1.refs_0_), channel_id=1, source_target_pairs={{0,8},{8,16},{16,24},{24,28},{28,20},{20,12},{12,4},{4,0},{1,9},{9... | collective-permute-start | bytes 786440 | tf_op jit(solution)/shard_map/ppermute | solution.py:157
  35.5 9.1 %collective-permute-start.14 = (f32[40,256]{1,0:T(8,128)S(1)}, f32[40,256]{1,0:T(8,128)S(1)}, u32[]{:S(2)}, u32[]{:S(2)}) collective-permute-start(f32[40,256]{1,0:T(8,128)S(1)} %add.46), channel_id=1, source_target_pairs={{0,16},{4,20},{8,24},{12,28},{16,0},{20,4},{24,8},{28,12},{1,17},{... | collective-permute-start | bytes 122888 | tf_op jit(solution)/shard_map/ppermute | solution.py:139
  38.1 11.8 %collective-permute-start.16 = (bf16[8,64,256]{2,1,0:T(8,128)(2,1)S(1)}, bf16[8,64,256]{2,1,0:T(8,128)(2,1)S(1)}, u32[]{:S(2)}, u32[]{:S(2)}) collective-permute-start(bf16[8,64,256]{2,1,0:T(8,128)(2,1)S(1)} %collective-permute-done.13.refs_1_), channel_id=1, source_target_pairs={{8,0},{16,8},{24,16},{28,24},{20,28},{12,20},{4,12},{0,4},{9,1},{1... | collective-permute-start | bytes 786440 | tf_op jit(solution)/shard_map/ppermute | solution.py:157
  44.7 8.1 %collective-permute-start.15 = (bf16[8,64,256]{2,1,0:T(8,128)(2,1)S(1)}, bf16[8,64,256]{2,1,0:T(8,128)(2,1)S(1)}, u32[]{:S(2)}, u32[]{:S(2)}) collective-permute-start(bf16[8,64,256]{2,1,0:T(8,128)(2,1)S(1)} %collective-permute-done.12.refs_3_), channel_id=1, source_target_pairs={{8,0},{16,8},{24,16},{28,24},{20,28},{12,20},{4,12},{0,4},{9,1},{1... | collective-permute-start | bytes 786440 | tf_op jit(solution)/shard_map/ppermute | solution.py:166
  47.2 6.4 %collective-permute-start.3 = (bf16[8,64,256]{2,1,0:T(8,128)(2,1)S(1)}, bf16[8,64,256]{2,1,0:T(8,128)(2,1)S(1)}, u32[]{:S(2)}, u32[]{:S(2)}) collective-permute-start(bf16[8,64,256]{2,1,0:T(8,128)(2,1)S(1)} %collective-permute-done.2.refs_0_), channel_id=1, source_target_pairs={{0,8},{8,16},{16,24},{24,28},{28,20},{20,12},{12,4},{4,0},{1,9},{9... | collective-permute-start | bytes 786440 | tf_op jit(solution)/shard_map/ppermute | solution.py:164
  47.2 1.6 %collective-permute-start.17 = (f32[40,256]{1,0:T(8,128)S(1)}, f32[40,256]{1,0:T(8,128)S(1)}, u32[]{:S(2)}, u32[]{:S(2)}) collective-permute-start(f32[40,256]{1,0:T(8,128)S(1)} %add.47), channel_id=1, source_target_pairs={{0,1},{1,0},{2,3},{3,2},{4,5},{5,4},{6,7},{7,6},{8,9},{9,8},{10,11... | collective-permute-start | bytes 122888 | tf_op jit(solution)/shard_map/ppermute | solution.py:139
  47.2 4.1 %collective-permute-start.18 = (f32[40,256]{1,0:T(8,128)S(1)}, f32[40,256]{1,0:T(8,128)S(1)}, u32[]{:S(2)}, u32[]{:S(2)}) collective-permute-start(f32[40,256]{1,0:T(8,128)S(1)} %add.47), channel_id=1, source_target_pairs={{0,2},{1,3},{2,0},{3,1},{4,6},{5,7},{6,4},{7,5},{8,10},{9,11},{10,... | collective-permute-start | bytes 122888 | tf_op jit(solution)/shard_map/ppermute | solution.py:139
  48.8 4.0 %collective-permute-start.19 = (f32[40,256]{1,0:T(8,128)S(1)}, f32[40,256]{1,0:T(8,128)S(1)}, u32[]{:S(2)}, u32[]{:S(2)}) collective-permute-start(f32[40,256]{1,0:T(8,128)S(1)} %collective-permute-done.17), channel_id=1, source_target_pairs={{0,2},{1,3},{2,0},{3,1},{4,6},{5,7},{6,4},{7,5},{8,10},{9,11},{10,... | collective-permute-start | bytes 122888 | tf_op jit(solution)/shard_map/ppermute | solution.py:139
  51.0 12.7 %copy-start.4 = (f32[256,32]{0,1:T(8,128)S(1)}, f32[256,32]{0,1:T(8,128)}, u32[]{:S(2)}) copy-start(f32[256,32]{0,1:T(8,128)} %param.13) | copy-start | bytes 98308
  51.0 13.3 %copy-start.6 = (f32[256]{0:T(256)S(1)}, f32[256]{0:T(256)}, u32[]{:S(2)}) copy-start(f32[256]{0:T(256)} %param.15) | copy-start | bytes 3076
  54.5 1.6 %collective-permute-start.20 = (f32[256,256]{1,0:T(8,128)S(1)}, f32[256,256]{1,0:T(8,128)S(1)}, u32[]{:S(2)}, u32[]{:S(2)}) collective-permute-start(f32[256,256]{1,0:T(8,128)S(1)} %pad_maximum_fusion), channel_id=1, source_target_pairs={{0,1},{1,0},{2,3},{3,2},{4,5},{5,4},{6,7},{7,6},{8,9},{9,8},{10,11... | collective-permute-start | bytes 786440 | tf_op jit(solution)/shard_map/ppermute | solution.py:139
  56.1 5.6 %collective-permute-start.21 = (f32[128,256]{1,0:T(8,128)S(1)}, f32[128,256]{1,0:T(8,128)S(1)}, u32[]{:S(2)}, u32[]{:S(2)}) collective-permute-start(f32[128,256]{1,0:T(8,128)S(1)} %slice_add_fusion), channel_id=1, source_target_pairs={{0,2},{1,3},{2,0},{3,1},{4,6},{5,7},{6,4},{7,5},{8,10},{9,11},{10,... | collective-permute-start | bytes 393224 | tf_op jit(solution)/shard_map/ppermute | solution.py:139
  57.7 6.0 %collective-permute-start.23 = (f32[160,256]{1,0:T(8,128)S(1)}, f32[160,256]{1,0:T(8,128)S(1)}, u32[]{:S(2)}, u32[]{:S(2)}) collective-permute-start(f32[160,256]{1,0:T(8,128)S(1)} %constant_dynamic-update-slice_fusion.held), channel_id=1, source_target_pairs={{0,4},{4,0},{8,12},{12,8},{16,20},{20,16},{24,28},{28,24},{1,5},{5... | collective-permute-start | bytes 491528 | tf_op jit(solution)/shard_map/ppermute | solution.py:139
  61.7 2.6 %collective-permute-start.22 = (f32[128,256]{1,0:T(8,128)S(1)}, f32[128,256]{1,0:T(8,128)S(1)}, u32[]{:S(2)}, u32[]{:S(2)}) collective-permute-start(f32[128,256]{1,0:T(8,128)S(1)} %collective-permute-done.21.far), channel_id=1, source_target_pairs={{0,1},{1,0},{2,3},{3,2},{4,5},{5,4},{6,7},{7,6},{8,9},{9,8},{10,11... | collective-permute-start | bytes 393224 | tf_op jit(solution)/shard_map/ppermute | solution.py:139

commit v4 on v3

--- a/solution.py
+++ b/solution.py
@@ -77,20 +77,19 @@
     )(slot_block, current, *panels, earlier, *before)
 
 
-def tile_kernel(held, given, cands, tile, high, low, points):
+def two_parts(value):
+    top = value.astype(jnp.bfloat16)
+    return top, (value - top.astype(jnp.float32)).astype(jnp.bfloat16)
+
+
+def tile_kernel(s0, s1, s2, s3, cands, tile, high, low, points):
     obs = lax.axis_index("obs")
-    side = lax.rem(lax.axis_index("cand"), 2)
     share = points.shape[0] // 4
-    size = held.shape[0] // 4
-    rows = size - share
-    for m in range(4):
-        points[pl.ds(pl.multiple_of((obs ^ m) * share, share), share), :] = held[m * size + rows : (m + 1) * size, :]
-        for piece, place in ((held, side), (given, 1 - side)):
-            inverse = piece[m * size : m * size + rows, :]
-            top = inverse.astype(jnp.bfloat16)
-            here = pl.ds(pl.multiple_of((2 * m + place) * rows, rows), rows)
-            high[here, :] = top
-            low[here, :] = (inverse - top.astype(jnp.float32)).astype(jnp.bfloat16)
+    rows = high.shape[0] // 4
+    for m, spread in enumerate((s0, s1, s2, s3)):
+        points[pl.ds(pl.multiple_of((obs ^ m) * share, share), share), :] = spread[rows:, :]
+        here = slice(m * rows, (m + 1) * rows)
+        high[here, :], low[here, :] = two_parts(spread[:rows, :])
     p = points[...]
     p = p / jnp.sum(p, axis=0, keepdims=True)
     c = cands[...]
@@ -101,21 +100,23 @@
     tile[...] = jnp.exp(-10.0 * squared)
 
 
-def solve_kernel(mine, other, mate, far, mate_far, tile, high, low, prior, solved, remaining, residual):
-    half, rows = mine.shape[0], solved.shape[0]
+def solve_kernel(mine, other, mate, far, mate_far, tile, high, low, given, prior, solved, remaining, residual):
+    half, rows = mine.shape[0], solved.shape[0] // 2
     core = lax.rem(lax.axis_index("obs"), 2)
+    side = lax.rem(lax.axis_index("cand"), 2)
     first = pl.ds(pl.multiple_of(core * half, half), half)
     second = pl.ds(pl.multiple_of((1 - core) * half, half), half)
     residual[first, :] = tile[first, :] - (mine[...] + mate[half:, :] + far[...])
     residual[second, :] = tile[second, :] - (other[...] + mate[:half, :] + mate_far[...])
-    value = residual[...]
-    top = value.astype(jnp.bfloat16)
-    rest = (value - top.astype(jnp.float32)).astype(jnp.bfloat16)
-    part = jnp.dot(low[...], top, preferred_element_type=jnp.float32)
-    part += jnp.dot(high[...], rest, preferred_element_type=jnp.float32)
-    part += jnp.dot(high[...], top, preferred_element_type=jnp.float32)
-    solved[...] = part[:rows]
-    remaining[...] = prior[...] - jnp.sum(part * part, axis=0, keepdims=True)
+    top, rest = two_parts(residual[...])
+    squares = prior[...]
+    for place, (left, left_rest) in ((side, (high[...], low[...])), (1 - side, two_parts(given[...]))):
+        part = jnp.dot(left_rest, top, preferred_element_type=jnp.float32)
+        part += jnp.dot(left, rest, preferred_element_type=jnp.float32)
+        part += jnp.dot(left, top, preferred_element_type=jnp.float32)
+        solved[pl.ds(pl.multiple_of(place * rows, rows), rows), :] = part[:rows]
+        squares -= jnp.sum(part * part, axis=0, keepdims=True)
+    remaining[...] = squares
 
 
 def on_ring(
@@ -172,8 +173,7 @@
     spreads = [spread, flip(spread, "obs", 1, 4)]
     spreads += [flip(spreads[0], "obs", 2, 4), flip(spreads[1], "obs", 2, 4)]
     early, late, total, spreads = tie((early, late, total, spreads))
-    spread = jnp.concatenate(spreads, axis=0)
-    given = flip(spread, "cand", 1, 8)
+    given = flip(jnp.concatenate([v[:-share] for v in spreads], axis=0), "cand", 1, 8)
     sources = [(-4, 0, held), (4, half, held)]
     mine, other = add(last_kernel, sources, slot_block, block_index, [early, late], earlier_rows, [total])
 
@@ -182,15 +182,15 @@
         tile_kernel,
         out_shape=[
             jax.ShapeDtypeStruct((size, cols), jnp.float32),
-            jax.ShapeDtypeStruct((4 * rows, size), jnp.bfloat16),
-            jax.ShapeDtypeStruct((4 * rows, size), jnp.bfloat16),
+            jax.ShapeDtypeStruct((2 * rows, size), jnp.bfloat16),
+            jax.ShapeDtypeStruct((2 * rows, size), jnp.bfloat16),
         ],
-        in_specs=[VMEM] * 3,
+        in_specs=[VMEM] * 5,
         out_specs=[VMEM] * 3,
         scratch_shapes=[pltpu.VMEM((obs_weights.shape[2], size), jnp.float32)],
         compiler_params=pltpu.CompilerParams(vmem_limit_bytes=LIMIT),
         cost_estimate=pl.CostEstimate(flops=10**7, bytes_accessed=10**6, transcendentals=65536),
-    )(spread, given, cand_weights.T)
+    )(*spreads, cand_weights.T)
 
     mate = flip(jnp.concatenate([mine, other], axis=0), "obs", 1, 4)
     far = flip(mine + mate[mine.shape[0] :], "obs", 2, 4)
@@ -201,12 +201,12 @@
             jax.ShapeDtypeStruct((rows, cols), jnp.float32),
             jax.ShapeDtypeStruct((1, cols), jnp.float32),
         ],
-        in_specs=[VMEM] * 9,
+        in_specs=[VMEM] * 10,
         out_specs=[VMEM] * 2,
         scratch_shapes=[pltpu.VMEM((panel.shape[2], cols), jnp.float32)],
         compiler_params=pltpu.CompilerParams(vmem_limit_bytes=LIMIT),
         cost_estimate=pl.CostEstimate(flops=2 * 10**8, bytes_accessed=10**6, transcendentals=0),
-    )(mine, other, mate, far, mate_far, tile, high, low, prior_var[None])
+    )(mine, other, mate, far, mate_far, tile, high, low, given, prior_var[None])
     return (solved_rows, remaining[0])
 
 

time: 65.5 us -> 64.3 us (0.982)
  waiting for transfers between devices: 23.7 us -> 22.4 us
    ppermute x10, waiting for transfers between devices: 18.9 us -> 17.7 us  [flip(): return lax.ppermute(value, axis, [(i, i ^ bits) for i in range(size)])]
    unnamed x17 -> x14, local copies, waits for them, and re-layouts: 3.93 us -> 3.91 us
where the time goes in v4:
time: 64.3 us; the launch traced here: 64.1 us
  starting transfers between devices  27.7 us (43%)
  waiting for transfers between devices  22.4 us (35%)
  Pallas kernels  6.46 us (10%)
  local copies, waits for them, and re-layouts  5.79 us (9%)
  between operations  1.6 us (2%)
    ppermute x10, waiting for transfers between devices, flip(): return lax.ppermute(value, axis, [(i, i ^ bits) for i in range(size)])  17.7 us
    ppermute x10, starting transfers between devices, flip(): return lax.ppermute(value, axis, [(i, i ^ bits) for i in range(size)])  12.9 us
    ppermute x6, starting transfers between devices, onward(): lax.ppermute(pair[0], 'cand', RING)  10.9 us
    pallas_call x5, Pallas kernels, add(): pl.pallas_call(functools.partial(kernel, sources), out_shape=[jax.ShapeDt...  4.88 us
    unnamed x14, local copies, waits for them, and re-layouts  3.91 us
    ppermute x1, starting transfers between devices, on_ring(): next_late = onward(late) if k < 3 else lax.ppermute(late[1], 'cand', BACK)  2.52 us
    ppermute x6, waiting for transfers between devices, onward(): lax.ppermute(pair[0], 'cand', RING)  2.37 us
    ppermute x6, waiting for transfers between devices, onward(): lax.ppermute(pair[1], 'cand', BACK)  1.61 us
  transfers between devices with their start and end apart: 24, of which 11 were waited for; matrix products, arithmetic and copies ran while one was open for 2% of the time, Pallas kernels for 7%

profile of v4, /device:TPU:0, one launch (start us, length us, event | category | flops | bytes accessed | tf_op | source)
XLA Modules:
  0.0 64.1 jit_solution(11441551576803763563)
XLA Ops:
  0.6 0.0 copy-start
  1.4 0.8 %dynamic-slice_bitcast_fusion.1 = (f32[32,256]{1,0:T(8,128)S(1)}, f32[32,256]{1,0:T(8,128)S(1)}) fusion(f32[16,64,256]{2,1,0:T(8,128)} %param.14, s32[]{:T(128)S(6)} %select_n.52, s32[]{:T(128)S(6)} %select_n.54, s32[]{:T(128)S(6)} %select_n.59), kind=kLoop, calls=%fused_computation.9 | loop fusion | bytes 131084 | tf_op jit(solution)/shard_map/squeeze | solution.py:149
  2.2 3.0 %collective-permute-start.6 = (f32[40,256]{1,0:T(8,128)S(1)}, f32[40,256]{1,0:T(8,128)S(1)}, u32[]{:S(2)}, u32[]{:S(2)}) collective-permute-start(f32[40,256]{1,0:T(8,128)S(1)} %fusion.2), channel_id=1, source_target_pairs={{0,4},{4,0},{8,12},{12,8},{16,20},{20,16},{24,28},{28,24},{1,5},{5... | collective-permute-start | bytes 122888 | tf_op jit(solution)/shard_map/ppermute | solution.py:140
  5.2 1.1 %fusion.3 = (bf16[8,64,256]{2,1,0:T(8,128)(2,1)S(1)}, bf16[8,64,256]{2,1,0:T(8,128)(2,1)S(1)}) fusion(bf16[16,64,256]{2,1,0:T(8,128)(2,1)} %bitcast.17), kind=kLoop, calls=%fused_computation.11 | loop fusion | bytes 1048576 | tf_op jit(solution)/shard_map/slice | solution.py:161
  6.3 1.6 %collective-permute-start.4 = (bf16[8,64,256]{2,1,0:T(8,128)(2,1)S(1)}, bf16[8,64,256]{2,1,0:T(8,128)(2,1)S(1)}, u32[]{:S(2)}, u32[]{:S(2)}) collective-permute-start(bf16[8,64,256]{2,1,0:T(8,128)(2,1)S(1)} %get-tuple-element.56), channel_id=1, source_target_pairs={{0,8},{8,16},{16,24},{24,28},{28,20},{20,12},{12,4},{4,0},{1,9},{9... | collective-permute-start | bytes 786440 | tf_op jit(solution)/shard_map/ppermute | solution.py:158
  7.9 0.4 collective-permute-start.5
  8.4 1.6 %collective-permute-start = (bf16[8,64,256]{2,1,0:T(8,128)(2,1)S(1)}, bf16[8,64,256]{2,1,0:T(8,128)(2,1)S(1)}, u32[]{:S(2)}, u32[]{:S(2)}) collective-permute-start(bf16[8,64,256]{2,1,0:T(8,128)(2,1)S(1)} %get-tuple-element.57), channel_id=1, source_target_pairs={{0,8},{8,16},{16,24},{24,28},{28,20},{20,12},{12,4},{4,0},{1,9},{9... | collective-permute-start | bytes 786440 | tf_op jit(solution)/shard_map/ppermute | solution.py:158
  10.0 0.4 collective-permute-start.9
  10.4 2.2 %copy-done.1 = bf16[128,64,256]{2,1,0:T(8,128)(2,1)S(1)} copy-done((bf16[128,64,256]{2,1,0:T(8,128)(2,1)S(1)}, bf16[128,64,256]{2,1,0:T(8,128)(2,1)}, u32[]{:S(2)}) %copy-start.1) | copy-done | bytes 4194328
  12.6 1.0 %copy-done.3 = bf16[16,256,64]{1,2,0:T(8,128)(2,1)S(1)} copy-done((bf16[16,256,64]{1,2,0:T(8,128)(2,1)S(1)}, bf16[16,256,64]{1,2,0:T(8,128)(2,1)}, u32[]{:S(2)}) %copy-start.3) | copy-done | bytes 524312
  13.6 0.7 %copy-done.5 = s32[128]{0:T(128)S(1)} copy-done((s32[128]{0:T(128)S(1)}, s32[128]{0:T(128)}, u32[]{:S(2)}) %copy-start.5) | copy-done | bytes 536
  14.3 0.9 %shard_map.95.refs_5_ = f32[256,256]{1,0:T(8,128)S(1)} custom-call(s32[128]{0:T(128)S(1)} %copy-done.5, s32[1]{0:T(128)} %copy.10.current, bf16[16,64,256]{2,1,0:T(8,128)(2,1)S(1)} %bitcast.18, bf16[128,64,256]{2,1,0:T(8,128)(2,1)S(1)} %copy-done.1), custom_call_target="tpu_custom_call" | custom-call | flops 134217728 | bytes 1048576 | tf_op jit(solution)/shard_map/pallas_call | solution.py:65
  15.2 0.0 collective-permute-done.6
  15.2 0.4 collective-permute-done.4.refs_2_
  15.6 1.6 %collective-permute-done.5.refs_3_ = bf16[8,64,256]{2,1,0:T(8,128)(2,1)S(1)} collective-permute-done((bf16[8,64,256]{2,1,0:T(8,128)(2,1)S(1)}, bf16[8,64,256]{2,1,0:T(8,128)(2,1)S(1)}, u32[]{:S(2)}, u32[]{:S(2)}) %collective-permute-start.5) | collective-permute-done | bytes 262176 | tf_op jit(solution)/shard_map/ppermute | solution.py:158
  17.2 1.6 %collective-permute-start.7 = (bf16[8,64,256]{2,1,0:T(8,128)(2,1)S(1)}, bf16[8,64,256]{2,1,0:T(8,128)(2,1)S(1)}, u32[]{:S(2)}, u32[]{:S(2)}) collective-permute-start(bf16[8,64,256]{2,1,0:T(8,128)(2,1)S(1)} %collective-permute-done.4.refs_2_), channel_id=1, source_target_pairs={{0,8},{8,16},{16,24},{24,28},{28,20},{20,12},{12,4},{4,0},{1,9},{9... | collective-permute-start | bytes 786440 | tf_op jit(solution)/shard_map/ppermute | solution.py:158
  18.8 0.4 collective-permute-start.8
  19.2 2.0 %collective-permute-done.refs_0_ = bf16[8,64,256]{2,1,0:T(8,128)(2,1)S(1)} collective-permute-done((bf16[8,64,256]{2,1,0:T(8,128)(2,1)S(1)}, bf16[8,64,256]{2,1,0:T(8,128)(2,1)S(1)}, u32[]{:S(2)}, u32[]{:S(2)}) %collective-permute-start) | collective-permute-done | bytes 262176 | tf_op jit(solution)/shard_map/ppermute | solution.py:158
  21.2 1.6 %collective-permute-start.1 = (bf16[8,64,256]{2,1,0:T(8,128)(2,1)S(1)}, bf16[8,64,256]{2,1,0:T(8,128)(2,1)S(1)}, u32[]{:S(2)}, u32[]{:S(2)}) collective-permute-start(bf16[8,64,256]{2,1,0:T(8,128)(2,1)S(1)} %collective-permute-done.refs_0_), channel_id=1, source_target_pairs={{0,8},{8,16},{16,24},{24,28},{28,20},{20,12},{12,4},{4,0},{1,9},{9... | collective-permute-start | bytes 786440 | tf_op jit(solution)/shard_map/ppermute | solution.py:158
  22.8 1.6 %collective-permute-start.10 = (f32[40,256]{1,0:T(8,128)S(1)}, f32[40,256]{1,0:T(8,128)S(1)}, u32[]{:S(2)}, u32[]{:S(2)}) collective-permute-start(f32[40,256]{1,0:T(8,128)S(1)} %fusion.1), channel_id=1, source_target_pairs={{0,8},{4,12},{8,0},{12,4},{16,24},{20,28},{24,16},{28,20},{1,9},{5... | collective-permute-start | bytes 122888 | tf_op jit(solution)/shard_map/ppermute | solution.py:140
  24.4 0.0 collective-permute-done.9.refs_1_
  24.4 0.0 collective-permute-start.13
  24.4 1.0 %shard_map.96.refs_5_ = f32[256,256]{1,0:T(8,128)S(1)} custom-call(s32[128]{0:T(128)S(1)} %copy-done.5, s32[1]{0:T(128)} %copy.10.current, bf16[8,64,256]{2,1,0:T(8,128)(2,1)S(1)} %collective-permute-done.refs_0_, bf16[8,64,256]{2,1,0:T(8,128)(2,1)S(1)} %collective-permute-done.9.refs_1_, bf16[8,64,256]{2,1,0:T(8,128)(2,1)S(1)} %collective-permute-done.4.refs_2_, ...), custom_call_target="tpu_custom_call" | custom-call | flops 268435456 | bytes 2097152 | tf_op jit(solution)/shard_map/pallas_call | solution.py:65
  25.4 5.5 %collective-permute-done.10 = f32[40,256]{1,0:T(8,128)S(1)} collective-permute-done((f32[40,256]{1,0:T(8,128)S(1)}, f32[40,256]{1,0:T(8,128)S(1)}, u32[]{:S(2)}, u32[]{:S(2)}) %collective-permute-start.10) | collective-permute-done | bytes 40992 | tf_op jit(solution)/shard_map/ppermute | solution.py:140
  31.0 2.5 %collective-permute-start.11 = (bf16[8,64,256]{2,1,0:T(8,128)(2,1)S(1)}, bf16[8,64,256]{2,1,0:T(8,128)(2,1)S(1)}, u32[]{:S(2)}, u32[]{:S(2)}) collective-permute-start(bf16[8,64,256]{2,1,0:T(8,128)(2,1)S(1)} %collective-permute-done.7.refs_2_), channel_id=1, source_target_pairs={{0,8},{8,16},{16,24},{24,28},{28,20},{20,12},{12,4},{4,0},{1,9},{9... | collective-permute-start | bytes 786440 | tf_op jit(solution)/shard_map/ppermute | solution.py:158
  33.5 0.0 collective-permute-done.1.refs_0_
  33.5 2.0 %collective-permute-start.2 = (bf16[8,64,256]{2,1,0:T(8,128)(2,1)S(1)}, bf16[8,64,256]{2,1,0:T(8,128)(2,1)S(1)}, u32[]{:S(2)}, u32[]{:S(2)}) collective-permute-start(bf16[8,64,256]{2,1,0:T(8,128)(2,1)S(1)} %collective-permute-done.1.refs_0_), channel_id=1, source_target_pairs={{0,8},{8,16},{16,24},{24,28},{28,20},{20,12},{12,4},{4,0},{1,9},{9... | collective-permute-start | bytes 786440 | tf_op jit(solution)/shard_map/ppermute | solution.py:158
  35.5 2.6 %collective-permute-start.14 = (f32[40,256]{1,0:T(8,128)S(1)}, f32[40,256]{1,0:T(8,128)S(1)}, u32[]{:S(2)}, u32[]{:S(2)}) collective-permute-start(f32[40,256]{1,0:T(8,128)S(1)} %add.46), channel_id=1, source_target_pairs={{0,16},{4,20},{8,24},{12,28},{16,0},{20,4},{24,8},{28,12},{1,17},{... | collective-permute-start | bytes 122888 | tf_op jit(solution)/shard_map/ppermute | solution.py:140
  38.1 1.0 %shard_map.97.refs_5_ = f32[256,256]{1,0:T(8,128)S(1)} custom-call(s32[128]{0:T(128)S(1)} %copy-done.5, s32[1]{0:T(128)} %copy.10.current, bf16[8,64,256]{2,1,0:T(8,128)(2,1)S(1)} %collective-permute-done.1.refs_0_, bf16[8,64,256]{2,1,0:T(8,128)(2,1)S(1)} %collective-permute-done.13.refs_1_, bf16[8,64,256]{2,1,0:T(8,128)(2,1)S(1)} %collective-permute-done.7.refs_2_, ...), custom_call_target="tpu_custom_call" | custom-call | flops 268435456 | bytes 2097152 | tf_op jit(solution)/shard_map/pallas_call | solution.py:65
  39.2 5.5 %collective-permute-done.14 = f32[40,256]{1,0:T(8,128)S(1)} collective-permute-done((f32[40,256]{1,0:T(8,128)S(1)}, f32[40,256]{1,0:T(8,128)S(1)}, u32[]{:S(2)}, u32[]{:S(2)}) %collective-permute-start.14) | collective-permute-done | bytes 40992 | tf_op jit(solution)/shard_map/ppermute | solution.py:140
  44.7 2.5 %collective-permute-start.15 = (bf16[8,64,256]{2,1,0:T(8,128)(2,1)S(1)}, bf16[8,64,256]{2,1,0:T(8,128)(2,1)S(1)}, u32[]{:S(2)}, u32[]{:S(2)}) collective-permute-start(bf16[8,64,256]{2,1,0:T(8,128)(2,1)S(1)} %collective-permute-done.12.refs_3_), channel_id=1, source_target_pairs={{8,0},{16,8},{24,16},{28,24},{20,28},{12,20},{4,12},{0,4},{9,1},{1... | collective-permute-start | bytes 786440 | tf_op jit(solution)/shard_map/ppermute | solution.py:167
  47.2 1.6 %collective-permute-start.18 = (f32[40,256]{1,0:T(8,128)S(1)}, f32[40,256]{1,0:T(8,128)S(1)}, u32[]{:S(2)}, u32[]{:S(2)}) collective-permute-start(f32[40,256]{1,0:T(8,128)S(1)} %add.47.s0), channel_id=1, source_target_pairs={{0,2},{1,3},{2,0},{3,1},{4,6},{5,7},{6,4},{7,5},{8,10},{9,11},{10,... | collective-permute-start | bytes 122888 | tf_op jit(solution)/shard_map/ppermute | solution.py:140
  48.8 1.1 %collective-permute-start.19 = (f32[40,256]{1,0:T(8,128)S(1)}, f32[40,256]{1,0:T(8,128)S(1)}, u32[]{:S(2)}, u32[]{:S(2)}) collective-permute-start(f32[40,256]{1,0:T(8,128)S(1)} %collective-permute-done.17.s1), channel_id=1, source_target_pairs={{0,2},{1,3},{2,0},{3,1},{4,6},{5,7},{6,4},{7,5},{8,10},{9,11},{10,... | collective-permute-start | bytes 122888 | tf_op jit(solution)/shard_map/ppermute | solution.py:140
  49.9 1.0 %shard_map.98.before = f32[256,256]{1,0:T(8,128)S(1)} custom-call(s32[128]{0:T(128)S(1)} %copy-done.5, s32[1]{0:T(128)} %copy.10.current, bf16[8,64,256]{2,1,0:T(8,128)(2,1)S(1)} %collective-permute-done.2.refs_0_, bf16[8,64,256]{2,1,0:T(8,128)(2,1)S(1)} %collective-permute-done.16.refs_1_, bf16[8,64,256]{2,1,0:T(8,128)(2,1)S(1)} %collective-permute-done.11.refs_2_, ...), custom_call_target="tpu_custom_call" | custom-call | flops 268435456 | bytes 2097152 | tf_op jit(solution)/shard_map/pallas_call | solution.py:65
  51.0 0.0 copy-start.4
  51.0 0.0 copy-start.6
  51.0 0.3 collective-permute-done.18.s2
  51.3 1.5 %collective-permute-done.19.s3 = f32[40,256]{1,0:T(8,128)S(1)} collective-permute-done((f32[40,256]{1,0:T(8,128)S(1)}, f32[40,256]{1,0:T(8,128)S(1)}, u32[]{:S(2)}, u32[]{:S(2)}) %collective-permute-start.19) | collective-permute-done | bytes 40992 | tf_op jit(solution)/shard_map/ppermute | solution.py:140
  52.8 0.8 %collective-permute-done.3.panel_a = bf16[8,64,256]{2,1,0:T(8,128)(2,1)S(1)} collective-permute-done((bf16[8,64,256]{2,1,0:T(8,128)(2,1)S(1)}, bf16[8,64,256]{2,1,0:T(8,128)(2,1)S(1)}, u32[]{:S(2)}, u32[]{:S(2)}) %collective-permute-start.3) | collective-permute-done | bytes 262176 | tf_op jit(solution)/shard_map/ppermute | solution.py:165
  53.6 0.9 %shard_map.99 = (f32[128,256]{1,0:T(8,128)S(1)}, f32[128,256]{1,0:T(8,128)S(1)}) custom-call(s32[128]{0:T(128)S(1)} %copy-done.5, s32[1]{0:T(128)} %copy.10.current, bf16[8,64,256]{2,1,0:T(8,128)(2,1)S(1)} %collective-permute-done.3.panel_a, bf16[8,64,256]{2,1,0:T(8,128)(2,1)S(1)} %collective-permute-done.15.panel_b, bf16[128,64,256]{2,1,0:T(8,128)(2,1)S(1)} %copy-done.2, ...), custom_call_target="tpu_custom_call" | custom-call | flops 134217728 | bytes 1048576 | tf_op jit(solution)/shard_map/pallas_call | solution.py:65
  54.5 0.1 collective-permute-start.20
  54.6 1.5 %collective-permute-done.20.mate = f32[256,256]{1,0:T(8,128)S(1)} collective-permute-done((f32[256,256]{1,0:T(8,128)S(1)}, f32[256,256]{1,0:T(8,128)S(1)}, u32[]{:S(2)}, u32[]{:S(2)}) %collective-permute-start.20) | collective-permute-done | bytes 262176 | tf_op jit(solution)/shard_map/ppermute | solution.py:140
  56.1 1.6 %collective-permute-start.21 = (f32[128,256]{1,0:T(8,128)S(1)}, f32[128,256]{1,0:T(8,128)S(1)}, u32[]{:S(2)}, u32[]{:S(2)}) collective-permute-start(f32[128,256]{1,0:T(8,128)S(1)} %slice_add_fusion), channel_id=1, source_target_pairs={{0,2},{1,3},{2,0},{3,1},{4,6},{5,7},{6,4},{7,5},{8,10},{9,11},{10,... | collective-permute-start | bytes 393224 | tf_op jit(solution)/shard_map/ppermute | solution.py:140
  57.7 1.4 %collective-permute-start.23 = (f32[128,256]{1,0:T(8,128)S(1)}, f32[128,256]{1,0:T(8,128)S(1)}, u32[]{:S(2)}, u32[]{:S(2)}) collective-permute-start(f32[128,256]{1,0:T(8,128)S(1)} %pad_maximum_fusion.1), channel_id=1, source_target_pairs={{0,4},{4,0},{8,12},{12,8},{16,20},{20,16},{24,28},{28,24},{1,5},{5... | collective-permute-start | bytes 393224 | tf_op jit(solution)/shard_map/ppermute | solution.py:140
  59.1 2.6 %collective-permute-done.21.far = f32[128,256]{1,0:T(8,128)S(1)} collective-permute-done((f32[128,256]{1,0:T(8,128)S(1)}, f32[128,256]{1,0:T(8,128)S(1)}, u32[]{:S(2)}, u32[]{:S(2)}) %collective-permute-start.21) | collective-permute-done | bytes 131104 | tf_op jit(solution)/shard_map/ppermute | solution.py:140
  61.7 0.6 shard_map.100
  62.3 0.7 %collective-permute-done.23.given = f32[128,256]{1,0:T(8,128)S(1)} collective-permute-done((f32[128,256]{1,0:T(8,128)S(1)}, f32[128,256]{1,0:T(8,128)S(1)}, u32[]{:S(2)}, u32[]{:S(2)}) %collective-permute-start.23) | collective-permute-done | bytes 131104 | tf_op jit(solution)/shard_map/ppermute | solution.py:140
  63.1 1.0 %shard_map.101 = (f32[64,256]{1,0:T(8,128)}, f32[1,256]{1,0:T(1,128)}) custom-call(f32[128,256]{1,0:T(8,128)S(1)} %get-tuple-element.43.mine, f32[128,256]{1,0:T(8,128)S(1)} %get-tuple-element.44.other, f32[256,256]{1,0:T(8,128)S(1)} %collective-permute-done.20.mate, f32[128,256]{1,0:T(8,128)S(1)} %collective-permute-done.21.far, ...), custom_call_target="tpu_custom_call" | custom-call | flops 200000000 | bytes 1000000 | tf_op jit(solution)/shard_map/pallas_call | solution.py:198
  (35 shorter events, 0.2 us)
Async XLA Ops:
  0.6 1.6 %copy-start = (f32[16,256,32]{1,2,0:T(8,128)S(1)}, f32[16,256,32]{1,2,0:T(8,128)}, u32[]{:S(2)}) copy-start(f32[16,256,32]{1,2,0:T(8,128)} %param.12) | copy-start | bytes 1572868
  2.2 13.0 %collective-permute-start.6 = (f32[40,256]{1,0:T(8,128)S(1)}, f32[40,256]{1,0:T(8,128)S(1)}, u32[]{:S(2)}, u32[]{:S(2)}) collective-permute-start(f32[40,256]{1,0:T(8,128)S(1)} %fusion.2), channel_id=1, source_target_pairs={{0,4},{4,0},{8,12},{12,8},{16,20},{20,16},{24,28},{28,24},{1,5},{5... | collective-permute-start | bytes 122888 | tf_op jit(solution)/shard_map/ppermute | solution.py:140
  6.3 9.3 %collective-permute-start.4 = (bf16[8,64,256]{2,1,0:T(8,128)(2,1)S(1)}, bf16[8,64,256]{2,1,0:T(8,128)(2,1)S(1)}, u32[]{:S(2)}, u32[]{:S(2)}) collective-permute-start(bf16[8,64,256]{2,1,0:T(8,128)(2,1)S(1)} %get-tuple-element.56), channel_id=1, source_target_pairs={{0,8},{8,16},{16,24},{24,28},{28,20},{20,12},{12,4},{4,0},{1,9},{9... | collective-permute-start | bytes 786440 | tf_op jit(solution)/shard_map/ppermute | solution.py:158
  7.9 9.2 %collective-permute-start.5 = (bf16[8,64,256]{2,1,0:T(8,128)(2,1)S(1)}, bf16[8,64,256]{2,1,0:T(8,128)(2,1)S(1)}, u32[]{:S(2)}, u32[]{:S(2)}) collective-permute-start(bf16[8,64,256]{2,1,0:T(8,128)(2,1)S(1)} %get-tuple-element.56), channel_id=1, source_target_pairs={{8,0},{16,8},{24,16},{28,24},{20,28},{12,20},{4,12},{0,4},{9,1},{1... | collective-permute-start | bytes 786440 | tf_op jit(solution)/shard_map/ppermute | solution.py:158
  8.4 12.8 %collective-permute-start = (bf16[8,64,256]{2,1,0:T(8,128)(2,1)S(1)}, bf16[8,64,256]{2,1,0:T(8,128)(2,1)S(1)}, u32[]{:S(2)}, u32[]{:S(2)}) collective-permute-start(bf16[8,64,256]{2,1,0:T(8,128)(2,1)S(1)} %get-tuple-element.57), channel_id=1, source_target_pairs={{0,8},{8,16},{16,24},{24,28},{28,20},{20,12},{12,4},{4,0},{1,9},{9... | collective-permute-start | bytes 786440 | tf_op jit(solution)/shard_map/ppermute | solution.py:158
  10.0 14.4 %collective-permute-start.9 = (bf16[8,64,256]{2,1,0:T(8,128)(2,1)S(1)}, bf16[8,64,256]{2,1,0:T(8,128)(2,1)S(1)}, u32[]{:S(2)}, u32[]{:S(2)}) collective-permute-start(bf16[8,64,256]{2,1,0:T(8,128)(2,1)S(1)} %get-tuple-element.57), channel_id=1, source_target_pairs={{8,0},{16,8},{24,16},{28,24},{20,28},{12,20},{4,12},{0,4},{9,1},{1... | collective-permute-start | bytes 786440 | tf_op jit(solution)/shard_map/ppermute | solution.py:158
  10.4 2.2 %copy-start.1 = (bf16[128,64,256]{2,1,0:T(8,128)(2,1)S(1)}, bf16[128,64,256]{2,1,0:T(8,128)(2,1)}, u32[]{:S(2)}) copy-start(bf16[128,64,256]{2,1,0:T(8,128)(2,1)} %earlier.3) | copy-start | bytes 12582916
  12.6 1.0 %copy-start.3 = (bf16[16,256,64]{1,2,0:T(8,128)(2,1)S(1)}, bf16[16,256,64]{1,2,0:T(8,128)(2,1)}, u32[]{:S(2)}) copy-start(bf16[16,256,64]{1,2,0:T(8,128)(2,1)} %param.10) | copy-start | bytes 1572868
  13.6 0.7 %copy-start.5 = (s32[128]{0:T(128)S(1)}, s32[128]{0:T(128)}, u32[]{:S(2)}) copy-start(s32[128]{0:T(128)} %slot_block.9) | copy-start | bytes 1540
  14.3 10.1 %copy-start.2 = (bf16[128,64,256]{2,1,0:T(8,128)(2,1)S(1)}, bf16[128,64,256]{2,1,0:T(8,128)(2,1)}, u32[]{:S(2)}) copy-start(bf16[128,64,256]{2,1,0:T(8,128)(2,1)} %earlier.3) | copy-start | bytes 12582916
  17.2 13.8 %collective-permute-start.7 = (bf16[8,64,256]{2,1,0:T(8,128)(2,1)S(1)}, bf16[8,64,256]{2,1,0:T(8,128)(2,1)S(1)}, u32[]{:S(2)}, u32[]{:S(2)}) collective-permute-start(bf16[8,64,256]{2,1,0:T(8,128)(2,1)S(1)} %collective-permute-done.4.refs_2_), channel_id=1, source_target_pairs={{0,8},{8,16},{16,24},{24,28},{28,20},{20,12},{12,4},{4,0},{1,9},{9... | collective-permute-start | bytes 786440 | tf_op jit(solution)/shard_map/ppermute | solution.py:158
  18.8 12.2 %collective-permute-start.8 = (bf16[8,64,256]{2,1,0:T(8,128)(2,1)S(1)}, bf16[8,64,256]{2,1,0:T(8,128)(2,1)S(1)}, u32[]{:S(2)}, u32[]{:S(2)}) collective-permute-start(bf16[8,64,256]{2,1,0:T(8,128)(2,1)S(1)} %collective-permute-done.5.refs_3_), channel_id=1, source_target_pairs={{8,0},{16,8},{24,16},{28,24},{20,28},{12,20},{4,12},{0,4},{9,1},{1... | collective-permute-start | bytes 786440 | tf_op jit(solution)/shard_map/ppermute | solution.py:158
  21.2 12.3 %collective-permute-start.1 = (bf16[8,64,256]{2,1,0:T(8,128)(2,1)S(1)}, bf16[8,64,256]{2,1,0:T(8,128)(2,1)S(1)}, u32[]{:S(2)}, u32[]{:S(2)}) collective-permute-start(bf16[8,64,256]{2,1,0:T(8,128)(2,1)S(1)} %collective-permute-done.refs_0_), channel_id=1, source_target_pairs={{0,8},{8,16},{16,24},{24,28},{28,20},{20,12},{12,4},{4,0},{1,9},{9... | collective-permute-start | bytes 786440 | tf_op jit(solution)/shard_map/ppermute | solution.py:158
  22.8 8.2 %collective-permute-start.10 = (f32[40,256]{1,0:T(8,128)S(1)}, f32[40,256]{1,0:T(8,128)S(1)}, u32[]{:S(2)}, u32[]{:S(2)}) collective-permute-start(f32[40,256]{1,0:T(8,128)S(1)} %fusion.1), channel_id=1, source_target_pairs={{0,8},{4,12},{8,0},{12,4},{16,24},{20,28},{24,16},{28,20},{1,9},{5... | collective-permute-start | bytes 122888 | tf_op jit(solution)/shard_map/ppermute | solution.py:140
  24.4 13.8 %collective-permute-start.13 = (bf16[8,64,256]{2,1,0:T(8,128)(2,1)S(1)}, bf16[8,64,256]{2,1,0:T(8,128)(2,1)S(1)}, u32[]{:S(2)}, u32[]{:S(2)}) collective-permute-start(bf16[8,64,256]{2,1,0:T(8,128)(2,1)S(1)} %collective-permute-done.9.refs_1_), channel_id=1, source_target_pairs={{8,0},{16,8},{24,16},{28,24},{20,28},{12,20},{4,12},{0,4},{9,1},{1... | collective-permute-start | bytes 786440 | tf_op jit(solution)/shard_map/ppermute | solution.py:158
  31.0 13.7 %collective-permute-start.11 = (bf16[8,64,256]{2,1,0:T(8,128)(2,1)S(1)}, bf16[8,64,256]{2,1,0:T(8,128)(2,1)S(1)}, u32[]{:S(2)}, u32[]{:S(2)}) collective-permute-start(bf16[8,64,256]{2,1,0:T(8,128)(2,1)S(1)} %collective-permute-done.7.refs_2_), channel_id=1, source_target_pairs={{0,8},{8,16},{16,24},{24,28},{28,20},{20,12},{12,4},{4,0},{1,9},{9... | collective-permute-start | bytes 786440 | tf_op jit(solution)/shard_map/ppermute | solution.py:158
  33.5 11.1 %collective-permute-start.12 = (bf16[8,64,256]{2,1,0:T(8,128)(2,1)S(1)}, bf16[8,64,256]{2,1,0:T(8,128)(2,1)S(1)}, u32[]{:S(2)}, u32[]{:S(2)}) collective-permute-start(bf16[8,64,256]{2,1,0:T(8,128)(2,1)S(1)} %collective-permute-done.8.refs_3_), channel_id=1, source_target_pairs={{8,0},{16,8},{24,16},{28,24},{20,28},{12,20},{4,12},{0,4},{9,1},{1... | collective-permute-start | bytes 786440 | tf_op jit(solution)/shard_map/ppermute | solution.py:158
  33.5 13.7 %collective-permute-start.2 = (bf16[8,64,256]{2,1,0:T(8,128)(2,1)S(1)}, bf16[8,64,256]{2,1,0:T(8,128)(2,1)S(1)}, u32[]{:S(2)}, u32[]{:S(2)}) collective-permute-start(bf16[8,64,256]{2,1,0:T(8,128)(2,1)S(1)} %collective-permute-done.1.refs_0_), channel_id=1, source_target_pairs={{0,8},{8,16},{16,24},{24,28},{28,20},{20,12},{12,4},{4,0},{1,9},{9... | collective-permute-start | bytes 786440 | tf_op jit(solution)/shard_map/ppermute | solution.py:158
  35.5 9.1 %collective-permute-start.14 = (f32[40,256]{1,0:T(8,128)S(1)}, f32[40,256]{1,0:T(8,128)S(1)}, u32[]{:S(2)}, u32[]{:S(2)}) collective-permute-start(f32[40,256]{1,0:T(8,128)S(1)} %add.46), channel_id=1, source_target_pairs={{0,16},{4,20},{8,24},{12,28},{16,0},{20,4},{24,8},{28,12},{1,17},{... | collective-permute-start | bytes 122888 | tf_op jit(solution)/shard_map/ppermute | solution.py:140
  38.1 11.8 %collective-permute-start.16 = (bf16[8,64,256]{2,1,0:T(8,128)(2,1)S(1)}, bf16[8,64,256]{2,1,0:T(8,128)(2,1)S(1)}, u32[]{:S(2)}, u32[]{:S(2)}) collective-permute-start(bf16[8,64,256]{2,1,0:T(8,128)(2,1)S(1)} %collective-permute-done.13.refs_1_), channel_id=1, source_target_pairs={{8,0},{16,8},{24,16},{28,24},{20,28},{12,20},{4,12},{0,4},{9,1},{1... | collective-permute-start | bytes 786440 | tf_op jit(solution)/shard_map/ppermute | solution.py:158
  44.7 8.1 %collective-permute-start.15 = (bf16[8,64,256]{2,1,0:T(8,128)(2,1)S(1)}, bf16[8,64,256]{2,1,0:T(8,128)(2,1)S(1)}, u32[]{:S(2)}, u32[]{:S(2)}) collective-permute-start(bf16[8,64,256]{2,1,0:T(8,128)(2,1)S(1)} %collective-permute-done.12.refs_3_), channel_id=1, source_target_pairs={{8,0},{16,8},{24,16},{28,24},{20,28},{12,20},{4,12},{0,4},{9,1},{1... | collective-permute-start | bytes 786440 | tf_op jit(solution)/shard_map/ppermute | solution.py:167
  47.2 6.4 %collective-permute-start.3 = (bf16[8,64,256]{2,1,0:T(8,128)(2,1)S(1)}, bf16[8,64,256]{2,1,0:T(8,128)(2,1)S(1)}, u32[]{:S(2)}, u32[]{:S(2)}) collective-permute-start(bf16[8,64,256]{2,1,0:T(8,128)(2,1)S(1)} %collective-permute-done.2.refs_0_), channel_id=1, source_target_pairs={{0,8},{8,16},{16,24},{24,28},{28,20},{20,12},{12,4},{4,0},{1,9},{9... | collective-permute-start | bytes 786440 | tf_op jit(solution)/shard_map/ppermute | solution.py:165
  47.2 1.6 %collective-permute-start.17 = (f32[40,256]{1,0:T(8,128)S(1)}, f32[40,256]{1,0:T(8,128)S(1)}, u32[]{:S(2)}, u32[]{:S(2)}) collective-permute-start(f32[40,256]{1,0:T(8,128)S(1)} %add.47.s0), channel_id=1, source_target_pairs={{0,1},{1,0},{2,3},{3,2},{4,5},{5,4},{6,7},{7,6},{8,9},{9,8},{10,11... | collective-permute-start | bytes 122888 | tf_op jit(solution)/shard_map/ppermute | solution.py:140
  47.2 4.1 %collective-permute-start.18 = (f32[40,256]{1,0:T(8,128)S(1)}, f32[40,256]{1,0:T(8,128)S(1)}, u32[]{:S(2)}, u32[]{:S(2)}) collective-permute-start(f32[40,256]{1,0:T(8,128)S(1)} %add.47.s0), channel_id=1, source_target_pairs={{0,2},{1,3},{2,0},{3,1},{4,6},{5,7},{6,4},{7,5},{8,10},{9,11},{10,... | collective-permute-start | bytes 122888 | tf_op jit(solution)/shard_map/ppermute | solution.py:140
  48.8 4.0 %collective-permute-start.19 = (f32[40,256]{1,0:T(8,128)S(1)}, f32[40,256]{1,0:T(8,128)S(1)}, u32[]{:S(2)}, u32[]{:S(2)}) collective-permute-start(f32[40,256]{1,0:T(8,128)S(1)} %collective-permute-done.17.s1), channel_id=1, source_target_pairs={{0,2},{1,3},{2,0},{3,1},{4,6},{5,7},{6,4},{7,5},{8,10},{9,11},{10,... | collective-permute-start | bytes 122888 | tf_op jit(solution)/shard_map/ppermute | solution.py:140
  51.0 10.8 %copy-start.4 = (f32[256,32]{0,1:T(8,128)S(1)}, f32[256,32]{0,1:T(8,128)}, u32[]{:S(2)}) copy-start(f32[256,32]{0,1:T(8,128)} %param.13) | copy-start | bytes 98308
  51.0 12.1 %copy-start.6 = (f32[256]{0:T(256)S(1)}, f32[256]{0:T(256)}, u32[]{:S(2)}) copy-start(f32[256]{0:T(256)} %param.15) | copy-start | bytes 3076
  54.5 1.6 %collective-permute-start.20 = (f32[256,256]{1,0:T(8,128)S(1)}, f32[256,256]{1,0:T(8,128)S(1)}, u32[]{:S(2)}, u32[]{:S(2)}) collective-permute-start(f32[256,256]{1,0:T(8,128)S(1)} %pad_maximum_fusion), channel_id=1, source_target_pairs={{0,1},{1,0},{2,3},{3,2},{4,5},{5,4},{6,7},{7,6},{8,9},{9,8},{10,11... | collective-permute-start | bytes 786440 | tf_op jit(solution)/shard_map/ppermute | solution.py:140
  56.1 5.6 %collective-permute-start.21 = (f32[128,256]{1,0:T(8,128)S(1)}, f32[128,256]{1,0:T(8,128)S(1)}, u32[]{:S(2)}, u32[]{:S(2)}) collective-permute-start(f32[128,256]{1,0:T(8,128)S(1)} %slice_add_fusion), channel_id=1, source_target_pairs={{0,2},{1,3},{2,0},{3,1},{4,6},{5,7},{6,4},{7,5},{8,10},{9,11},{10,... | collective-permute-start | bytes 393224 | tf_op jit(solution)/shard_map/ppermute | solution.py:140
  57.7 5.3 %collective-permute-start.23 = (f32[128,256]{1,0:T(8,128)S(1)}, f32[128,256]{1,0:T(8,128)S(1)}, u32[]{:S(2)}, u32[]{:S(2)}) collective-permute-start(f32[128,256]{1,0:T(8,128)S(1)} %pad_maximum_fusion.1), channel_id=1, source_target_pairs={{0,4},{4,0},{8,12},{12,8},{16,20},{20,16},{24,28},{28,24},{1,5},{5... | collective-permute-start | bytes 393224 | tf_op jit(solution)/shard_map/ppermute | solution.py:140
  61.7 1.4 %collective-permute-start.22 = (f32[128,256]{1,0:T(8,128)S(1)}, f32[128,256]{1,0:T(8,128)S(1)}, u32[]{:S(2)}, u32[]{:S(2)}) collective-permute-start(f32[128,256]{1,0:T(8,128)S(1)} %collective-permute-done.21.far), channel_id=1, source_target_pairs={{0,1},{1,0},{2,3},{3,2},{4,5},{5,4},{6,7},{7,6},{8,9},{9,8},{10,11... | collective-permute-start | bytes 393224 | tf_op jit(solution)/shard_map/ppermute | solution.py:140

commit v5 on v4

--- a/solution.py
+++ b/solution.py
@@ -24,34 +24,46 @@
     return jnp.where(place < 4, 2 * place, 2 * (7 - place) + 1)
 
 
-def partial_sum(sources, slot_block, current, panels, earlier, rows):
+def look_up(source, slots, slot_block, current, earlier, rows):
     cand = lax.axis_index("cand")
     place = jnp.where(lax.rem(cand, 2) == 0, cand // 2, 7 - cand // 2)
-    slots, depth, _ = panels[0].shape
-    value = None
-    for j, (offset, first, held) in enumerate(sources):
-        base = ring_holder(place + offset) * held + first
-        for s in range(slots):
-            block = slot_block[base + s]
-            kept = (block < current[0]).astype(jnp.float32).astype(rows.dtype)
-            rows[j, s * depth : (s + 1) * depth, :] = earlier[block] * kept
-        left = panels[j][...].reshape(slots * depth, panels[j].shape[-1])
-        term = lax.dot_general(left, rows[j], ROWS, preferred_element_type=jnp.float32)
-        value = term if value is None else value + term
-    return value
+    offset, first, held = source
+    base = ring_holder(place + offset) * held + first
+    depth = rows.shape[0] // slots
+    for s in range(slots):
+        block = slot_block[base + s]
+        kept = (block < current[0]).astype(jnp.float32).astype(rows.dtype)
+        rows[s * depth : (s + 1) * depth, :] = earlier[block] * kept
+
+
+def product(panel, rows):
+    left = panel[...].reshape(rows.shape[0], panel.shape[-1])
+    return lax.dot_general(left, rows[...], ROWS, preferred_element_type=jnp.float32)
 
 
 def own_kernel(sources, slot_block, current, panel, earlier, total, rows):
-    total[...] = partial_sum(sources, slot_block, current, [panel], earlier, rows)
+    look_up(sources[0], panel.shape[0], slot_block, current, earlier, rows.at[0])
+    total[...] = product(panel, rows.at[0])
 
 
 def add_kernel(sources, slot_block, current, *refs):
     *panels, earlier, before, total, rows = refs
-    total[...] = before[...] + partial_sum(sources, slot_block, current, panels, earlier, rows)
-
-
-def last_kernel(sources, slot_block, current, panel_a, panel_b, earlier, before, mine, other, rows):
-    value = before[...] + partial_sum(sources, slot_block, current, [panel_a, panel_b], earlier, rows)
+    value = before[...]
+    for j, panel in enumerate(panels):
+        look_up(sources[j], panel.shape[0], slot_block, current, earlier, rows.at[j])
+        value += product(panel, rows.at[j])
+    total[...] = value
+
+
+def add_ahead_kernel(sources, slot_block, current, *refs):
+    *refs, ahead, rows = refs
+    add_kernel(sources, slot_block, current, *refs, rows)
+    for j in range(2):
+        look_up(sources[-2 + j], refs[0].shape[0], slot_block, current, refs[-3], ahead.at[j])
+
+
+def last_kernel(panel_a, panel_b, rows, before, mine, other):
+    value = before[...] + product(panel_a, rows.at[0]) + product(panel_b, rows.at[1])
     size = mine.shape[0]
     first = lax.rem(lax.axis_index("obs"), 2) == 0
     mine[...] = jnp.where(first, value[:size], value[size:])
@@ -61,12 +73,14 @@
 def add(kernel, sources, slot_block, current, panels, earlier, before=()):
     slots, depth, size = panels[0].shape
     cols = earlier.shape[-1]
-    shapes = [(size // 2, cols)] * 2 if kernel is last_kernel else [(size, cols)]
+    outs = [jax.ShapeDtypeStruct((size, cols), jnp.float32)]
+    if kernel is add_ahead_kernel:
+        outs.append(jax.ShapeDtypeStruct((2, slots * depth, cols), earlier.dtype))
     return pl.pallas_call(
         functools.partial(kernel, sources),
-        out_shape=[jax.ShapeDtypeStruct(shape, jnp.float32) for shape in shapes],
+        out_shape=outs,
         in_specs=[SMEM] * 2 + [VMEM] * (len(panels) + 1 + len(before)),
-        out_specs=[VMEM] * len(shapes),
+        out_specs=[VMEM] * len(outs),
         scratch_shapes=[pltpu.VMEM((len(panels), slots * depth, cols), earlier.dtype)],
         compiler_params=pltpu.CompilerParams(vmem_limit_bytes=LIMIT),
         cost_estimate=pl.CostEstimate(
@@ -75,6 +89,20 @@
             transcendentals=0,
         ),
     )(slot_block, current, *panels, earlier, *before)
+
+
+def add_last(panels, rows, before):
+    size, cols = before.shape
+    return pl.pallas_call(
+        last_kernel,
+        out_shape=[jax.ShapeDtypeStruct((size // 2, cols), jnp.float32)] * 2,
+        in_specs=[VMEM] * 4,
+        out_specs=[VMEM] * 2,
+        compiler_params=pltpu.CompilerParams(vmem_limit_bytes=LIMIT),
+        cost_estimate=pl.CostEstimate(
+            flops=4 * panels[0].size * cols, bytes_accessed=8 * panels[0].size, transcendentals=0
+        ),
+    )(*panels, rows, before)
 
 
 def two_parts(value):
@@ -166,16 +194,20 @@
         late, total, spread = tie((late, total, spread))
         next_late = onward(late) if k < 3 else lax.ppermute(late[1], "cand", BACK)
         sources = [(-k, 0, held), (k, 0, held), (-k, half, held), (k, half, held)]
-        (total,) = add(add_kernel, sources, slot_block, block_index, [*early, *late], earlier_rows, [total])
+        panels = [*early, *late]
+        if k < 3:
+            (total,) = add(add_kernel, sources, slot_block, block_index, panels, earlier_rows, [total])
+        else:
+            sources += [(-4, 0, held), (4, half, held)]
+            total, ahead = add(add_ahead_kernel, sources, slot_block, block_index, panels, earlier_rows, [total])
         if k < 3:
             spread = spread + flip(spread, "cand", 2 * k, 8)
         early, late = next_early, next_late
     spreads = [spread, flip(spread, "obs", 1, 4)]
     spreads += [flip(spreads[0], "obs", 2, 4), flip(spreads[1], "obs", 2, 4)]
-    early, late, total, spreads = tie((early, late, total, spreads))
+    early, late, total, ahead, spreads = tie((early, late, total, ahead, spreads))
     given = flip(jnp.concatenate([v[:-share] for v in spreads], axis=0), "cand", 1, 8)
-    sources = [(-4, 0, held), (4, half, held)]
-    mine, other = add(last_kernel, sources, slot_block, block_index, [early, late], earlier_rows, [total])
+    mine, other = add_last([early, late], ahead, total)
 
     size = panel.shape[2]
     tile, high, low = pl.pallas_call(

time: 64.3 us -> 63.8 us (level)
  no operation moved by 1% of the time
where the time goes in v5:
time: 63.8 us; the launch traced here: 63.5 us
  starting transfers between devices  27.7 us (43%)
  waiting for transfers between devices  22.3 us (35%)
  Pallas kernels  5.97 us (9%)
  local copies, waits for them, and re-layouts  5.79 us (9%)
  between operations  1.6 us (3%)
    ppermute x10, waiting for transfers between devices, flip(): return lax.ppermute(value, axis, [(i, i ^ bits) for i in range(size)])  17.6 us
    ppermute x10, starting transfers between devices, flip(): return lax.ppermute(value, axis, [(i, i ^ bits) for i in range(size)])  12.9 us
    ppermute x6, starting transfers between devices, onward(): lax.ppermute(pair[0], 'cand', RING)  10.9 us
    pallas_call x4, Pallas kernels, add(): pl.pallas_call(functools.partial(kernel, sources), out_shape=outs, in_spe...  4.07 us
    unnamed x14, local copies, waits for them, and re-layouts  3.91 us
    ppermute x1, starting transfers between devices, on_ring(): next_late = onward(late) if k < 3 else lax.ppermute(late[1], 'cand', BACK)  2.52 us
    ppermute x6, waiting for transfers between devices, onward(): lax.ppermute(pair[0], 'cand', RING)  2.37 us
    ppermute x6, waiting for transfers between devices, onward(): lax.ppermute(pair[1], 'cand', BACK)  1.61 us
  transfers between devices with their start and end apart: 24, of which 11 were waited for; matrix products, arithmetic and copies ran while one was open for 2% of the time, Pallas kernels for 7%

profile of v5, /device:TPU:0, one launch (start us, length us, event | category | flops | bytes accessed | tf_op | source)
XLA Modules:
  0.0 63.5 jit_solution(8876975262683894680)
XLA Ops:
  0.6 0.0 copy-start
  1.4 0.8 %dynamic-slice_bitcast_fusion.1 = (f32[32,256]{1,0:T(8,128)S(1)}, f32[32,256]{1,0:T(8,128)S(1)}) fusion(f32[16,64,256]{2,1,0:T(8,128)} %param.14, s32[]{:T(128)S(6)} %select_n.52, s32[]{:T(128)S(6)} %select_n.54, s32[]{:T(128)S(6)} %select_n.59), kind=kLoop, calls=%fused_computation.9 | loop fusion | bytes 131084 | tf_op jit(solution)/shard_map/squeeze | solution.py:177
  2.2 3.0 %collective-permute-start.6 = (f32[40,256]{1,0:T(8,128)S(1)}, f32[40,256]{1,0:T(8,128)S(1)}, u32[]{:S(2)}, u32[]{:S(2)}) collective-permute-start(f32[40,256]{1,0:T(8,128)S(1)} %fusion.2), channel_id=1, source_target_pairs={{0,4},{4,0},{8,12},{12,8},{16,20},{20,16},{24,28},{28,24},{1,5},{5... | collective-permute-start | bytes 122888 | tf_op jit(solution)/shard_map/ppermute | solution.py:168
  5.2 1.1 %fusion.3 = (bf16[8,64,256]{2,1,0:T(8,128)(2,1)S(1)}, bf16[8,64,256]{2,1,0:T(8,128)(2,1)S(1)}) fusion(bf16[16,64,256]{2,1,0:T(8,128)(2,1)} %bitcast.17), kind=kLoop, calls=%fused_computation.11 | loop fusion | bytes 1048576 | tf_op jit(solution)/shard_map/slice | solution.py:189
  6.3 1.6 %collective-permute-start.4 = (bf16[8,64,256]{2,1,0:T(8,128)(2,1)S(1)}, bf16[8,64,256]{2,1,0:T(8,128)(2,1)S(1)}, u32[]{:S(2)}, u32[]{:S(2)}) collective-permute-start(bf16[8,64,256]{2,1,0:T(8,128)(2,1)S(1)} %get-tuple-element.62), channel_id=1, source_target_pairs={{0,8},{8,16},{16,24},{24,28},{28,20},{20,12},{12,4},{4,0},{1,9},{9... | collective-permute-start | bytes 786440 | tf_op jit(solution)/shard_map/ppermute | solution.py:186
  7.9 0.4 collective-permute-start.5
  8.4 1.6 %collective-permute-start = (bf16[8,64,256]{2,1,0:T(8,128)(2,1)S(1)}, bf16[8,64,256]{2,1,0:T(8,128)(2,1)S(1)}, u32[]{:S(2)}, u32[]{:S(2)}) collective-permute-start(bf16[8,64,256]{2,1,0:T(8,128)(2,1)S(1)} %get-tuple-element.63), channel_id=1, source_target_pairs={{0,8},{8,16},{16,24},{24,28},{28,20},{20,12},{12,4},{4,0},{1,9},{9... | collective-permute-start | bytes 786440 | tf_op jit(solution)/shard_map/ppermute | solution.py:186
  10.0 0.4 collective-permute-start.9
  10.4 2.2 %copy-done.1 = bf16[128,64,256]{2,1,0:T(8,128)(2,1)S(1)} copy-done((bf16[128,64,256]{2,1,0:T(8,128)(2,1)S(1)}, bf16[128,64,256]{2,1,0:T(8,128)(2,1)}, u32[]{:S(2)}) %copy-start.1) | copy-done | bytes 4194328
  12.6 1.0 %copy-done.3 = bf16[16,256,64]{1,2,0:T(8,128)(2,1)S(1)} copy-done((bf16[16,256,64]{1,2,0:T(8,128)(2,1)S(1)}, bf16[16,256,64]{1,2,0:T(8,128)(2,1)}, u32[]{:S(2)}) %copy-start.3) | copy-done | bytes 524312
  13.6 0.7 %copy-done.5 = s32[128]{0:T(128)S(1)} copy-done((s32[128]{0:T(128)S(1)}, s32[128]{0:T(128)}, u32[]{:S(2)}) %copy-start.5) | copy-done | bytes 536
  14.3 0.9 %shard_map.95.refs_5_ = f32[256,256]{1,0:T(8,128)S(1)} custom-call(s32[128]{0:T(128)S(1)} %copy-done.5, s32[1]{0:T(128)} %copy.10.current, bf16[16,64,256]{2,1,0:T(8,128)(2,1)S(1)} %bitcast.18, bf16[128,64,256]{2,1,0:T(8,128)(2,1)S(1)} %copy-done.1), custom_call_target="tpu_custom_call" | custom-call | flops 134217728 | bytes 1048576 | tf_op jit(solution)/shard_map/pallas_call | solution.py:79
  15.2 0.0 collective-permute-done.6
  15.2 0.4 collective-permute-done.4.refs_2_
  15.6 1.6 %collective-permute-done.5.refs_3_ = bf16[8,64,256]{2,1,0:T(8,128)(2,1)S(1)} collective-permute-done((bf16[8,64,256]{2,1,0:T(8,128)(2,1)S(1)}, bf16[8,64,256]{2,1,0:T(8,128)(2,1)S(1)}, u32[]{:S(2)}, u32[]{:S(2)}) %collective-permute-start.5) | collective-permute-done | bytes 262176 | tf_op jit(solution)/shard_map/ppermute | solution.py:186
  17.2 1.6 %collective-permute-start.7 = (bf16[8,64,256]{2,1,0:T(8,128)(2,1)S(1)}, bf16[8,64,256]{2,1,0:T(8,128)(2,1)S(1)}, u32[]{:S(2)}, u32[]{:S(2)}) collective-permute-start(bf16[8,64,256]{2,1,0:T(8,128)(2,1)S(1)} %collective-permute-done.4.refs_2_), channel_id=1, source_target_pairs={{0,8},{8,16},{16,24},{24,28},{28,20},{20,12},{12,4},{4,0},{1,9},{9... | collective-permute-start | bytes 786440 | tf_op jit(solution)/shard_map/ppermute | solution.py:186
  18.8 0.4 collective-permute-start.8
  19.2 2.0 %collective-permute-done.refs_0_ = bf16[8,64,256]{2,1,0:T(8,128)(2,1)S(1)} collective-permute-done((bf16[8,64,256]{2,1,0:T(8,128)(2,1)S(1)}, bf16[8,64,256]{2,1,0:T(8,128)(2,1)S(1)}, u32[]{:S(2)}, u32[]{:S(2)}) %collective-permute-start) | collective-permute-done | bytes 262176 | tf_op jit(solution)/shard_map/ppermute | solution.py:186
  21.2 1.6 %collective-permute-start.1 = (bf16[8,64,256]{2,1,0:T(8,128)(2,1)S(1)}, bf16[8,64,256]{2,1,0:T(8,128)(2,1)S(1)}, u32[]{:S(2)}, u32[]{:S(2)}) collective-permute-start(bf16[8,64,256]{2,1,0:T(8,128)(2,1)S(1)} %collective-permute-done.refs_0_), channel_id=1, source_target_pairs={{0,8},{8,16},{16,24},{24,28},{28,20},{20,12},{12,4},{4,0},{1,9},{9... | collective-permute-start | bytes 786440 | tf_op jit(solution)/shard_map/ppermute | solution.py:186
  22.8 1.6 %collective-permute-start.10 = (f32[40,256]{1,0:T(8,128)S(1)}, f32[40,256]{1,0:T(8,128)S(1)}, u32[]{:S(2)}, u32[]{:S(2)}) collective-permute-start(f32[40,256]{1,0:T(8,128)S(1)} %fusion.1), channel_id=1, source_target_pairs={{0,8},{4,12},{8,0},{12,4},{16,24},{20,28},{24,16},{28,20},{1,9},{5... | collective-permute-start | bytes 122888 | tf_op jit(solution)/shard_map/ppermute | solution.py:168
  24.4 0.0 collective-permute-start.13
  24.4 1.0 %shard_map.96.refs_5_ = f32[256,256]{1,0:T(8,128)S(1)} custom-call(s32[128]{0:T(128)S(1)} %copy-done.5, s32[1]{0:T(128)} %copy.10.current, bf16[8,64,256]{2,1,0:T(8,128)(2,1)S(1)} %collective-permute-done.refs_0_, bf16[8,64,256]{2,1,0:T(8,128)(2,1)S(1)} %collective-permute-done.9.refs_1_, bf16[8,64,256]{2,1,0:T(8,128)(2,1)S(1)} %collective-permute-done.4.refs_2_, ...), custom_call_target="tpu_custom_call" | custom-call | flops 268435456 | bytes 2097152 | tf_op jit(solution)/shard_map/pallas_call | solution.py:79
  25.4 5.5 %collective-permute-done.10 = f32[40,256]{1,0:T(8,128)S(1)} collective-permute-done((f32[40,256]{1,0:T(8,128)S(1)}, f32[40,256]{1,0:T(8,128)S(1)}, u32[]{:S(2)}, u32[]{:S(2)}) %collective-permute-start.10) | collective-permute-done | bytes 40992 | tf_op jit(solution)/shard_map/ppermute | solution.py:168
  31.0 0.0 collective-permute-done.7.refs_2_
  31.0 2.5 %collective-permute-start.11 = (bf16[8,64,256]{2,1,0:T(8,128)(2,1)S(1)}, bf16[8,64,256]{2,1,0:T(8,128)(2,1)S(1)}, u32[]{:S(2)}, u32[]{:S(2)}) collective-permute-start(bf16[8,64,256]{2,1,0:T(8,128)(2,1)S(1)} %collective-permute-done.7.refs_2_), channel_id=1, source_target_pairs={{0,8},{8,16},{16,24},{24,28},{28,20},{20,12},{12,4},{4,0},{1,9},{9... | collective-permute-start | bytes 786440 | tf_op jit(solution)/shard_map/ppermute | solution.py:186
  33.5 2.0 %collective-permute-start.2 = (bf16[8,64,256]{2,1,0:T(8,128)(2,1)S(1)}, bf16[8,64,256]{2,1,0:T(8,128)(2,1)S(1)}, u32[]{:S(2)}, u32[]{:S(2)}) collective-permute-start(bf16[8,64,256]{2,1,0:T(8,128)(2,1)S(1)} %collective-permute-done.1.refs_0_), channel_id=1, source_target_pairs={{0,8},{8,16},{16,24},{24,28},{28,20},{20,12},{12,4},{4,0},{1,9},{9... | collective-permute-start | bytes 786440 | tf_op jit(solution)/shard_map/ppermute | solution.py:186
  35.5 2.6 %collective-permute-start.14 = (f32[40,256]{1,0:T(8,128)S(1)}, f32[40,256]{1,0:T(8,128)S(1)}, u32[]{:S(2)}, u32[]{:S(2)}) collective-permute-start(f32[40,256]{1,0:T(8,128)S(1)} %add.46), channel_id=1, source_target_pairs={{0,16},{4,20},{8,24},{12,28},{16,0},{20,4},{24,8},{28,12},{1,17},{... | collective-permute-start | bytes 122888 | tf_op jit(solution)/shard_map/ppermute | solution.py:168
  38.1 0.0 collective-permute-done.13.refs_1_
  38.1 0.0 collective-permute-start.16
  38.1 1.0 %shard_map.97.refs_5_ = f32[256,256]{1,0:T(8,128)S(1)} custom-call(s32[128]{0:T(128)S(1)} %copy-done.5, s32[1]{0:T(128)} %copy.10.current, bf16[8,64,256]{2,1,0:T(8,128)(2,1)S(1)} %collective-permute-done.1.refs_0_, bf16[8,64,256]{2,1,0:T(8,128)(2,1)S(1)} %collective-permute-done.13.refs_1_, bf16[8,64,256]{2,1,0:T(8,128)(2,1)S(1)} %collective-permute-done.7.refs_2_, ...), custom_call_target="tpu_custom_call" | custom-call | flops 268435456 | bytes 2097152 | tf_op jit(solution)/shard_map/pallas_call | solution.py:79
  39.2 0.0 copy-start.4
  39.2 5.5 %collective-permute-done.14 = f32[40,256]{1,0:T(8,128)S(1)} collective-permute-done((f32[40,256]{1,0:T(8,128)S(1)}, f32[40,256]{1,0:T(8,128)S(1)}, u32[]{:S(2)}, u32[]{:S(2)}) %collective-permute-start.14) | collective-permute-done | bytes 40992 | tf_op jit(solution)/shard_map/ppermute | solution.py:168
  44.7 2.5 %collective-permute-start.15 = (bf16[8,64,256]{2,1,0:T(8,128)(2,1)S(1)}, bf16[8,64,256]{2,1,0:T(8,128)(2,1)S(1)}, u32[]{:S(2)}, u32[]{:S(2)}) collective-permute-start(bf16[8,64,256]{2,1,0:T(8,128)(2,1)S(1)} %collective-permute-done.12.refs_3_), channel_id=1, source_target_pairs={{8,0},{16,8},{24,16},{28,24},{20,28},{12,20},{4,12},{0,4},{9,1},{1... | collective-permute-start | bytes 786440 | tf_op jit(solution)/shard_map/ppermute | solution.py:195
  47.2 1.6 %collective-permute-start.18 = (f32[40,256]{1,0:T(8,128)S(1)}, f32[40,256]{1,0:T(8,128)S(1)}, u32[]{:S(2)}, u32[]{:S(2)}) collective-permute-start(f32[40,256]{1,0:T(8,128)S(1)} %add.47.s0), channel_id=1, source_target_pairs={{0,2},{1,3},{2,0},{3,1},{4,6},{5,7},{6,4},{7,5},{8,10},{9,11},{10,... | collective-permute-start | bytes 122888 | tf_op jit(solution)/shard_map/ppermute | solution.py:168
  48.8 1.1 %collective-permute-start.19 = (f32[40,256]{1,0:T(8,128)S(1)}, f32[40,256]{1,0:T(8,128)S(1)}, u32[]{:S(2)}, u32[]{:S(2)}) collective-permute-start(f32[40,256]{1,0:T(8,128)S(1)} %collective-permute-done.17.s1), channel_id=1, source_target_pairs={{0,2},{1,3},{2,0},{3,1},{4,6},{5,7},{6,4},{7,5},{8,10},{9,11},{10,... | collective-permute-start | bytes 122888 | tf_op jit(solution)/shard_map/ppermute | solution.py:168
  49.9 1.1 %shard_map.98 = (f32[256,256]{1,0:T(8,128)S(1)}, bf16[2,512,256]{2,1,0:T(8,128)(2,1)S(1)}) custom-call(s32[128]{0:T(128)S(1)} %copy-done.5, s32[1]{0:T(128)} %copy.10.current, bf16[8,64,256]{2,1,0:T(8,128)(2,1)S(1)} %collective-permute-done.2.refs_0_, bf16[8,64,256]{2,1,0:T(8,128)(2,1)S(1)} %collective-permute-done.16.refs_1_, ...), custom_call_target="tpu_custom_call" | custom-call | flops 268435456 | bytes 2097152 | tf_op jit(solution)/shard_map/pallas_call | solution.py:79
  51.1 0.2 collective-permute-done.18.s2
  51.3 1.5 %collective-permute-done.19.s3 = f32[40,256]{1,0:T(8,128)S(1)} collective-permute-done((f32[40,256]{1,0:T(8,128)S(1)}, f32[40,256]{1,0:T(8,128)S(1)}, u32[]{:S(2)}, u32[]{:S(2)}) %collective-permute-start.19) | collective-permute-done | bytes 40992 | tf_op jit(solution)/shard_map/ppermute | solution.py:168
  52.8 0.8 %collective-permute-done.3.panel_a = bf16[8,64,256]{2,1,0:T(8,128)(2,1)S(1)} collective-permute-done((bf16[8,64,256]{2,1,0:T(8,128)(2,1)S(1)}, bf16[8,64,256]{2,1,0:T(8,128)(2,1)S(1)}, u32[]{:S(2)}, u32[]{:S(2)}) %collective-permute-start.3) | collective-permute-done | bytes 262176 | tf_op jit(solution)/shard_map/ppermute | solution.py:193
  53.6 0.3 shard_map.99
  53.9 0.1 collective-permute-start.20
  54.0 1.5 %collective-permute-done.20.mate = f32[256,256]{1,0:T(8,128)S(1)} collective-permute-done((f32[256,256]{1,0:T(8,128)S(1)}, f32[256,256]{1,0:T(8,128)S(1)}, u32[]{:S(2)}, u32[]{:S(2)}) %collective-permute-start.20) | collective-permute-done | bytes 262176 | tf_op jit(solution)/shard_map/ppermute | solution.py:168
  55.6 1.6 %collective-permute-start.21 = (f32[128,256]{1,0:T(8,128)S(1)}, f32[128,256]{1,0:T(8,128)S(1)}, u32[]{:S(2)}, u32[]{:S(2)}) collective-permute-start(f32[128,256]{1,0:T(8,128)S(1)} %slice_add_fusion), channel_id=1, source_target_pairs={{0,2},{1,3},{2,0},{3,1},{4,6},{5,7},{6,4},{7,5},{8,10},{9,11},{10,... | collective-permute-start | bytes 393224 | tf_op jit(solution)/shard_map/ppermute | solution.py:168
  57.2 1.4 %collective-permute-start.23 = (f32[128,256]{1,0:T(8,128)S(1)}, f32[128,256]{1,0:T(8,128)S(1)}, u32[]{:S(2)}, u32[]{:S(2)}) collective-permute-start(f32[128,256]{1,0:T(8,128)S(1)} %pad_maximum_fusion.1), channel_id=1, source_target_pairs={{0,4},{4,0},{8,12},{12,8},{16,20},{20,16},{24,28},{28,24},{1,5},{5... | collective-permute-start | bytes 393224 | tf_op jit(solution)/shard_map/ppermute | solution.py:168
  58.6 2.6 %collective-permute-done.21.far = f32[128,256]{1,0:T(8,128)S(1)} collective-permute-done((f32[128,256]{1,0:T(8,128)S(1)}, f32[128,256]{1,0:T(8,128)S(1)}, u32[]{:S(2)}, u32[]{:S(2)}) %collective-permute-start.21) | collective-permute-done | bytes 131104 | tf_op jit(solution)/shard_map/ppermute | solution.py:168
  61.2 0.6 shard_map.100
  61.8 0.7 %collective-permute-done.23.given = f32[128,256]{1,0:T(8,128)S(1)} collective-permute-done((f32[128,256]{1,0:T(8,128)S(1)}, f32[128,256]{1,0:T(8,128)S(1)}, u32[]{:S(2)}, u32[]{:S(2)}) %collective-permute-start.23) | collective-permute-done | bytes 131104 | tf_op jit(solution)/shard_map/ppermute | solution.py:168
  62.5 1.0 %shard_map.101 = (f32[64,256]{1,0:T(8,128)}, f32[1,256]{1,0:T(1,128)}) custom-call(f32[128,256]{1,0:T(8,128)S(1)} %get-tuple-element.49.mine, f32[128,256]{1,0:T(8,128)S(1)} %get-tuple-element.50.other, f32[256,256]{1,0:T(8,128)S(1)} %collective-permute-done.20.mate, f32[128,256]{1,0:T(8,128)S(1)} %collective-permute-done.21.far, ...), custom_call_target="tpu_custom_call" | custom-call | flops 200000000 | bytes 1000000 | tf_op jit(solution)/shard_map/pallas_call | solution.py:230
  (35 shorter events, 0.2 us)
Async XLA Ops:
  0.6 1.6 %copy-start = (f32[16,256,32]{1,2,0:T(8,128)S(1)}, f32[16,256,32]{1,2,0:T(8,128)}, u32[]{:S(2)}) copy-start(f32[16,256,32]{1,2,0:T(8,128)} %param.12) | copy-start | bytes 1572868
  2.2 13.0 %collective-permute-start.6 = (f32[40,256]{1,0:T(8,128)S(1)}, f32[40,256]{1,0:T(8,128)S(1)}, u32[]{:S(2)}, u32[]{:S(2)}) collective-permute-start(f32[40,256]{1,0:T(8,128)S(1)} %fusion.2), channel_id=1, source_target_pairs={{0,4},{4,0},{8,12},{12,8},{16,20},{20,16},{24,28},{28,24},{1,5},{5... | collective-permute-start | bytes 122888 | tf_op jit(solution)/shard_map/ppermute | solution.py:168
  6.3 9.3 %collective-permute-start.4 = (bf16[8,64,256]{2,1,0:T(8,128)(2,1)S(1)}, bf16[8,64,256]{2,1,0:T(8,128)(2,1)S(1)}, u32[]{:S(2)}, u32[]{:S(2)}) collective-permute-start(bf16[8,64,256]{2,1,0:T(8,128)(2,1)S(1)} %get-tuple-element.62), channel_id=1, source_target_pairs={{0,8},{8,16},{16,24},{24,28},{28,20},{20,12},{12,4},{4,0},{1,9},{9... | collective-permute-start | bytes 786440 | tf_op jit(solution)/shard_map/ppermute | solution.py:186
  7.9 9.2 %collective-permute-start.5 = (bf16[8,64,256]{2,1,0:T(8,128)(2,1)S(1)}, bf16[8,64,256]{2,1,0:T(8,128)(2,1)S(1)}, u32[]{:S(2)}, u32[]{:S(2)}) collective-permute-start(bf16[8,64,256]{2,1,0:T(8,128)(2,1)S(1)} %get-tuple-element.62), channel_id=1, source_target_pairs={{8,0},{16,8},{24,16},{28,24},{20,28},{12,20},{4,12},{0,4},{9,1},{1... | collective-permute-start | bytes 786440 | tf_op jit(solution)/shard_map/ppermute | solution.py:186
  8.4 12.8 %collective-permute-start = (bf16[8,64,256]{2,1,0:T(8,128)(2,1)S(1)}, bf16[8,64,256]{2,1,0:T(8,128)(2,1)S(1)}, u32[]{:S(2)}, u32[]{:S(2)}) collective-permute-start(bf16[8,64,256]{2,1,0:T(8,128)(2,1)S(1)} %get-tuple-element.63), channel_id=1, source_target_pairs={{0,8},{8,16},{16,24},{24,28},{28,20},{20,12},{12,4},{4,0},{1,9},{9... | collective-permute-start | bytes 786440 | tf_op jit(solution)/shard_map/ppermute | solution.py:186
  10.0 14.4 %collective-permute-start.9 = (bf16[8,64,256]{2,1,0:T(8,128)(2,1)S(1)}, bf16[8,64,256]{2,1,0:T(8,128)(2,1)S(1)}, u32[]{:S(2)}, u32[]{:S(2)}) collective-permute-start(bf16[8,64,256]{2,1,0:T(8,128)(2,1)S(1)} %get-tuple-element.63), channel_id=1, source_target_pairs={{8,0},{16,8},{24,16},{28,24},{20,28},{12,20},{4,12},{0,4},{9,1},{1... | collective-permute-start | bytes 786440 | tf_op jit(solution)/shard_map/ppermute | solution.py:186
  10.4 2.2 %copy-start.1 = (bf16[128,64,256]{2,1,0:T(8,128)(2,1)S(1)}, bf16[128,64,256]{2,1,0:T(8,128)(2,1)}, u32[]{:S(2)}) copy-start(bf16[128,64,256]{2,1,0:T(8,128)(2,1)} %refs_4_.5) | copy-start | bytes 12582916
  12.6 1.0 %copy-start.3 = (bf16[16,256,64]{1,2,0:T(8,128)(2,1)S(1)}, bf16[16,256,64]{1,2,0:T(8,128)(2,1)}, u32[]{:S(2)}) copy-start(bf16[16,256,64]{1,2,0:T(8,128)(2,1)} %param.10) | copy-start | bytes 1572868
  13.6 0.7 %copy-start.5 = (s32[128]{0:T(128)S(1)}, s32[128]{0:T(128)}, u32[]{:S(2)}) copy-start(s32[128]{0:T(128)} %slot_block.7) | copy-start | bytes 1540
  14.3 10.1 %copy-start.2 = (bf16[128,64,256]{2,1,0:T(8,128)(2,1)S(1)}, bf16[128,64,256]{2,1,0:T(8,128)(2,1)}, u32[]{:S(2)}) copy-start(bf16[128,64,256]{2,1,0:T(8,128)(2,1)} %refs_4_.5) | copy-start | bytes 12582916
  17.2 13.8 %collective-permute-start.7 = (bf16[8,64,256]{2,1,0:T(8,128)(2,1)S(1)}, bf16[8,64,256]{2,1,0:T(8,128)(2,1)S(1)}, u32[]{:S(2)}, u32[]{:S(2)}) collective-permute-start(bf16[8,64,256]{2,1,0:T(8,128)(2,1)S(1)} %collective-permute-done.4.refs_2_), channel_id=1, source_target_pairs={{0,8},{8,16},{16,24},{24,28},{28,20},{20,12},{12,4},{4,0},{1,9},{9... | collective-permute-start | bytes 786440 | tf_op jit(solution)/shard_map/ppermute | solution.py:186
  18.8 12.2 %collective-permute-start.8 = (bf16[8,64,256]{2,1,0:T(8,128)(2,1)S(1)}, bf16[8,64,256]{2,1,0:T(8,128)(2,1)S(1)}, u32[]{:S(2)}, u32[]{:S(2)}) collective-permute-start(bf16[8,64,256]{2,1,0:T(8,128)(2,1)S(1)} %collective-permute-done.5.refs_3_), channel_id=1, source_target_pairs={{8,0},{16,8},{24,16},{28,24},{20,28},{12,20},{4,12},{0,4},{9,1},{1... | collective-permute-start | bytes 786440 | tf_op jit(solution)/shard_map/ppermute | solution.py:186
  21.2 12.3 %collective-permute-start.1 = (bf16[8,64,256]{2,1,0:T(8,128)(2,1)S(1)}, bf16[8,64,256]{2,1,0:T(8,128)(2,1)S(1)}, u32[]{:S(2)}, u32[]{:S(2)}) collective-permute-start(bf16[8,64,256]{2,1,0:T(8,128)(2,1)S(1)} %collective-permute-done.refs_0_), channel_id=1, source_target_pairs={{0,8},{8,16},{16,24},{24,28},{28,20},{20,12},{12,4},{4,0},{1,9},{9... | collective-permute-start | bytes 786440 | tf_op jit(solution)/shard_map/ppermute | solution.py:186
  22.8 8.2 %collective-permute-start.10 = (f32[40,256]{1,0:T(8,128)S(1)}, f32[40,256]{1,0:T(8,128)S(1)}, u32[]{:S(2)}, u32[]{:S(2)}) collective-permute-start(f32[40,256]{1,0:T(8,128)S(1)} %fusion.1), channel_id=1, source_target_pairs={{0,8},{4,12},{8,0},{12,4},{16,24},{20,28},{24,16},{28,20},{1,9},{5... | collective-permute-start | bytes 122888 | tf_op jit(solution)/shard_map/ppermute | solution.py:168
  24.4 13.8 %collective-permute-start.13 = (bf16[8,64,256]{2,1,0:T(8,128)(2,1)S(1)}, bf16[8,64,256]{2,1,0:T(8,128)(2,1)S(1)}, u32[]{:S(2)}, u32[]{:S(2)}) collective-permute-start(bf16[8,64,256]{2,1,0:T(8,128)(2,1)S(1)} %collective-permute-done.9.refs_1_), channel_id=1, source_target_pairs={{8,0},{16,8},{24,16},{28,24},{20,28},{12,20},{4,12},{0,4},{9,1},{1... | collective-permute-start | bytes 786440 | tf_op jit(solution)/shard_map/ppermute | solution.py:186
  31.0 13.7 %collective-permute-start.11 = (bf16[8,64,256]{2,1,0:T(8,128)(2,1)S(1)}, bf16[8,64,256]{2,1,0:T(8,128)(2,1)S(1)}, u32[]{:S(2)}, u32[]{:S(2)}) collective-permute-start(bf16[8,64,256]{2,1,0:T(8,128)(2,1)S(1)} %collective-permute-done.7.refs_2_), channel_id=1, source_target_pairs={{0,8},{8,16},{16,24},{24,28},{28,20},{20,12},{12,4},{4,0},{1,9},{9... | collective-permute-start | bytes 786440 | tf_op jit(solution)/shard_map/ppermute | solution.py:186
  33.5 11.2 %collective-permute-start.12 = (bf16[8,64,256]{2,1,0:T(8,128)(2,1)S(1)}, bf16[8,64,256]{2,1,0:T(8,128)(2,1)S(1)}, u32[]{:S(2)}, u32[]{:S(2)}) collective-permute-start(bf16[8,64,256]{2,1,0:T(8,128)(2,1)S(1)} %collective-permute-done.8.refs_3_), channel_id=1, source_target_pairs={{8,0},{16,8},{24,16},{28,24},{20,28},{12,20},{4,12},{0,4},{9,1},{1... | collective-permute-start | bytes 786440 | tf_op jit(solution)/shard_map/ppermute | solution.py:186
  33.5 13.7 %collective-permute-start.2 = (bf16[8,64,256]{2,1,0:T(8,128)(2,1)S(1)}, bf16[8,64,256]{2,1,0:T(8,128)(2,1)S(1)}, u32[]{:S(2)}, u32[]{:S(2)}) collective-permute-start(bf16[8,64,256]{2,1,0:T(8,128)(2,1)S(1)} %collective-permute-done.1.refs_0_), channel_id=1, source_target_pairs={{0,8},{8,16},{16,24},{24,28},{28,20},{20,12},{12,4},{4,0},{1,9},{9... | collective-permute-start | bytes 786440 | tf_op jit(solution)/shard_map/ppermute | solution.py:186
  35.5 9.1 %collective-permute-start.14 = (f32[40,256]{1,0:T(8,128)S(1)}, f32[40,256]{1,0:T(8,128)S(1)}, u32[]{:S(2)}, u32[]{:S(2)}) collective-permute-start(f32[40,256]{1,0:T(8,128)S(1)} %add.46), channel_id=1, source_target_pairs={{0,16},{4,20},{8,24},{12,28},{16,0},{20,4},{24,8},{28,12},{1,17},{... | collective-permute-start | bytes 122888 | tf_op jit(solution)/shard_map/ppermute | solution.py:168
  38.1 11.8 %collective-permute-start.16 = (bf16[8,64,256]{2,1,0:T(8,128)(2,1)S(1)}, bf16[8,64,256]{2,1,0:T(8,128)(2,1)S(1)}, u32[]{:S(2)}, u32[]{:S(2)}) collective-permute-start(bf16[8,64,256]{2,1,0:T(8,128)(2,1)S(1)} %collective-permute-done.13.refs_1_), channel_id=1, source_target_pairs={{8,0},{16,8},{24,16},{28,24},{20,28},{12,20},{4,12},{0,4},{9,1},{1... | collective-permute-start | bytes 786440 | tf_op jit(solution)/shard_map/ppermute | solution.py:186
  39.2 22.0 %copy-start.4 = (f32[256,32]{0,1:T(8,128)S(1)}, f32[256,32]{0,1:T(8,128)}, u32[]{:S(2)}) copy-start(f32[256,32]{0,1:T(8,128)} %param.13) | copy-start | bytes 98308
  44.6 17.9 %copy-start.6 = (f32[256]{0:T(256)S(1)}, f32[256]{0:T(256)}, u32[]{:S(2)}) copy-start(f32[256]{0:T(256)} %param.15) | copy-start | bytes 3076
  44.7 8.1 %collective-permute-start.15 = (bf16[8,64,256]{2,1,0:T(8,128)(2,1)S(1)}, bf16[8,64,256]{2,1,0:T(8,128)(2,1)S(1)}, u32[]{:S(2)}, u32[]{:S(2)}) collective-permute-start(bf16[8,64,256]{2,1,0:T(8,128)(2,1)S(1)} %collective-permute-done.12.refs_3_), channel_id=1, source_target_pairs={{8,0},{16,8},{24,16},{28,24},{20,28},{12,20},{4,12},{0,4},{9,1},{1... | collective-permute-start | bytes 786440 | tf_op jit(solution)/shard_map/ppermute | solution.py:195
  47.2 6.4 %collective-permute-start.3 = (bf16[8,64,256]{2,1,0:T(8,128)(2,1)S(1)}, bf16[8,64,256]{2,1,0:T(8,128)(2,1)S(1)}, u32[]{:S(2)}, u32[]{:S(2)}) collective-permute-start(bf16[8,64,256]{2,1,0:T(8,128)(2,1)S(1)} %collective-permute-done.2.refs_0_), channel_id=1, source_target_pairs={{0,8},{8,16},{16,24},{24,28},{28,20},{20,12},{12,4},{4,0},{1,9},{9... | collective-permute-start | bytes 786440 | tf_op jit(solution)/shard_map/ppermute | solution.py:193
  47.2 1.6 %collective-permute-start.17 = (f32[40,256]{1,0:T(8,128)S(1)}, f32[40,256]{1,0:T(8,128)S(1)}, u32[]{:S(2)}, u32[]{:S(2)}) collective-permute-start(f32[40,256]{1,0:T(8,128)S(1)} %add.47.s0), channel_id=1, source_target_pairs={{0,1},{1,0},{2,3},{3,2},{4,5},{5,4},{6,7},{7,6},{8,9},{9,8},{10,11... | collective-permute-start | bytes 122888 | tf_op jit(solution)/shard_map/ppermute | solution.py:168
  47.2 4.1 %collective-permute-start.18 = (f32[40,256]{1,0:T(8,128)S(1)}, f32[40,256]{1,0:T(8,128)S(1)}, u32[]{:S(2)}, u32[]{:S(2)}) collective-permute-start(f32[40,256]{1,0:T(8,128)S(1)} %add.47.s0), channel_id=1, source_target_pairs={{0,2},{1,3},{2,0},{3,1},{4,6},{5,7},{6,4},{7,5},{8,10},{9,11},{10,... | collective-permute-start | bytes 122888 | tf_op jit(solution)/shard_map/ppermute | solution.py:168
  48.8 4.0 %collective-permute-start.19 = (f32[40,256]{1,0:T(8,128)S(1)}, f32[40,256]{1,0:T(8,128)S(1)}, u32[]{:S(2)}, u32[]{:S(2)}) collective-permute-start(f32[40,256]{1,0:T(8,128)S(1)} %collective-permute-done.17.s1), channel_id=1, source_target_pairs={{0,2},{1,3},{2,0},{3,1},{4,6},{5,7},{6,4},{7,5},{8,10},{9,11},{10,... | collective-permute-start | bytes 122888 | tf_op jit(solution)/shard_map/ppermute | solution.py:168
  53.9 1.6 %collective-permute-start.20 = (f32[256,256]{1,0:T(8,128)S(1)}, f32[256,256]{1,0:T(8,128)S(1)}, u32[]{:S(2)}, u32[]{:S(2)}) collective-permute-start(f32[256,256]{1,0:T(8,128)S(1)} %pad_maximum_fusion), channel_id=1, source_target_pairs={{0,1},{1,0},{2,3},{3,2},{4,5},{5,4},{6,7},{7,6},{8,9},{9,8},{10,11... | collective-permute-start | bytes 786440 | tf_op jit(solution)/shard_map/ppermute | solution.py:168
  55.6 5.6 %collective-permute-start.21 = (f32[128,256]{1,0:T(8,128)S(1)}, f32[128,256]{1,0:T(8,128)S(1)}, u32[]{:S(2)}, u32[]{:S(2)}) collective-permute-start(f32[128,256]{1,0:T(8,128)S(1)} %slice_add_fusion), channel_id=1, source_target_pairs={{0,2},{1,3},{2,0},{3,1},{4,6},{5,7},{6,4},{7,5},{8,10},{9,11},{10,... | collective-permute-start | bytes 393224 | tf_op jit(solution)/shard_map/ppermute | solution.py:168
  57.2 5.3 %collective-permute-start.23 = (f32[128,256]{1,0:T(8,128)S(1)}, f32[128,256]{1,0:T(8,128)S(1)}, u32[]{:S(2)}, u32[]{:S(2)}) collective-permute-start(f32[128,256]{1,0:T(8,128)S(1)} %pad_maximum_fusion.1), channel_id=1, source_target_pairs={{0,4},{4,0},{8,12},{12,8},{16,20},{20,16},{24,28},{28,24},{1,5},{5... | collective-permute-start | bytes 393224 | tf_op jit(solution)/shard_map/ppermute | solution.py:168
  61.2 1.4 %collective-permute-start.22 = (f32[128,256]{1,0:T(8,128)S(1)}, f32[128,256]{1,0:T(8,128)S(1)}, u32[]{:S(2)}, u32[]{:S(2)}) collective-permute-start(f32[128,256]{1,0:T(8,128)S(1)} %collective-permute-done.21.far), channel_id=1, source_target_pairs={{0,1},{1,0},{2,3},{3,2},{4,5},{5,4},{6,7},{7,6},{8,9},{9,8},{10,11... | collective-permute-start | bytes 393224 | tf_op jit(solution)/shard_map/ppermute | solution.py:168

commit v6 on v5

--- a/solution.py
+++ b/solution.py
@@ -201,7 +201,7 @@
             sources += [(-4, 0, held), (4, half, held)]
             total, ahead = add(add_ahead_kernel, sources, slot_block, block_index, panels, earlier_rows, [total])
         if k < 3:
-            spread = spread + flip(spread, "cand", 2 * k, 8)
+            spread = spread + flip(spread, "cand", 8 >> k, 8)
         early, late = next_early, next_late
     spreads = [spread, flip(spread, "obs", 1, 4)]
     spreads += [flip(spreads[0], "obs", 2, 4), flip(spreads[1], "obs", 2, 4)]

time: 63.8 us -> 63.4 us (level)
  waiting for transfers between devices: 22.3 us -> 21.1 us
  starting transfers between devices: 27.7 us -> 28.5 us
    ppermute x10, waiting for transfers between devices: 17.6 us -> 16.4 us  [flip(): return lax.ppermute(value, axis, [(i, i ^ bits) for i in range(size)])]
    ppermute x6, starting transfers between devices: 1.36 us -> 2.39 us  [onward(): lax.ppermute(pair[1], 'cand', BACK)]
where the time goes in v6:
time: 63.4 us; the launch traced here: 63.1 us
  starting transfers between devices  28.5 us (45%)
  waiting for transfers between devices  21.1 us (33%)
  Pallas kernels  5.96 us (9%)
  local copies, waits for them, and re-layouts  5.79 us (9%)
  between operations  1.6 us (3%)
    ppermute x10, waiting for transfers between devices, flip(): return lax.ppermute(value, axis, [(i, i ^ bits) for i in range(size)])  16.4 us
    ppermute x10, starting transfers between devices, flip(): return lax.ppermute(value, axis, [(i, i ^ bits) for i in range(size)])  12.9 us
    ppermute x6, starting transfers between devices, onward(): lax.ppermute(pair[0], 'cand', RING)  10.3 us
    pallas_call x4, Pallas kernels, add(): pl.pallas_call(functools.partial(kernel, sources), out_shape=outs, in_spe...  4.06 us
    unnamed x14, local copies, waits for them, and re-layouts  3.91 us
    ppermute x1, starting transfers between devices, on_ring(): next_late = onward(late) if k < 3 else lax.ppermute(late[1], 'cand', BACK)  2.97 us
    ppermute x6, starting transfers between devices, onward(): lax.ppermute(pair[1], 'cand', BACK)  2.39 us
    ppermute x6, waiting for transfers between devices, onward(): lax.ppermute(pair[0], 'cand', RING)  2.37 us
  transfers between devices with their start and end apart: 24, of which 11 were waited for; matrix products, arithmetic and copies ran while one was open for 2% of the time, Pallas kernels for 7%

profile of v6, /device:TPU:0, one launch (start us, length us, event | category | flops | bytes accessed | tf_op | source)
XLA Modules:
  0.0 63.1 jit_solution(2188940881052481685)
XLA Ops:
  0.6 0.0 copy-start
  1.4 0.8 %dynamic-slice_bitcast_fusion.1 = (f32[32,256]{1,0:T(8,128)S(1)}, f32[32,256]{1,0:T(8,128)S(1)}) fusion(f32[16,64,256]{2,1,0:T(8,128)} %param.14, s32[]{:T(128)S(6)} %select_n.52, s32[]{:T(128)S(6)} %select_n.54, s32[]{:T(128)S(6)} %select_n.59), kind=kLoop, calls=%fused_computation.9 | loop fusion | bytes 131084 | tf_op jit(solution)/shard_map/squeeze | solution.py:177
  2.2 3.0 %collective-permute-start.6 = (f32[40,256]{1,0:T(8,128)S(1)}, f32[40,256]{1,0:T(8,128)S(1)}, u32[]{:S(2)}, u32[]{:S(2)}) collective-permute-start(f32[40,256]{1,0:T(8,128)S(1)} %fusion.2), channel_id=1, source_target_pairs={{0,4},{4,0},{8,12},{12,8},{16,20},{20,16},{24,28},{28,24},{1,5},{5... | collective-permute-start | bytes 122888 | tf_op jit(solution)/shard_map/ppermute | solution.py:168
  5.2 1.1 %fusion.3 = (bf16[8,64,256]{2,1,0:T(8,128)(2,1)S(1)}, bf16[8,64,256]{2,1,0:T(8,128)(2,1)S(1)}) fusion(bf16[16,64,256]{2,1,0:T(8,128)(2,1)} %bitcast.17), kind=kLoop, calls=%fused_computation.11 | loop fusion | bytes 1048576 | tf_op jit(solution)/shard_map/slice | solution.py:189
  6.3 1.6 %collective-permute-start.4 = (bf16[8,64,256]{2,1,0:T(8,128)(2,1)S(1)}, bf16[8,64,256]{2,1,0:T(8,128)(2,1)S(1)}, u32[]{:S(2)}, u32[]{:S(2)}) collective-permute-start(bf16[8,64,256]{2,1,0:T(8,128)(2,1)S(1)} %get-tuple-element.62), channel_id=1, source_target_pairs={{0,8},{8,16},{16,24},{24,28},{28,20},{20,12},{12,4},{4,0},{1,9},{9... | collective-permute-start | bytes 786440 | tf_op jit(solution)/shard_map/ppermute | solution.py:186
  7.9 0.4 collective-permute-start.5
  8.4 1.6 %collective-permute-start = (bf16[8,64,256]{2,1,0:T(8,128)(2,1)S(1)}, bf16[8,64,256]{2,1,0:T(8,128)(2,1)S(1)}, u32[]{:S(2)}, u32[]{:S(2)}) collective-permute-start(bf16[8,64,256]{2,1,0:T(8,128)(2,1)S(1)} %get-tuple-element.63), channel_id=1, source_target_pairs={{0,8},{8,16},{16,24},{24,28},{28,20},{20,12},{12,4},{4,0},{1,9},{9... | collective-permute-start | bytes 786440 | tf_op jit(solution)/shard_map/ppermute | solution.py:186
  10.0 0.4 collective-permute-start.9
  10.4 2.2 %copy-done.1 = bf16[128,64,256]{2,1,0:T(8,128)(2,1)S(1)} copy-done((bf16[128,64,256]{2,1,0:T(8,128)(2,1)S(1)}, bf16[128,64,256]{2,1,0:T(8,128)(2,1)}, u32[]{:S(2)}) %copy-start.1) | copy-done | bytes 4194328
  12.6 1.0 %copy-done.3 = bf16[16,256,64]{1,2,0:T(8,128)(2,1)S(1)} copy-done((bf16[16,256,64]{1,2,0:T(8,128)(2,1)S(1)}, bf16[16,256,64]{1,2,0:T(8,128)(2,1)}, u32[]{:S(2)}) %copy-start.3) | copy-done | bytes 524312
  13.6 0.7 %copy-done.5 = s32[128]{0:T(128)S(1)} copy-done((s32[128]{0:T(128)S(1)}, s32[128]{0:T(128)}, u32[]{:S(2)}) %copy-start.5) | copy-done | bytes 536
  14.3 0.9 %shard_map.95.refs_5_ = f32[256,256]{1,0:T(8,128)S(1)} custom-call(s32[128]{0:T(128)S(1)} %copy-done.5, s32[1]{0:T(128)} %copy.10.current, bf16[16,64,256]{2,1,0:T(8,128)(2,1)S(1)} %bitcast.18, bf16[128,64,256]{2,1,0:T(8,128)(2,1)S(1)} %copy-done.1), custom_call_target="tpu_custom_call" | custom-call | flops 134217728 | bytes 1048576 | tf_op jit(solution)/shard_map/pallas_call | solution.py:79
  15.2 0.0 collective-permute-done.6
  15.2 0.4 collective-permute-done.4.refs_2_
  15.6 1.6 %collective-permute-done.5.refs_3_ = bf16[8,64,256]{2,1,0:T(8,128)(2,1)S(1)} collective-permute-done((bf16[8,64,256]{2,1,0:T(8,128)(2,1)S(1)}, bf16[8,64,256]{2,1,0:T(8,128)(2,1)S(1)}, u32[]{:S(2)}, u32[]{:S(2)}) %collective-permute-start.5) | collective-permute-done | bytes 262176 | tf_op jit(solution)/shard_map/ppermute | solution.py:186
  17.2 1.6 %collective-permute-start.7 = (bf16[8,64,256]{2,1,0:T(8,128)(2,1)S(1)}, bf16[8,64,256]{2,1,0:T(8,128)(2,1)S(1)}, u32[]{:S(2)}, u32[]{:S(2)}) collective-permute-start(bf16[8,64,256]{2,1,0:T(8,128)(2,1)S(1)} %collective-permute-done.4.refs_2_), channel_id=1, source_target_pairs={{0,8},{8,16},{16,24},{24,28},{28,20},{20,12},{12,4},{4,0},{1,9},{9... | collective-permute-start | bytes 786440 | tf_op jit(solution)/shard_map/ppermute | solution.py:186
  18.8 0.4 collective-permute-start.8
  19.2 2.0 %collective-permute-done.refs_0_ = bf16[8,64,256]{2,1,0:T(8,128)(2,1)S(1)} collective-permute-done((bf16[8,64,256]{2,1,0:T(8,128)(2,1)S(1)}, bf16[8,64,256]{2,1,0:T(8,128)(2,1)S(1)}, u32[]{:S(2)}, u32[]{:S(2)}) %collective-permute-start) | collective-permute-done | bytes 262176 | tf_op jit(solution)/shard_map/ppermute | solution.py:186
  21.2 1.6 %collective-permute-start.1 = (bf16[8,64,256]{2,1,0:T(8,128)(2,1)S(1)}, bf16[8,64,256]{2,1,0:T(8,128)(2,1)S(1)}, u32[]{:S(2)}, u32[]{:S(2)}) collective-permute-start(bf16[8,64,256]{2,1,0:T(8,128)(2,1)S(1)} %collective-permute-done.refs_0_), channel_id=1, source_target_pairs={{0,8},{8,16},{16,24},{24,28},{28,20},{20,12},{12,4},{4,0},{1,9},{9... | collective-permute-start | bytes 786440 | tf_op jit(solution)/shard_map/ppermute | solution.py:186
  22.8 2.6 %collective-permute-start.10 = (f32[40,256]{1,0:T(8,128)S(1)}, f32[40,256]{1,0:T(8,128)S(1)}, u32[]{:S(2)}, u32[]{:S(2)}) collective-permute-start(f32[40,256]{1,0:T(8,128)S(1)} %fusion.1), channel_id=1, source_target_pairs={{0,16},{4,20},{8,24},{12,28},{16,0},{20,4},{24,8},{28,12},{1,17},{... | collective-permute-start | bytes 122888 | tf_op jit(solution)/shard_map/ppermute | solution.py:168
  25.4 1.0 %shard_map.96.refs_5_ = f32[256,256]{1,0:T(8,128)S(1)} custom-call(s32[128]{0:T(128)S(1)} %copy-done.5, s32[1]{0:T(128)} %copy.10.current, bf16[8,64,256]{2,1,0:T(8,128)(2,1)S(1)} %collective-permute-done.refs_0_, bf16[8,64,256]{2,1,0:T(8,128)(2,1)S(1)} %collective-permute-done.9.refs_1_, bf16[8,64,256]{2,1,0:T(8,128)(2,1)S(1)} %collective-permute-done.4.refs_2_, ...), custom_call_target="tpu_custom_call" | custom-call | flops 268435456 | bytes 2097152 | tf_op jit(solution)/shard_map/pallas_call | solution.py:79
  26.4 4.6 %collective-permute-done.10 = f32[40,256]{1,0:T(8,128)S(1)} collective-permute-done((f32[40,256]{1,0:T(8,128)S(1)}, f32[40,256]{1,0:T(8,128)S(1)}, u32[]{:S(2)}, u32[]{:S(2)}) %collective-permute-start.10) | collective-permute-done | bytes 40992 | tf_op jit(solution)/shard_map/ppermute | solution.py:168
  31.1 0.0 collective-permute-done.7.refs_2_
  31.1 2.4 %collective-permute-start.11 = (bf16[8,64,256]{2,1,0:T(8,128)(2,1)S(1)}, bf16[8,64,256]{2,1,0:T(8,128)(2,1)S(1)}, u32[]{:S(2)}, u32[]{:S(2)}) collective-permute-start(bf16[8,64,256]{2,1,0:T(8,128)(2,1)S(1)} %collective-permute-done.7.refs_2_), channel_id=1, source_target_pairs={{0,8},{8,16},{16,24},{24,28},{28,20},{20,12},{12,4},{4,0},{1,9},{9... | collective-permute-start | bytes 786440 | tf_op jit(solution)/shard_map/ppermute | solution.py:186
  33.5 0.5 collective-permute-start.12
  34.0 1.5 %collective-permute-start.2 = (bf16[8,64,256]{2,1,0:T(8,128)(2,1)S(1)}, bf16[8,64,256]{2,1,0:T(8,128)(2,1)S(1)}, u32[]{:S(2)}, u32[]{:S(2)}) collective-permute-start(bf16[8,64,256]{2,1,0:T(8,128)(2,1)S(1)} %collective-permute-done.1.refs_0_), channel_id=1, source_target_pairs={{0,8},{8,16},{16,24},{24,28},{28,20},{20,12},{12,4},{4,0},{1,9},{9... | collective-permute-start | bytes 786440 | tf_op jit(solution)/shard_map/ppermute | solution.py:186
  35.5 1.9 %collective-permute-start.14 = (f32[40,256]{1,0:T(8,128)S(1)}, f32[40,256]{1,0:T(8,128)S(1)}, u32[]{:S(2)}, u32[]{:S(2)}) collective-permute-start(f32[40,256]{1,0:T(8,128)S(1)} %add.46), channel_id=1, source_target_pairs={{0,8},{4,12},{8,0},{12,4},{16,24},{20,28},{24,16},{28,20},{1,9},{5... | collective-permute-start | bytes 122888 | tf_op jit(solution)/shard_map/ppermute | solution.py:168
  37.4 0.5 collective-permute-start.16
  38.0 1.0 %shard_map.97.refs_5_ = f32[256,256]{1,0:T(8,128)S(1)} custom-call(s32[128]{0:T(128)S(1)} %copy-done.5, s32[1]{0:T(128)} %copy.10.current, bf16[8,64,256]{2,1,0:T(8,128)(2,1)S(1)} %collective-permute-done.1.refs_0_, bf16[8,64,256]{2,1,0:T(8,128)(2,1)S(1)} %collective-permute-done.13.refs_1_, bf16[8,64,256]{2,1,0:T(8,128)(2,1)S(1)} %collective-permute-done.7.refs_2_, ...), custom_call_target="tpu_custom_call" | custom-call | flops 268435456 | bytes 2097152 | tf_op jit(solution)/shard_map/pallas_call | solution.py:79
  39.0 0.0 copy-start.4
  39.0 4.7 %collective-permute-done.14 = f32[40,256]{1,0:T(8,128)S(1)} collective-permute-done((f32[40,256]{1,0:T(8,128)S(1)}, f32[40,256]{1,0:T(8,128)S(1)}, u32[]{:S(2)}, u32[]{:S(2)}) %collective-permute-start.14) | collective-permute-done | bytes 40992 | tf_op jit(solution)/shard_map/ppermute | solution.py:168
  43.8 0.0 collective-permute-done.12.refs_3_
  43.8 3.0 %collective-permute-start.15 = (bf16[8,64,256]{2,1,0:T(8,128)(2,1)S(1)}, bf16[8,64,256]{2,1,0:T(8,128)(2,1)S(1)}, u32[]{:S(2)}, u32[]{:S(2)}) collective-permute-start(bf16[8,64,256]{2,1,0:T(8,128)(2,1)S(1)} %collective-permute-done.12.refs_3_), channel_id=1, source_target_pairs={{8,0},{16,8},{24,16},{28,24},{20,28},{12,20},{4,12},{0,4},{9,1},{1... | collective-permute-start | bytes 786440 | tf_op jit(solution)/shard_map/ppermute | solution.py:195
  46.8 1.6 %collective-permute-start.18 = (f32[40,256]{1,0:T(8,128)S(1)}, f32[40,256]{1,0:T(8,128)S(1)}, u32[]{:S(2)}, u32[]{:S(2)}) collective-permute-start(f32[40,256]{1,0:T(8,128)S(1)} %add.47.s0), channel_id=1, source_target_pairs={{0,2},{1,3},{2,0},{3,1},{4,6},{5,7},{6,4},{7,5},{8,10},{9,11},{10,... | collective-permute-start | bytes 122888 | tf_op jit(solution)/shard_map/ppermute | solution.py:168
  48.4 1.1 %collective-permute-start.19 = (f32[40,256]{1,0:T(8,128)S(1)}, f32[40,256]{1,0:T(8,128)S(1)}, u32[]{:S(2)}, u32[]{:S(2)}) collective-permute-start(f32[40,256]{1,0:T(8,128)S(1)} %collective-permute-done.17.s1), channel_id=1, source_target_pairs={{0,2},{1,3},{2,0},{3,1},{4,6},{5,7},{6,4},{7,5},{8,10},{9,11},{10,... | collective-permute-start | bytes 122888 | tf_op jit(solution)/shard_map/ppermute | solution.py:168
  49.5 1.1 %shard_map.98 = (f32[256,256]{1,0:T(8,128)S(1)}, bf16[2,512,256]{2,1,0:T(8,128)(2,1)S(1)}) custom-call(s32[128]{0:T(128)S(1)} %copy-done.5, s32[1]{0:T(128)} %copy.10.current, bf16[8,64,256]{2,1,0:T(8,128)(2,1)S(1)} %collective-permute-done.2.refs_0_, bf16[8,64,256]{2,1,0:T(8,128)(2,1)S(1)} %collective-permute-done.16.refs_1_, ...), custom_call_target="tpu_custom_call" | custom-call | flops 268435456 | bytes 2097152 | tf_op jit(solution)/shard_map/pallas_call | solution.py:79
  50.7 0.2 collective-permute-done.18.s2
  50.9 1.5 %collective-permute-done.19.s3 = f32[40,256]{1,0:T(8,128)S(1)} collective-permute-done((f32[40,256]{1,0:T(8,128)S(1)}, f32[40,256]{1,0:T(8,128)S(1)}, u32[]{:S(2)}, u32[]{:S(2)}) %collective-permute-start.19) | collective-permute-done | bytes 40992 | tf_op jit(solution)/shard_map/ppermute | solution.py:168
  52.4 0.8 %collective-permute-done.3.panel_a = bf16[8,64,256]{2,1,0:T(8,128)(2,1)S(1)} collective-permute-done((bf16[8,64,256]{2,1,0:T(8,128)(2,1)S(1)}, bf16[8,64,256]{2,1,0:T(8,128)(2,1)S(1)}, u32[]{:S(2)}, u32[]{:S(2)}) %collective-permute-start.3) | collective-permute-done | bytes 262176 | tf_op jit(solution)/shard_map/ppermute | solution.py:193
  53.2 0.3 shard_map.99
  53.5 0.1 collective-permute-start.20
  53.6 1.5 %collective-permute-done.20.mate = f32[256,256]{1,0:T(8,128)S(1)} collective-permute-done((f32[256,256]{1,0:T(8,128)S(1)}, f32[256,256]{1,0:T(8,128)S(1)}, u32[]{:S(2)}, u32[]{:S(2)}) %collective-permute-start.20) | collective-permute-done | bytes 262176 | tf_op jit(solution)/shard_map/ppermute | solution.py:168
  55.1 1.6 %collective-permute-start.21 = (f32[128,256]{1,0:T(8,128)S(1)}, f32[128,256]{1,0:T(8,128)S(1)}, u32[]{:S(2)}, u32[]{:S(2)}) collective-permute-start(f32[128,256]{1,0:T(8,128)S(1)} %slice_add_fusion), channel_id=1, source_target_pairs={{0,2},{1,3},{2,0},{3,1},{4,6},{5,7},{6,4},{7,5},{8,10},{9,11},{10,... | collective-permute-start | bytes 393224 | tf_op jit(solution)/shard_map/ppermute | solution.py:168
  56.8 1.0 %collective-permute-start.23 = (f32[128,256]{1,0:T(8,128)S(1)}, f32[128,256]{1,0:T(8,128)S(1)}, u32[]{:S(2)}, u32[]{:S(2)}) collective-permute-start(f32[128,256]{1,0:T(8,128)S(1)} %pad_maximum_fusion.1), channel_id=1, source_target_pairs={{0,4},{4,0},{8,12},{12,8},{16,20},{20,16},{24,28},{28,24},{1,5},{5... | collective-permute-start | bytes 393224 | tf_op jit(solution)/shard_map/ppermute | solution.py:168
  57.7 3.0 %collective-permute-done.21.far = f32[128,256]{1,0:T(8,128)S(1)} collective-permute-done((f32[128,256]{1,0:T(8,128)S(1)}, f32[128,256]{1,0:T(8,128)S(1)}, u32[]{:S(2)}, u32[]{:S(2)}) %collective-permute-start.21) | collective-permute-done | bytes 131104 | tf_op jit(solution)/shard_map/ppermute | solution.py:168
  60.8 0.6 shard_map.100
  61.4 0.7 %collective-permute-done.23.given = f32[128,256]{1,0:T(8,128)S(1)} collective-permute-done((f32[128,256]{1,0:T(8,128)S(1)}, f32[128,256]{1,0:T(8,128)S(1)}, u32[]{:S(2)}, u32[]{:S(2)}) %collective-permute-start.23) | collective-permute-done | bytes 131104 | tf_op jit(solution)/shard_map/ppermute | solution.py:168
  62.1 1.0 %shard_map.101 = (f32[64,256]{1,0:T(8,128)}, f32[1,256]{1,0:T(1,128)}) custom-call(f32[128,256]{1,0:T(8,128)S(1)} %get-tuple-element.49.mine, f32[128,256]{1,0:T(8,128)S(1)} %get-tuple-element.50.other, f32[256,256]{1,0:T(8,128)S(1)} %collective-permute-done.20.mate, f32[128,256]{1,0:T(8,128)S(1)} %collective-permute-done.21.far, ...), custom_call_target="tpu_custom_call" | custom-call | flops 200000000 | bytes 1000000 | tf_op jit(solution)/shard_map/pallas_call | solution.py:230
  (35 shorter events, 0.2 us)
Async XLA Ops:
  0.6 1.6 %copy-start = (f32[16,256,32]{1,2,0:T(8,128)S(1)}, f32[16,256,32]{1,2,0:T(8,128)}, u32[]{:S(2)}) copy-start(f32[16,256,32]{1,2,0:T(8,128)} %param.12) | copy-start | bytes 1572868
  2.2 13.0 %collective-permute-start.6 = (f32[40,256]{1,0:T(8,128)S(1)}, f32[40,256]{1,0:T(8,128)S(1)}, u32[]{:S(2)}, u32[]{:S(2)}) collective-permute-start(f32[40,256]{1,0:T(8,128)S(1)} %fusion.2), channel_id=1, source_target_pairs={{0,4},{4,0},{8,12},{12,8},{16,20},{20,16},{24,28},{28,24},{1,5},{5... | collective-permute-start | bytes 122888 | tf_op jit(solution)/shard_map/ppermute | solution.py:168
  6.3 9.3 %collective-permute-start.4 = (bf16[8,64,256]{2,1,0:T(8,128)(2,1)S(1)}, bf16[8,64,256]{2,1,0:T(8,128)(2,1)S(1)}, u32[]{:S(2)}, u32[]{:S(2)}) collective-permute-start(bf16[8,64,256]{2,1,0:T(8,128)(2,1)S(1)} %get-tuple-element.62), channel_id=1, source_target_pairs={{0,8},{8,16},{16,24},{24,28},{28,20},{20,12},{12,4},{4,0},{1,9},{9... | collective-permute-start | bytes 786440 | tf_op jit(solution)/shard_map/ppermute | solution.py:186
  7.9 9.2 %collective-permute-start.5 = (bf16[8,64,256]{2,1,0:T(8,128)(2,1)S(1)}, bf16[8,64,256]{2,1,0:T(8,128)(2,1)S(1)}, u32[]{:S(2)}, u32[]{:S(2)}) collective-permute-start(bf16[8,64,256]{2,1,0:T(8,128)(2,1)S(1)} %get-tuple-element.62), channel_id=1, source_target_pairs={{8,0},{16,8},{24,16},{28,24},{20,28},{12,20},{4,12},{0,4},{9,1},{1... | collective-permute-start | bytes 786440 | tf_op jit(solution)/shard_map/ppermute | solution.py:186
  8.4 12.8 %collective-permute-start = (bf16[8,64,256]{2,1,0:T(8,128)(2,1)S(1)}, bf16[8,64,256]{2,1,0:T(8,128)(2,1)S(1)}, u32[]{:S(2)}, u32[]{:S(2)}) collective-permute-start(bf16[8,64,256]{2,1,0:T(8,128)(2,1)S(1)} %get-tuple-element.63), channel_id=1, source_target_pairs={{0,8},{8,16},{16,24},{24,28},{28,20},{20,12},{12,4},{4,0},{1,9},{9... | collective-permute-start | bytes 786440 | tf_op jit(solution)/shard_map/ppermute | solution.py:186
  10.0 15.4 %collective-permute-start.9 = (bf16[8,64,256]{2,1,0:T(8,128)(2,1)S(1)}, bf16[8,64,256]{2,1,0:T(8,128)(2,1)S(1)}, u32[]{:S(2)}, u32[]{:S(2)}) collective-permute-start(bf16[8,64,256]{2,1,0:T(8,128)(2,1)S(1)} %get-tuple-element.63), channel_id=1, source_target_pairs={{8,0},{16,8},{24,16},{28,24},{20,28},{12,20},{4,12},{0,4},{9,1},{1... | collective-permute-start | bytes 786440 | tf_op jit(solution)/shard_map/ppermute | solution.py:186
  10.4 2.2 %copy-start.1 = (bf16[128,64,256]{2,1,0:T(8,128)(2,1)S(1)}, bf16[128,64,256]{2,1,0:T(8,128)(2,1)}, u32[]{:S(2)}) copy-start(bf16[128,64,256]{2,1,0:T(8,128)(2,1)} %refs_4_.5) | copy-start | bytes 12582916
  12.6 1.0 %copy-start.3 = (bf16[16,256,64]{1,2,0:T(8,128)(2,1)S(1)}, bf16[16,256,64]{1,2,0:T(8,128)(2,1)}, u32[]{:S(2)}) copy-start(bf16[16,256,64]{1,2,0:T(8,128)(2,1)} %param.10) | copy-start | bytes 1572868
  13.6 0.7 %copy-start.5 = (s32[128]{0:T(128)S(1)}, s32[128]{0:T(128)}, u32[]{:S(2)}) copy-start(s32[128]{0:T(128)} %slot_block.7) | copy-start | bytes 1540
  14.3 11.1 %copy-start.2 = (bf16[128,64,256]{2,1,0:T(8,128)(2,1)S(1)}, bf16[128,64,256]{2,1,0:T(8,128)(2,1)}, u32[]{:S(2)}) copy-start(bf16[128,64,256]{2,1,0:T(8,128)(2,1)} %refs_4_.5) | copy-start | bytes 12582916
  17.2 13.9 %collective-permute-start.7 = (bf16[8,64,256]{2,1,0:T(8,128)(2,1)S(1)}, bf16[8,64,256]{2,1,0:T(8,128)(2,1)S(1)}, u32[]{:S(2)}, u32[]{:S(2)}) collective-permute-start(bf16[8,64,256]{2,1,0:T(8,128)(2,1)S(1)} %collective-permute-done.4.refs_2_), channel_id=1, source_target_pairs={{0,8},{8,16},{16,24},{24,28},{28,20},{20,12},{12,4},{4,0},{1,9},{9... | collective-permute-start | bytes 786440 | tf_op jit(solution)/shard_map/ppermute | solution.py:186
  18.8 12.3 %collective-permute-start.8 = (bf16[8,64,256]{2,1,0:T(8,128)(2,1)S(1)}, bf16[8,64,256]{2,1,0:T(8,128)(2,1)S(1)}, u32[]{:S(2)}, u32[]{:S(2)}) collective-permute-start(bf16[8,64,256]{2,1,0:T(8,128)(2,1)S(1)} %collective-permute-done.5.refs_3_), channel_id=1, source_target_pairs={{8,0},{16,8},{24,16},{28,24},{20,28},{12,20},{4,12},{0,4},{9,1},{1... | collective-permute-start | bytes 786440 | tf_op jit(solution)/shard_map/ppermute | solution.py:186
  21.2 12.8 %collective-permute-start.1 = (bf16[8,64,256]{2,1,0:T(8,128)(2,1)S(1)}, bf16[8,64,256]{2,1,0:T(8,128)(2,1)S(1)}, u32[]{:S(2)}, u32[]{:S(2)}) collective-permute-start(bf16[8,64,256]{2,1,0:T(8,128)(2,1)S(1)} %collective-permute-done.refs_0_), channel_id=1, source_target_pairs={{0,8},{8,16},{16,24},{24,28},{28,20},{20,12},{12,4},{4,0},{1,9},{9... | collective-permute-start | bytes 786440 | tf_op jit(solution)/shard_map/ppermute | solution.py:186
  22.8 8.3 %collective-permute-start.10 = (f32[40,256]{1,0:T(8,128)S(1)}, f32[40,256]{1,0:T(8,128)S(1)}, u32[]{:S(2)}, u32[]{:S(2)}) collective-permute-start(f32[40,256]{1,0:T(8,128)S(1)} %fusion.1), channel_id=1, source_target_pairs={{0,16},{4,20},{8,24},{12,28},{16,0},{20,4},{24,8},{28,12},{1,17},{... | collective-permute-start | bytes 122888 | tf_op jit(solution)/shard_map/ppermute | solution.py:168
  25.4 12.1 %collective-permute-start.13 = (bf16[8,64,256]{2,1,0:T(8,128)(2,1)S(1)}, bf16[8,64,256]{2,1,0:T(8,128)(2,1)S(1)}, u32[]{:S(2)}, u32[]{:S(2)}) collective-permute-start(bf16[8,64,256]{2,1,0:T(8,128)(2,1)S(1)} %collective-permute-done.9.refs_1_), channel_id=1, source_target_pairs={{8,0},{16,8},{24,16},{28,24},{20,28},{12,20},{4,12},{0,4},{9,1},{1... | collective-permute-start | bytes 786440 | tf_op jit(solution)/shard_map/ppermute | solution.py:186
  31.1 12.7 %collective-permute-start.11 = (bf16[8,64,256]{2,1,0:T(8,128)(2,1)S(1)}, bf16[8,64,256]{2,1,0:T(8,128)(2,1)S(1)}, u32[]{:S(2)}, u32[]{:S(2)}) collective-permute-start(bf16[8,64,256]{2,1,0:T(8,128)(2,1)S(1)} %collective-permute-done.7.refs_2_), channel_id=1, source_target_pairs={{0,8},{8,16},{16,24},{24,28},{28,20},{20,12},{12,4},{4,0},{1,9},{9... | collective-permute-start | bytes 786440 | tf_op jit(solution)/shard_map/ppermute | solution.py:186
  33.5 10.3 %collective-permute-start.12 = (bf16[8,64,256]{2,1,0:T(8,128)(2,1)S(1)}, bf16[8,64,256]{2,1,0:T(8,128)(2,1)S(1)}, u32[]{:S(2)}, u32[]{:S(2)}) collective-permute-start(bf16[8,64,256]{2,1,0:T(8,128)(2,1)S(1)} %collective-permute-done.8.refs_3_), channel_id=1, source_target_pairs={{8,0},{16,8},{24,16},{28,24},{20,28},{12,20},{4,12},{0,4},{9,1},{1... | collective-permute-start | bytes 786440 | tf_op jit(solution)/shard_map/ppermute | solution.py:186
  34.0 12.8 %collective-permute-start.2 = (bf16[8,64,256]{2,1,0:T(8,128)(2,1)S(1)}, bf16[8,64,256]{2,1,0:T(8,128)(2,1)S(1)}, u32[]{:S(2)}, u32[]{:S(2)}) collective-permute-start(bf16[8,64,256]{2,1,0:T(8,128)(2,1)S(1)} %collective-permute-done.1.refs_0_), channel_id=1, source_target_pairs={{0,8},{8,16},{16,24},{24,28},{28,20},{20,12},{12,4},{4,0},{1,9},{9... | collective-permute-start | bytes 786440 | tf_op jit(solution)/shard_map/ppermute | solution.py:186
  35.5 8.3 %collective-permute-start.14 = (f32[40,256]{1,0:T(8,128)S(1)}, f32[40,256]{1,0:T(8,128)S(1)}, u32[]{:S(2)}, u32[]{:S(2)}) collective-permute-start(f32[40,256]{1,0:T(8,128)S(1)} %add.46), channel_id=1, source_target_pairs={{0,8},{4,12},{8,0},{12,4},{16,24},{20,28},{24,16},{28,20},{1,9},{5... | collective-permute-start | bytes 122888 | tf_op jit(solution)/shard_map/ppermute | solution.py:168
  37.4 12.1 %collective-permute-start.16 = (bf16[8,64,256]{2,1,0:T(8,128)(2,1)S(1)}, bf16[8,64,256]{2,1,0:T(8,128)(2,1)S(1)}, u32[]{:S(2)}, u32[]{:S(2)}) collective-permute-start(bf16[8,64,256]{2,1,0:T(8,128)(2,1)S(1)} %collective-permute-done.13.refs_1_), channel_id=1, source_target_pairs={{8,0},{16,8},{24,16},{28,24},{20,28},{12,20},{4,12},{0,4},{9,1},{1... | collective-permute-start | bytes 786440 | tf_op jit(solution)/shard_map/ppermute | solution.py:186
  39.0 21.7 %copy-start.4 = (f32[256,32]{0,1:T(8,128)S(1)}, f32[256,32]{0,1:T(8,128)}, u32[]{:S(2)}) copy-start(f32[256,32]{0,1:T(8,128)} %param.13) | copy-start | bytes 98308
  43.8 18.3 %copy-start.6 = (f32[256]{0:T(256)S(1)}, f32[256]{0:T(256)}, u32[]{:S(2)}) copy-start(f32[256]{0:T(256)} %param.15) | copy-start | bytes 3076
  43.8 8.6 %collective-permute-start.15 = (bf16[8,64,256]{2,1,0:T(8,128)(2,1)S(1)}, bf16[8,64,256]{2,1,0:T(8,128)(2,1)S(1)}, u32[]{:S(2)}, u32[]{:S(2)}) collective-permute-start(bf16[8,64,256]{2,1,0:T(8,128)(2,1)S(1)} %collective-permute-done.12.refs_3_), channel_id=1, source_target_pairs={{8,0},{16,8},{24,16},{28,24},{20,28},{12,20},{4,12},{0,4},{9,1},{1... | collective-permute-start | bytes 786440 | tf_op jit(solution)/shard_map/ppermute | solution.py:195
  46.8 6.4 %collective-permute-start.3 = (bf16[8,64,256]{2,1,0:T(8,128)(2,1)S(1)}, bf16[8,64,256]{2,1,0:T(8,128)(2,1)S(1)}, u32[]{:S(2)}, u32[]{:S(2)}) collective-permute-start(bf16[8,64,256]{2,1,0:T(8,128)(2,1)S(1)} %collective-permute-done.2.refs_0_), channel_id=1, source_target_pairs={{0,8},{8,16},{16,24},{24,28},{28,20},{20,12},{12,4},{4,0},{1,9},{9... | collective-permute-start | bytes 786440 | tf_op jit(solution)/shard_map/ppermute | solution.py:193
  46.8 1.6 %collective-permute-start.17 = (f32[40,256]{1,0:T(8,128)S(1)}, f32[40,256]{1,0:T(8,128)S(1)}, u32[]{:S(2)}, u32[]{:S(2)}) collective-permute-start(f32[40,256]{1,0:T(8,128)S(1)} %add.47.s0), channel_id=1, source_target_pairs={{0,1},{1,0},{2,3},{3,2},{4,5},{5,4},{6,7},{7,6},{8,9},{9,8},{10,11... | collective-permute-start | bytes 122888 | tf_op jit(solution)/shard_map/ppermute | solution.py:168
  46.8 4.1 %collective-permute-start.18 = (f32[40,256]{1,0:T(8,128)S(1)}, f32[40,256]{1,0:T(8,128)S(1)}, u32[]{:S(2)}, u32[]{:S(2)}) collective-permute-start(f32[40,256]{1,0:T(8,128)S(1)} %add.47.s0), channel_id=1, source_target_pairs={{0,2},{1,3},{2,0},{3,1},{4,6},{5,7},{6,4},{7,5},{8,10},{9,11},{10,... | collective-permute-start | bytes 122888 | tf_op jit(solution)/shard_map/ppermute | solution.py:168
  48.4 4.0 %collective-permute-start.19 = (f32[40,256]{1,0:T(8,128)S(1)}, f32[40,256]{1,0:T(8,128)S(1)}, u32[]{:S(2)}, u32[]{:S(2)}) collective-permute-start(f32[40,256]{1,0:T(8,128)S(1)} %collective-permute-done.17.s1), channel_id=1, source_target_pairs={{0,2},{1,3},{2,0},{3,1},{4,6},{5,7},{6,4},{7,5},{8,10},{9,11},{10,... | collective-permute-start | bytes 122888 | tf_op jit(solution)/shard_map/ppermute | solution.py:168
  53.5 1.6 %collective-permute-start.20 = (f32[256,256]{1,0:T(8,128)S(1)}, f32[256,256]{1,0:T(8,128)S(1)}, u32[]{:S(2)}, u32[]{:S(2)}) collective-permute-start(f32[256,256]{1,0:T(8,128)S(1)} %pad_maximum_fusion), channel_id=1, source_target_pairs={{0,1},{1,0},{2,3},{3,2},{4,5},{5,4},{6,7},{7,6},{8,9},{9,8},{10,11... | collective-permute-start | bytes 786440 | tf_op jit(solution)/shard_map/ppermute | solution.py:168
  55.1 5.6 %collective-permute-start.21 = (f32[128,256]{1,0:T(8,128)S(1)}, f32[128,256]{1,0:T(8,128)S(1)}, u32[]{:S(2)}, u32[]{:S(2)}) collective-permute-start(f32[128,256]{1,0:T(8,128)S(1)} %slice_add_fusion), channel_id=1, source_target_pairs={{0,2},{1,3},{2,0},{3,1},{4,6},{5,7},{6,4},{7,5},{8,10},{9,11},{10,... | collective-permute-start | bytes 393224 | tf_op jit(solution)/shard_map/ppermute | solution.py:168
  56.8 5.3 %collective-permute-start.23 = (f32[128,256]{1,0:T(8,128)S(1)}, f32[128,256]{1,0:T(8,128)S(1)}, u32[]{:S(2)}, u32[]{:S(2)}) collective-permute-start(f32[128,256]{1,0:T(8,128)S(1)} %pad_maximum_fusion.1), channel_id=1, source_target_pairs={{0,4},{4,0},{8,12},{12,8},{16,20},{20,16},{24,28},{28,24},{1,5},{5... | collective-permute-start | bytes 393224 | tf_op jit(solution)/shard_map/ppermute | solution.py:168
  60.7 1.4 %collective-permute-start.22 = (f32[128,256]{1,0:T(8,128)S(1)}, f32[128,256]{1,0:T(8,128)S(1)}, u32[]{:S(2)}, u32[]{:S(2)}) collective-permute-start(f32[128,256]{1,0:T(8,128)S(1)} %collective-permute-done.21.far), channel_id=1, source_target_pairs={{0,1},{1,0},{2,3},{3,2},{4,5},{5,4},{6,7},{7,6},{8,9},{9,8},{10,11... | collective-permute-start | bytes 393224 | tf_op jit(solution)/shard_map/ppermute | solution.py:168

commit v7 on v6

--- a/solution.py
+++ b/solution.py
@@ -225,6 +225,7 @@
     )(*spreads, cand_weights.T)
 
     mate = flip(jnp.concatenate([mine, other], axis=0), "obs", 1, 4)
+    mate, tile, high, low = tie((mate, tile, high, low))
     far = flip(mine + mate[mine.shape[0] :], "obs", 2, 4)
     mate_far = flip(far, "obs", 1, 4)
     solved_rows, remaining = pl.pallas_call(

time: 63.4 us -> 63.4 us (level)
  no operation moved by 1% of the time
where the time goes in v7:
time: 63.4 us; the launch traced here: 63.1 us
  starting transfers between devices  28.5 us (45%)
  waiting for transfers between devices  21.1 us (33%)
  Pallas kernels  5.96 us (9%)
  local copies, waits for them, and re-layouts  5.79 us (9%)
  between operations  1.6 us (3%)
    ppermute x10, waiting for transfers between devices, flip(): return lax.ppermute(value, axis, [(i, i ^ bits) for i in range(size)])  16.4 us
    ppermute x10, starting transfers between devices, flip(): return lax.ppermute(value, axis, [(i, i ^ bits) for i in range(size)])  12.9 us
    ppermute x6, starting transfers between devices, onward(): lax.ppermute(pair[0], 'cand', RING)  10.3 us
    pallas_call x4, Pallas kernels, add(): pl.pallas_call(functools.partial(kernel, sources), out_shape=outs, in_spe...  4.06 us
    unnamed x14, local copies, waits for them, and re-layouts  3.91 us
    ppermute x1, starting transfers between devices, on_ring(): next_late = onward(late) if k < 3 else lax.ppermute(late[1], 'cand', BACK)  2.97 us
    ppermute x6, starting transfers between devices, onward(): lax.ppermute(pair[1], 'cand', BACK)  2.39 us
    ppermute x6, waiting for transfers between devices, onward(): lax.ppermute(pair[0], 'cand', RING)  2.37 us
  transfers between devices with their start and end apart: 24, of which 11 were waited for; matrix products, arithmetic and copies ran while one was open for 2% of the time, Pallas kernels for 7%

profile of v7, /device:TPU:0, one launch (start us, length us, event | category | flops | bytes accessed | tf_op | source)
XLA Modules:
  0.0 63.1 jit_solution(16074006345734718694)
XLA Ops:
  0.6 0.0 copy-start
  1.4 0.8 %dynamic-slice_bitcast_fusion.1 = (f32[32,256]{1,0:T(8,128)S(1)}, f32[32,256]{1,0:T(8,128)S(1)}) fusion(f32[16,64,256]{2,1,0:T(8,128)} %param.14, s32[]{:T(128)S(6)} %select_n.52, s32[]{:T(128)S(6)} %select_n.54, s32[]{:T(128)S(6)} %select_n.59), kind=kLoop, calls=%fused_computation.9 | loop fusion | bytes 131084 | tf_op jit(solution)/shard_map/squeeze | solution.py:177
  2.2 3.0 %collective-permute-start.6 = (f32[40,256]{1,0:T(8,128)S(1)}, f32[40,256]{1,0:T(8,128)S(1)}, u32[]{:S(2)}, u32[]{:S(2)}) collective-permute-start(f32[40,256]{1,0:T(8,128)S(1)} %fusion.2), channel_id=1, source_target_pairs={{0,4},{4,0},{8,12},{12,8},{16,20},{20,16},{24,28},{28,24},{1,5},{5... | collective-permute-start | bytes 122888 | tf_op jit(solution)/shard_map/ppermute | solution.py:168
  5.2 1.1 %fusion.3 = (bf16[8,64,256]{2,1,0:T(8,128)(2,1)S(1)}, bf16[8,64,256]{2,1,0:T(8,128)(2,1)S(1)}) fusion(bf16[16,64,256]{2,1,0:T(8,128)(2,1)} %bitcast.17), kind=kLoop, calls=%fused_computation.11 | loop fusion | bytes 1048576 | tf_op jit(solution)/shard_map/slice | solution.py:189
  6.3 1.6 %collective-permute-start.4 = (bf16[8,64,256]{2,1,0:T(8,128)(2,1)S(1)}, bf16[8,64,256]{2,1,0:T(8,128)(2,1)S(1)}, u32[]{:S(2)}, u32[]{:S(2)}) collective-permute-start(bf16[8,64,256]{2,1,0:T(8,128)(2,1)S(1)} %get-tuple-element.70), channel_id=1, source_target_pairs={{0,8},{8,16},{16,24},{24,28},{28,20},{20,12},{12,4},{4,0},{1,9},{9... | collective-permute-start | bytes 786440 | tf_op jit(solution)/shard_map/ppermute | solution.py:186
  7.9 0.4 collective-permute-start.5
  8.4 1.6 %collective-permute-start = (bf16[8,64,256]{2,1,0:T(8,128)(2,1)S(1)}, bf16[8,64,256]{2,1,0:T(8,128)(2,1)S(1)}, u32[]{:S(2)}, u32[]{:S(2)}) collective-permute-start(bf16[8,64,256]{2,1,0:T(8,128)(2,1)S(1)} %get-tuple-element.71), channel_id=1, source_target_pairs={{0,8},{8,16},{16,24},{24,28},{28,20},{20,12},{12,4},{4,0},{1,9},{9... | collective-permute-start | bytes 786440 | tf_op jit(solution)/shard_map/ppermute | solution.py:186
  10.0 0.4 collective-permute-start.9
  10.4 2.2 %copy-done.1 = bf16[128,64,256]{2,1,0:T(8,128)(2,1)S(1)} copy-done((bf16[128,64,256]{2,1,0:T(8,128)(2,1)S(1)}, bf16[128,64,256]{2,1,0:T(8,128)(2,1)}, u32[]{:S(2)}) %copy-start.1) | copy-done | bytes 4194328
  12.6 1.0 %copy-done.3 = bf16[16,256,64]{1,2,0:T(8,128)(2,1)S(1)} copy-done((bf16[16,256,64]{1,2,0:T(8,128)(2,1)S(1)}, bf16[16,256,64]{1,2,0:T(8,128)(2,1)}, u32[]{:S(2)}) %copy-start.3) | copy-done | bytes 524312
  13.6 0.7 %copy-done.5 = s32[128]{0:T(128)S(1)} copy-done((s32[128]{0:T(128)S(1)}, s32[128]{0:T(128)}, u32[]{:S(2)}) %copy-start.5) | copy-done | bytes 536
  14.3 0.9 %shard_map.95.refs_5_ = f32[256,256]{1,0:T(8,128)S(1)} custom-call(s32[128]{0:T(128)S(1)} %copy-done.5, s32[1]{0:T(128)} %copy.10.current, bf16[16,64,256]{2,1,0:T(8,128)(2,1)S(1)} %bitcast.18, bf16[128,64,256]{2,1,0:T(8,128)(2,1)S(1)} %copy-done.1), custom_call_target="tpu_custom_call" | custom-call | flops 134217728 | bytes 1048576 | tf_op jit(solution)/shard_map/pallas_call | solution.py:79
  15.2 0.0 collective-permute-done.6
  15.2 0.4 collective-permute-done.4.refs_2_
  15.6 1.6 %collective-permute-done.5.refs_3_ = bf16[8,64,256]{2,1,0:T(8,128)(2,1)S(1)} collective-permute-done((bf16[8,64,256]{2,1,0:T(8,128)(2,1)S(1)}, bf16[8,64,256]{2,1,0:T(8,128)(2,1)S(1)}, u32[]{:S(2)}, u32[]{:S(2)}) %collective-permute-start.5) | collective-permute-done | bytes 262176 | tf_op jit(solution)/shard_map/ppermute | solution.py:186
  17.2 1.6 %collective-permute-start.7 = (bf16[8,64,256]{2,1,0:T(8,128)(2,1)S(1)}, bf16[8,64,256]{2,1,0:T(8,128)(2,1)S(1)}, u32[]{:S(2)}, u32[]{:S(2)}) collective-permute-start(bf16[8,64,256]{2,1,0:T(8,128)(2,1)S(1)} %collective-permute-done.4.refs_2_), channel_id=1, source_target_pairs={{0,8},{8,16},{16,24},{24,28},{28,20},{20,12},{12,4},{4,0},{1,9},{9... | collective-permute-start | bytes 786440 | tf_op jit(solution)/shard_map/ppermute | solution.py:186
  18.8 0.4 collective-permute-start.8
  19.2 2.0 %collective-permute-done.refs_0_ = bf16[8,64,256]{2,1,0:T(8,128)(2,1)S(1)} collective-permute-done((bf16[8,64,256]{2,1,0:T(8,128)(2,1)S(1)}, bf16[8,64,256]{2,1,0:T(8,128)(2,1)S(1)}, u32[]{:S(2)}, u32[]{:S(2)}) %collective-permute-start) | collective-permute-done | bytes 262176 | tf_op jit(solution)/shard_map/ppermute | solution.py:186
  21.2 1.6 %collective-permute-start.1 = (bf16[8,64,256]{2,1,0:T(8,128)(2,1)S(1)}, bf16[8,64,256]{2,1,0:T(8,128)(2,1)S(1)}, u32[]{:S(2)}, u32[]{:S(2)}) collective-permute-start(bf16[8,64,256]{2,1,0:T(8,128)(2,1)S(1)} %collective-permute-done.refs_0_), channel_id=1, source_target_pairs={{0,8},{8,16},{16,24},{24,28},{28,20},{20,12},{12,4},{4,0},{1,9},{9... | collective-permute-start | bytes 786440 | tf_op jit(solution)/shard_map/ppermute | solution.py:186
  22.8 2.6 %collective-permute-start.10 = (f32[40,256]{1,0:T(8,128)S(1)}, f32[40,256]{1,0:T(8,128)S(1)}, u32[]{:S(2)}, u32[]{:S(2)}) collective-permute-start(f32[40,256]{1,0:T(8,128)S(1)} %fusion.1), channel_id=1, source_target_pairs={{0,16},{4,20},{8,24},{12,28},{16,0},{20,4},{24,8},{28,12},{1,17},{... | collective-permute-start | bytes 122888 | tf_op jit(solution)/shard_map/ppermute | solution.py:168
  25.4 1.0 %shard_map.96.refs_5_ = f32[256,256]{1,0:T(8,128)S(1)} custom-call(s32[128]{0:T(128)S(1)} %copy-done.5, s32[1]{0:T(128)} %copy.10.current, bf16[8,64,256]{2,1,0:T(8,128)(2,1)S(1)} %collective-permute-done.refs_0_, bf16[8,64,256]{2,1,0:T(8,128)(2,1)S(1)} %collective-permute-done.9.refs_1_, bf16[8,64,256]{2,1,0:T(8,128)(2,1)S(1)} %collective-permute-done.4.refs_2_, ...), custom_call_target="tpu_custom_call" | custom-call | flops 268435456 | bytes 2097152 | tf_op jit(solution)/shard_map/pallas_call | solution.py:79
  26.4 4.6 %collective-permute-done.10 = f32[40,256]{1,0:T(8,128)S(1)} collective-permute-done((f32[40,256]{1,0:T(8,128)S(1)}, f32[40,256]{1,0:T(8,128)S(1)}, u32[]{:S(2)}, u32[]{:S(2)}) %collective-permute-start.10) | collective-permute-done | bytes 40992 | tf_op jit(solution)/shard_map/ppermute | solution.py:168
  31.1 0.0 collective-permute-done.7.refs_2_
  31.1 2.4 %collective-permute-start.11 = (bf16[8,64,256]{2,1,0:T(8,128)(2,1)S(1)}, bf16[8,64,256]{2,1,0:T(8,128)(2,1)S(1)}, u32[]{:S(2)}, u32[]{:S(2)}) collective-permute-start(bf16[8,64,256]{2,1,0:T(8,128)(2,1)S(1)} %collective-permute-done.7.refs_2_), channel_id=1, source_target_pairs={{0,8},{8,16},{16,24},{24,28},{28,20},{20,12},{12,4},{4,0},{1,9},{9... | collective-permute-start | bytes 786440 | tf_op jit(solution)/shard_map/ppermute | solution.py:186
  33.5 0.5 collective-permute-start.12
  34.0 1.5 %collective-permute-start.2 = (bf16[8,64,256]{2,1,0:T(8,128)(2,1)S(1)}, bf16[8,64,256]{2,1,0:T(8,128)(2,1)S(1)}, u32[]{:S(2)}, u32[]{:S(2)}) collective-permute-start(bf16[8,64,256]{2,1,0:T(8,128)(2,1)S(1)} %collective-permute-done.1.refs_0_), channel_id=1, source_target_pairs={{0,8},{8,16},{16,24},{24,28},{28,20},{20,12},{12,4},{4,0},{1,9},{9... | collective-permute-start | bytes 786440 | tf_op jit(solution)/shard_map/ppermute | solution.py:186
  35.5 1.9 %collective-permute-start.14 = (f32[40,256]{1,0:T(8,128)S(1)}, f32[40,256]{1,0:T(8,128)S(1)}, u32[]{:S(2)}, u32[]{:S(2)}) collective-permute-start(f32[40,256]{1,0:T(8,128)S(1)} %add.46), channel_id=1, source_target_pairs={{0,8},{4,12},{8,0},{12,4},{16,24},{20,28},{24,16},{28,20},{1,9},{5... | collective-permute-start | bytes 122888 | tf_op jit(solution)/shard_map/ppermute | solution.py:168
  37.4 0.5 collective-permute-start.16
  38.0 1.0 %shard_map.97.refs_5_ = f32[256,256]{1,0:T(8,128)S(1)} custom-call(s32[128]{0:T(128)S(1)} %copy-done.5, s32[1]{0:T(128)} %copy.10.current, bf16[8,64,256]{2,1,0:T(8,128)(2,1)S(1)} %collective-permute-done.1.refs_0_, bf16[8,64,256]{2,1,0:T(8,128)(2,1)S(1)} %collective-permute-done.13.refs_1_, bf16[8,64,256]{2,1,0:T(8,128)(2,1)S(1)} %collective-permute-done.7.refs_2_, ...), custom_call_target="tpu_custom_call" | custom-call | flops 268435456 | bytes 2097152 | tf_op jit(solution)/shard_map/pallas_call | solution.py:79
  39.0 0.0 copy-start.4
  39.0 4.7 %collective-permute-done.14 = f32[40,256]{1,0:T(8,128)S(1)} collective-permute-done((f32[40,256]{1,0:T(8,128)S(1)}, f32[40,256]{1,0:T(8,128)S(1)}, u32[]{:S(2)}, u32[]{:S(2)}) %collective-permute-start.14) | collective-permute-done | bytes 40992 | tf_op jit(solution)/shard_map/ppermute | solution.py:168
  43.8 0.0 collective-permute-done.12.refs_3_
  43.8 3.0 %collective-permute-start.15 = (bf16[8,64,256]{2,1,0:T(8,128)(2,1)S(1)}, bf16[8,64,256]{2,1,0:T(8,128)(2,1)S(1)}, u32[]{:S(2)}, u32[]{:S(2)}) collective-permute-start(bf16[8,64,256]{2,1,0:T(8,128)(2,1)S(1)} %collective-permute-done.12.refs_3_), channel_id=1, source_target_pairs={{8,0},{16,8},{24,16},{28,24},{20,28},{12,20},{4,12},{0,4},{9,1},{1... | collective-permute-start | bytes 786440 | tf_op jit(solution)/shard_map/ppermute | solution.py:195
  46.8 1.6 %collective-permute-start.18 = (f32[40,256]{1,0:T(8,128)S(1)}, f32[40,256]{1,0:T(8,128)S(1)}, u32[]{:S(2)}, u32[]{:S(2)}) collective-permute-start(f32[40,256]{1,0:T(8,128)S(1)} %add.47.s0), channel_id=1, source_target_pairs={{0,2},{1,3},{2,0},{3,1},{4,6},{5,7},{6,4},{7,5},{8,10},{9,11},{10,... | collective-permute-start | bytes 122888 | tf_op jit(solution)/shard_map/ppermute | solution.py:168
  48.4 1.1 %collective-permute-start.19 = (f32[40,256]{1,0:T(8,128)S(1)}, f32[40,256]{1,0:T(8,128)S(1)}, u32[]{:S(2)}, u32[]{:S(2)}) collective-permute-start(f32[40,256]{1,0:T(8,128)S(1)} %collective-permute-done.17.s1), channel_id=1, source_target_pairs={{0,2},{1,3},{2,0},{3,1},{4,6},{5,7},{6,4},{7,5},{8,10},{9,11},{10,... | collective-permute-start | bytes 122888 | tf_op jit(solution)/shard_map/ppermute | solution.py:168
  49.5 1.1 %shard_map.98 = (f32[256,256]{1,0:T(8,128)S(1)}, bf16[2,512,256]{2,1,0:T(8,128)(2,1)S(1)}) custom-call(s32[128]{0:T(128)S(1)} %copy-done.5, s32[1]{0:T(128)} %copy.10.current, bf16[8,64,256]{2,1,0:T(8,128)(2,1)S(1)} %collective-permute-done.2.refs_0_, bf16[8,64,256]{2,1,0:T(8,128)(2,1)S(1)} %collective-permute-done.16.refs_1_, ...), custom_call_target="tpu_custom_call" | custom-call | flops 268435456 | bytes 2097152 | tf_op jit(solution)/shard_map/pallas_call | solution.py:79
  50.7 0.2 collective-permute-done.18.s2
  50.9 1.5 %collective-permute-done.19.s3 = f32[40,256]{1,0:T(8,128)S(1)} collective-permute-done((f32[40,256]{1,0:T(8,128)S(1)}, f32[40,256]{1,0:T(8,128)S(1)}, u32[]{:S(2)}, u32[]{:S(2)}) %collective-permute-start.19) | collective-permute-done | bytes 40992 | tf_op jit(solution)/shard_map/ppermute | solution.py:168
  52.4 0.8 %collective-permute-done.3.panel_a = bf16[8,64,256]{2,1,0:T(8,128)(2,1)S(1)} collective-permute-done((bf16[8,64,256]{2,1,0:T(8,128)(2,1)S(1)}, bf16[8,64,256]{2,1,0:T(8,128)(2,1)S(1)}, u32[]{:S(2)}, u32[]{:S(2)}) %collective-permute-start.3) | collective-permute-done | bytes 262176 | tf_op jit(solution)/shard_map/ppermute | solution.py:193
  53.2 0.3 shard_map.99
  53.5 0.1 collective-permute-start.20
  53.6 0.6 shard_map.100
  54.2 0.9 %collective-permute-done.20.mate = f32[256,256]{1,0:T(8,128)S(1)} collective-permute-done((f32[256,256]{1,0:T(8,128)S(1)}, f32[256,256]{1,0:T(8,128)S(1)}, u32[]{:S(2)}, u32[]{:S(2)}) %collective-permute-start.20) | collective-permute-done | bytes 262176 | tf_op jit(solution)/shard_map/ppermute | solution.py:168
  55.1 1.6 %collective-permute-start.21 = (f32[128,256]{1,0:T(8,128)S(1)}, f32[128,256]{1,0:T(8,128)S(1)}, u32[]{:S(2)}, u32[]{:S(2)}) collective-permute-start(f32[128,256]{1,0:T(8,128)S(1)} %slice_add_fusion), channel_id=1, source_target_pairs={{0,2},{1,3},{2,0},{3,1},{4,6},{5,7},{6,4},{7,5},{8,10},{9,11},{10,... | collective-permute-start | bytes 393224 | tf_op jit(solution)/shard_map/ppermute | solution.py:168
  56.8 1.0 %collective-permute-start.23 = (f32[128,256]{1,0:T(8,128)S(1)}, f32[128,256]{1,0:T(8,128)S(1)}, u32[]{:S(2)}, u32[]{:S(2)}) collective-permute-start(f32[128,256]{1,0:T(8,128)S(1)} %pad_maximum_fusion.1), channel_id=1, source_target_pairs={{0,4},{4,0},{8,12},{12,8},{16,20},{20,16},{24,28},{28,24},{1,5},{5... | collective-permute-start | bytes 393224 | tf_op jit(solution)/shard_map/ppermute | solution.py:168
  57.7 3.0 %collective-permute-done.21.far = f32[128,256]{1,0:T(8,128)S(1)} collective-permute-done((f32[128,256]{1,0:T(8,128)S(1)}, f32[128,256]{1,0:T(8,128)S(1)}, u32[]{:S(2)}, u32[]{:S(2)}) %collective-permute-start.21) | collective-permute-done | bytes 131104 | tf_op jit(solution)/shard_map/ppermute | solution.py:168
  60.7 1.4 %collective-permute-done.23.given = f32[128,256]{1,0:T(8,128)S(1)} collective-permute-done((f32[128,256]{1,0:T(8,128)S(1)}, f32[128,256]{1,0:T(8,128)S(1)}, u32[]{:S(2)}, u32[]{:S(2)}) %collective-permute-start.23) | collective-permute-done | bytes 131104 | tf_op jit(solution)/shard_map/ppermute | solution.py:168
  62.1 1.0 %shard_map.101 = (f32[64,256]{1,0:T(8,128)}, f32[1,256]{1,0:T(1,128)}) custom-call(f32[128,256]{1,0:T(8,128)S(1)} %get-tuple-element.53.mine, f32[128,256]{1,0:T(8,128)S(1)} %get-tuple-element.54.other, f32[256,256]{1,0:T(8,128)S(1)} %collective-permute-done.20.mate, f32[128,256]{1,0:T(8,128)S(1)} %collective-permute-done.21.far, ...), custom_call_target="tpu_custom_call" | custom-call | flops 200000000 | bytes 1000000 | tf_op jit(solution)/shard_map/pallas_call | solution.py:231
  (35 shorter events, 0.2 us)
Async XLA Ops:
  0.6 1.6 %copy-start = (f32[16,256,32]{1,2,0:T(8,128)S(1)}, f32[16,256,32]{1,2,0:T(8,128)}, u32[]{:S(2)}) copy-start(f32[16,256,32]{1,2,0:T(8,128)} %param.12) | copy-start | bytes 1572868
  2.2 13.0 %collective-permute-start.6 = (f32[40,256]{1,0:T(8,128)S(1)}, f32[40,256]{1,0:T(8,128)S(1)}, u32[]{:S(2)}, u32[]{:S(2)}) collective-permute-start(f32[40,256]{1,0:T(8,128)S(1)} %fusion.2), channel_id=1, source_target_pairs={{0,4},{4,0},{8,12},{12,8},{16,20},{20,16},{24,28},{28,24},{1,5},{5... | collective-permute-start | bytes 122888 | tf_op jit(solution)/shard_map/ppermute | solution.py:168
  6.3 9.3 %collective-permute-start.4 = (bf16[8,64,256]{2,1,0:T(8,128)(2,1)S(1)}, bf16[8,64,256]{2,1,0:T(8,128)(2,1)S(1)}, u32[]{:S(2)}, u32[]{:S(2)}) collective-permute-start(bf16[8,64,256]{2,1,0:T(8,128)(2,1)S(1)} %get-tuple-element.70), channel_id=1, source_target_pairs={{0,8},{8,16},{16,24},{24,28},{28,20},{20,12},{12,4},{4,0},{1,9},{9... | collective-permute-start | bytes 786440 | tf_op jit(solution)/shard_map/ppermute | solution.py:186
  7.9 9.2 %collective-permute-start.5 = (bf16[8,64,256]{2,1,0:T(8,128)(2,1)S(1)}, bf16[8,64,256]{2,1,0:T(8,128)(2,1)S(1)}, u32[]{:S(2)}, u32[]{:S(2)}) collective-permute-start(bf16[8,64,256]{2,1,0:T(8,128)(2,1)S(1)} %get-tuple-element.70), channel_id=1, source_target_pairs={{8,0},{16,8},{24,16},{28,24},{20,28},{12,20},{4,12},{0,4},{9,1},{1... | collective-permute-start | bytes 786440 | tf_op jit(solution)/shard_map/ppermute | solution.py:186
  8.4 12.8 %collective-permute-start = (bf16[8,64,256]{2,1,0:T(8,128)(2,1)S(1)}, bf16[8,64,256]{2,1,0:T(8,128)(2,1)S(1)}, u32[]{:S(2)}, u32[]{:S(2)}) collective-permute-start(bf16[8,64,256]{2,1,0:T(8,128)(2,1)S(1)} %get-tuple-element.71), channel_id=1, source_target_pairs={{0,8},{8,16},{16,24},{24,28},{28,20},{20,12},{12,4},{4,0},{1,9},{9... | collective-permute-start | bytes 786440 | tf_op jit(solution)/shard_map/ppermute | solution.py:186
  10.0 15.4 %collective-permute-start.9 = (bf16[8,64,256]{2,1,0:T(8,128)(2,1)S(1)}, bf16[8,64,256]{2,1,0:T(8,128)(2,1)S(1)}, u32[]{:S(2)}, u32[]{:S(2)}) collective-permute-start(bf16[8,64,256]{2,1,0:T(8,128)(2,1)S(1)} %get-tuple-element.71), channel_id=1, source_target_pairs={{8,0},{16,8},{24,16},{28,24},{20,28},{12,20},{4,12},{0,4},{9,1},{1... | collective-permute-start | bytes 786440 | tf_op jit(solution)/shard_map/ppermute | solution.py:186
  10.4 2.2 %copy-start.1 = (bf16[128,64,256]{2,1,0:T(8,128)(2,1)S(1)}, bf16[128,64,256]{2,1,0:T(8,128)(2,1)}, u32[]{:S(2)}) copy-start(bf16[128,64,256]{2,1,0:T(8,128)(2,1)} %refs_4_.5) | copy-start | bytes 12582916
  12.6 1.0 %copy-start.3 = (bf16[16,256,64]{1,2,0:T(8,128)(2,1)S(1)}, bf16[16,256,64]{1,2,0:T(8,128)(2,1)}, u32[]{:S(2)}) copy-start(bf16[16,256,64]{1,2,0:T(8,128)(2,1)} %param.10) | copy-start | bytes 1572868
  13.6 0.7 %copy-start.5 = (s32[128]{0:T(128)S(1)}, s32[128]{0:T(128)}, u32[]{:S(2)}) copy-start(s32[128]{0:T(128)} %slot_block.7) | copy-start | bytes 1540
  14.3 11.1 %copy-start.2 = (bf16[128,64,256]{2,1,0:T(8,128)(2,1)S(1)}, bf16[128,64,256]{2,1,0:T(8,128)(2,1)}, u32[]{:S(2)}) copy-start(bf16[128,64,256]{2,1,0:T(8,128)(2,1)} %refs_4_.5) | copy-start | bytes 12582916
  17.2 13.9 %collective-permute-start.7 = (bf16[8,64,256]{2,1,0:T(8,128)(2,1)S(1)}, bf16[8,64,256]{2,1,0:T(8,128)(2,1)S(1)}, u32[]{:S(2)}, u32[]{:S(2)}) collective-permute-start(bf16[8,64,256]{2,1,0:T(8,128)(2,1)S(1)} %collective-permute-done.4.refs_2_), channel_id=1, source_target_pairs={{0,8},{8,16},{16,24},{24,28},{28,20},{20,12},{12,4},{4,0},{1,9},{9... | collective-permute-start | bytes 786440 | tf_op jit(solution)/shard_map/ppermute | solution.py:186
  18.8 12.3 %collective-permute-start.8 = (bf16[8,64,256]{2,1,0:T(8,128)(2,1)S(1)}, bf16[8,64,256]{2,1,0:T(8,128)(2,1)S(1)}, u32[]{:S(2)}, u32[]{:S(2)}) collective-permute-start(bf16[8,64,256]{2,1,0:T(8,128)(2,1)S(1)} %collective-permute-done.5.refs_3_), channel_id=1, source_target_pairs={{8,0},{16,8},{24,16},{28,24},{20,28},{12,20},{4,12},{0,4},{9,1},{1... | collective-permute-start | bytes 786440 | tf_op jit(solution)/shard_map/ppermute | solution.py:186
  21.2 12.8 %collective-permute-start.1 = (bf16[8,64,256]{2,1,0:T(8,128)(2,1)S(1)}, bf16[8,64,256]{2,1,0:T(8,128)(2,1)S(1)}, u32[]{:S(2)}, u32[]{:S(2)}) collective-permute-start(bf16[8,64,256]{2,1,0:T(8,128)(2,1)S(1)} %collective-permute-done.refs_0_), channel_id=1, source_target_pairs={{0,8},{8,16},{16,24},{24,28},{28,20},{20,12},{12,4},{4,0},{1,9},{9... | collective-permute-start | bytes 786440 | tf_op jit(solution)/shard_map/ppermute | solution.py:186
  22.8 8.3 %collective-permute-start.10 = (f32[40,256]{1,0:T(8,128)S(1)}, f32[40,256]{1,0:T(8,128)S(1)}, u32[]{:S(2)}, u32[]{:S(2)}) collective-permute-start(f32[40,256]{1,0:T(8,128)S(1)} %fusion.1), channel_id=1, source_target_pairs={{0,16},{4,20},{8,24},{12,28},{16,0},{20,4},{24,8},{28,12},{1,17},{... | collective-permute-start | bytes 122888 | tf_op jit(solution)/shard_map/ppermute | solution.py:168
  25.4 12.1 %collective-permute-start.13 = (bf16[8,64,256]{2,1,0:T(8,128)(2,1)S(1)}, bf16[8,64,256]{2,1,0:T(8,128)(2,1)S(1)}, u32[]{:S(2)}, u32[]{:S(2)}) collective-permute-start(bf16[8,64,256]{2,1,0:T(8,128)(2,1)S(1)} %collective-permute-done.9.refs_1_), channel_id=1, source_target_pairs={{8,0},{16,8},{24,16},{28,24},{20,28},{12,20},{4,12},{0,4},{9,1},{1... | collective-permute-start | bytes 786440 | tf_op jit(solution)/shard_map/ppermute | solution.py:186
  31.1 12.7 %collective-permute-start.11 = (bf16[8,64,256]{2,1,0:T(8,128)(2,1)S(1)}, bf16[8,64,256]{2,1,0:T(8,128)(2,1)S(1)}, u32[]{:S(2)}, u32[]{:S(2)}) collective-permute-start(bf16[8,64,256]{2,1,0:T(8,128)(2,1)S(1)} %collective-permute-done.7.refs_2_), channel_id=1, source_target_pairs={{0,8},{8,16},{16,24},{24,28},{28,20},{20,12},{12,4},{4,0},{1,9},{9... | collective-permute-start | bytes 786440 | tf_op jit(solution)/shard_map/ppermute | solution.py:186
  33.5 10.3 %collective-permute-start.12 = (bf16[8,64,256]{2,1,0:T(8,128)(2,1)S(1)}, bf16[8,64,256]{2,1,0:T(8,128)(2,1)S(1)}, u32[]{:S(2)}, u32[]{:S(2)}) collective-permute-start(bf16[8,64,256]{2,1,0:T(8,128)(2,1)S(1)} %collective-permute-done.8.refs_3_), channel_id=1, source_target_pairs={{8,0},{16,8},{24,16},{28,24},{20,28},{12,20},{4,12},{0,4},{9,1},{1... | collective-permute-start | bytes 786440 | tf_op jit(solution)/shard_map/ppermute | solution.py:186
  34.0 12.8 %collective-permute-start.2 = (bf16[8,64,256]{2,1,0:T(8,128)(2,1)S(1)}, bf16[8,64,256]{2,1,0:T(8,128)(2,1)S(1)}, u32[]{:S(2)}, u32[]{:S(2)}) collective-permute-start(bf16[8,64,256]{2,1,0:T(8,128)(2,1)S(1)} %collective-permute-done.1.refs_0_), channel_id=1, source_target_pairs={{0,8},{8,16},{16,24},{24,28},{28,20},{20,12},{12,4},{4,0},{1,9},{9... | collective-permute-start | bytes 786440 | tf_op jit(solution)/shard_map/ppermute | solution.py:186
  35.5 8.3 %collective-permute-start.14 = (f32[40,256]{1,0:T(8,128)S(1)}, f32[40,256]{1,0:T(8,128)S(1)}, u32[]{:S(2)}, u32[]{:S(2)}) collective-permute-start(f32[40,256]{1,0:T(8,128)S(1)} %add.46), channel_id=1, source_target_pairs={{0,8},{4,12},{8,0},{12,4},{16,24},{20,28},{24,16},{28,20},{1,9},{5... | collective-permute-start | bytes 122888 | tf_op jit(solution)/shard_map/ppermute | solution.py:168
  37.4 12.1 %collective-permute-start.16 = (bf16[8,64,256]{2,1,0:T(8,128)(2,1)S(1)}, bf16[8,64,256]{2,1,0:T(8,128)(2,1)S(1)}, u32[]{:S(2)}, u32[]{:S(2)}) collective-permute-start(bf16[8,64,256]{2,1,0:T(8,128)(2,1)S(1)} %collective-permute-done.13.refs_1_), channel_id=1, source_target_pairs={{8,0},{16,8},{24,16},{28,24},{20,28},{12,20},{4,12},{0,4},{9,1},{1... | collective-permute-start | bytes 786440 | tf_op jit(solution)/shard_map/ppermute | solution.py:186
  39.0 14.6 %copy-start.4 = (f32[256,32]{0,1:T(8,128)S(1)}, f32[256,32]{0,1:T(8,128)}, u32[]{:S(2)}) copy-start(f32[256,32]{0,1:T(8,128)} %param.13) | copy-start | bytes 98308
  43.8 18.3 %copy-start.6 = (f32[256]{0:T(256)S(1)}, f32[256]{0:T(256)}, u32[]{:S(2)}) copy-start(f32[256]{0:T(256)} %param.15) | copy-start | bytes 3076
  43.8 8.6 %collective-permute-start.15 = (bf16[8,64,256]{2,1,0:T(8,128)(2,1)S(1)}, bf16[8,64,256]{2,1,0:T(8,128)(2,1)S(1)}, u32[]{:S(2)}, u32[]{:S(2)}) collective-permute-start(bf16[8,64,256]{2,1,0:T(8,128)(2,1)S(1)} %collective-permute-done.12.refs_3_), channel_id=1, source_target_pairs={{8,0},{16,8},{24,16},{28,24},{20,28},{12,20},{4,12},{0,4},{9,1},{1... | collective-permute-start | bytes 786440 | tf_op jit(solution)/shard_map/ppermute | solution.py:195
  46.8 6.4 %collective-permute-start.3 = (bf16[8,64,256]{2,1,0:T(8,128)(2,1)S(1)}, bf16[8,64,256]{2,1,0:T(8,128)(2,1)S(1)}, u32[]{:S(2)}, u32[]{:S(2)}) collective-permute-start(bf16[8,64,256]{2,1,0:T(8,128)(2,1)S(1)} %collective-permute-done.2.refs_0_), channel_id=1, source_target_pairs={{0,8},{8,16},{16,24},{24,28},{28,20},{20,12},{12,4},{4,0},{1,9},{9... | collective-permute-start | bytes 786440 | tf_op jit(solution)/shard_map/ppermute | solution.py:193
  46.8 1.6 %collective-permute-start.17 = (f32[40,256]{1,0:T(8,128)S(1)}, f32[40,256]{1,0:T(8,128)S(1)}, u32[]{:S(2)}, u32[]{:S(2)}) collective-permute-start(f32[40,256]{1,0:T(8,128)S(1)} %add.47.s0), channel_id=1, source_target_pairs={{0,1},{1,0},{2,3},{3,2},{4,5},{5,4},{6,7},{7,6},{8,9},{9,8},{10,11... | collective-permute-start | bytes 122888 | tf_op jit(solution)/shard_map/ppermute | solution.py:168
  46.8 4.1 %collective-permute-start.18 = (f32[40,256]{1,0:T(8,128)S(1)}, f32[40,256]{1,0:T(8,128)S(1)}, u32[]{:S(2)}, u32[]{:S(2)}) collective-permute-start(f32[40,256]{1,0:T(8,128)S(1)} %add.47.s0), channel_id=1, source_target_pairs={{0,2},{1,3},{2,0},{3,1},{4,6},{5,7},{6,4},{7,5},{8,10},{9,11},{10,... | collective-permute-start | bytes 122888 | tf_op jit(solution)/shard_map/ppermute | solution.py:168
  48.4 4.0 %collective-permute-start.19 = (f32[40,256]{1,0:T(8,128)S(1)}, f32[40,256]{1,0:T(8,128)S(1)}, u32[]{:S(2)}, u32[]{:S(2)}) collective-permute-start(f32[40,256]{1,0:T(8,128)S(1)} %collective-permute-done.17.s1), channel_id=1, source_target_pairs={{0,2},{1,3},{2,0},{3,1},{4,6},{5,7},{6,4},{7,5},{8,10},{9,11},{10,... | collective-permute-start | bytes 122888 | tf_op jit(solution)/shard_map/ppermute | solution.py:168
  53.5 1.6 %collective-permute-start.20 = (f32[256,256]{1,0:T(8,128)S(1)}, f32[256,256]{1,0:T(8,128)S(1)}, u32[]{:S(2)}, u32[]{:S(2)}) collective-permute-start(f32[256,256]{1,0:T(8,128)S(1)} %pad_maximum_fusion), channel_id=1, source_target_pairs={{0,1},{1,0},{2,3},{3,2},{4,5},{5,4},{6,7},{7,6},{8,9},{9,8},{10,11... | collective-permute-start | bytes 786440 | tf_op jit(solution)/shard_map/ppermute | solution.py:168
  55.1 5.6 %collective-permute-start.21 = (f32[128,256]{1,0:T(8,128)S(1)}, f32[128,256]{1,0:T(8,128)S(1)}, u32[]{:S(2)}, u32[]{:S(2)}) collective-permute-start(f32[128,256]{1,0:T(8,128)S(1)} %slice_add_fusion), channel_id=1, source_target_pairs={{0,2},{1,3},{2,0},{3,1},{4,6},{5,7},{6,4},{7,5},{8,10},{9,11},{10,... | collective-permute-start | bytes 393224 | tf_op jit(solution)/shard_map/ppermute | solution.py:168
  56.8 5.3 %collective-permute-start.23 = (f32[128,256]{1,0:T(8,128)S(1)}, f32[128,256]{1,0:T(8,128)S(1)}, u32[]{:S(2)}, u32[]{:S(2)}) collective-permute-start(f32[128,256]{1,0:T(8,128)S(1)} %pad_maximum_fusion.1), channel_id=1, source_target_pairs={{0,4},{4,0},{8,12},{12,8},{16,20},{20,16},{24,28},{28,24},{1,5},{5... | collective-permute-start | bytes 393224 | tf_op jit(solution)/shard_map/ppermute | solution.py:168
  60.7 1.4 %collective-permute-start.22 = (f32[128,256]{1,0:T(8,128)S(1)}, f32[128,256]{1,0:T(8,128)S(1)}, u32[]{:S(2)}, u32[]{:S(2)}) collective-permute-start(f32[128,256]{1,0:T(8,128)S(1)} %collective-permute-done.21.far), channel_id=1, source_target_pairs={{0,1},{1,0},{2,3},{3,2},{4,5},{5,4},{6,7},{7,6},{8,9},{9,8},{10,11... | collective-permute-start | bytes 393224 | tf_op jit(solution)/shard_map/ppermute | solution.py:168
